TPU v7x, 128 devices: a whole 4x4x4 slice. The times are simulated.
128 devices in a mesh: row: 16 (over z, x), col: 8 (over y, core).
Axes of the slice: x: 4, y: 4, z: 4, core: 2. Of those that a mesh axis runs over, the one named last changes fastest.
Arguments:
- tokens: bfloat16 [2048, 4096], P('row', 'col'), may hold values from -6 to 6
- up_weight: bfloat16 [128, 8, 128, 128], P(('col', 'row')), may hold values from -0.1875 to 0.1875
- up_rows: int32 [128, 8], P('col'), may hold values from 0 to 31, as said below
- down_weight: bfloat16 [128, 8, 128, 128], P(('col', 'row')), may hold values from -0.09375 to 0.09375
- down_cols: int32 [128, 8], P('col'), may hold values from 0 to 31, as said below
- grad_out: bfloat16 [2048, 4096], P('row', 'col'), may hold values from -6 to 6
Outputs:
- layer_out: bfloat16 [2048, 4096], P('row', 'col')
- grad_tokens: bfloat16 [2048, 4096], P('row', 'col')
- grad_up: bfloat16 [128, 8, 128, 128], P(('col', 'row'))
- grad_down: bfloat16 [128, 8, 128, 128], P(('col', 'row'))
Inputs may be any that keep to these rules, and one draw needn't show every extreme that they name: `up_rows`: row j lists 8 distinct block rows of the up projection's block column j in rising order; they are that block column's only nonzero blocks. `down_cols`: row i lists 8 distinct block columns of the down projection's block row i in rising order; they are that block row's only nonzero blocks.
All inputs are finite; a program needn't handle non-finite values.
Results may differ from a plain program's by a relative error of at most 0.019.
Values may be sent and summed in bfloat16 or wider, within the bound.
No kernel may reach another device: no remote copies, remote signals or barrier semaphores. Data moves between devices by JAX's collectives and lax.ppermute only.
A program may use at most 128 MiB of HBM per device.

v0:
```python
import math

import jax
import jax.numpy as jnp
from jax import lax
from jax.sharding import PartitionSpec as P


def gelu_tanh(values):
    return jax.nn.gelu(values, approximate=True)


def up_apply(token_blocks, panel_blocks, row_ids):
    summed = jnp.zeros(
        (token_blocks.shape[0], panel_blocks.shape[0], panel_blocks.shape[3]), jnp.float32
    )
    for slot_index in range(panel_blocks.shape[1]):
        picked = jnp.take(token_blocks, row_ids[:, slot_index], axis=1)
        summed = summed + jnp.einsum(
            "tja,jab->tjb", picked, panel_blocks[:, slot_index], preferred_element_type=jnp.float32
        )
    return summed


def up_transpose(grad_piece, panel_blocks, row_ids, block_count):
    summed = jnp.zeros((grad_piece.shape[0], block_count, panel_blocks.shape[2]), jnp.float32)
    for slot_index in range(panel_blocks.shape[1]):
        product = jnp.einsum(
            "tjb,jab->tja",
            grad_piece,
            panel_blocks[:, slot_index],
            preferred_element_type=jnp.float32,
        )
        summed = summed.at[:, row_ids[:, slot_index], :].add(product)
    return summed


def down_apply(hidden_piece, grad_blocks, panel_blocks, col_ids, block_count):
    tok_rows = hidden_piece.shape[0]
    out_part = jnp.zeros((tok_rows, block_count, panel_blocks.shape[3]), jnp.float32)
    grad_piece = jnp.zeros((tok_rows, panel_blocks.shape[0], panel_blocks.shape[2]), jnp.float32)
    for slot_index in range(panel_blocks.shape[1]):
        weight_slot = panel_blocks[:, slot_index]
        product = jnp.einsum(
            "tia,iab->tib", hidden_piece, weight_slot, preferred_element_type=jnp.float32
        )
        out_part = out_part.at[:, col_ids[:, slot_index], :].add(product)
        picked = jnp.take(grad_blocks, col_ids[:, slot_index], axis=1)
        grad_piece = grad_piece + jnp.einsum(
            "tib,iab->tia", picked, weight_slot, preferred_element_type=jnp.float32
        )
    return (out_part, grad_piece)


def per_device(tokens, up_weight, up_rows, down_weight, down_cols, grad_out):
    tok_rows = tokens.shape[0]
    block_size = up_weight.shape[2]
    slot_count = up_weight.shape[1]
    token_whole, grad_whole = (
        lax.all_gather(tokens, "col", axis=1, tiled=True),
        lax.all_gather(grad_out, "col", axis=1, tiled=True),
    )
    block_count = token_whole.shape[1] // block_size
    token_blocks = token_whole.reshape(tok_rows, block_count, block_size)
    grad_blocks = grad_whole.reshape(tok_rows, block_count, block_size)
    row_ids = up_rows
    pre_act = up_apply(token_blocks, lax.all_gather(up_weight, "row", axis=0, tiled=True), row_ids)
    hidden = gelu_tanh(pre_act).astype(jnp.bfloat16)
    hidden_piece = hidden
    col_ids = down_cols
    added, grad_piece = down_apply(
        hidden_piece,
        grad_blocks,
        lax.all_gather(down_weight, "row", axis=0, tiled=True),
        col_ids,
        block_count,
    )
    grad_hidden = grad_piece
    out_sum = lax.psum_scatter(
        added.astype(jnp.bfloat16), "col", scatter_dimension=1, tiled=True
    ).astype(jnp.float32)
    layer_out = out_sum.reshape(tok_rows, -1).astype(jnp.bfloat16)
    pull_back = jax.vjp(gelu_tanh, pre_act)[1]
    grad_pre = pull_back(grad_hidden)[0].astype(jnp.bfloat16)
    row_ids = up_rows
    grad_piece = grad_pre
    input_part = up_transpose(
        grad_piece, lax.all_gather(up_weight, "row", axis=0, tiled=True), row_ids, block_count
    )
    input_sum = lax.psum_scatter(
        input_part.astype(jnp.bfloat16), "col", scatter_dimension=1, tiled=True
    ).astype(jnp.float32)
    grad_tokens = input_sum.reshape(tok_rows, -1).astype(jnp.bfloat16)
    hidden_piece = hidden
    col_ids = down_cols
    terms_list = []
    for down_slot_index in range(slot_count):
        down_picked = jnp.take(grad_blocks, col_ids[:, down_slot_index], axis=1)
        terms_list.append(
            jnp.einsum(
                "tia,tib->iab", hidden_piece, down_picked, preferred_element_type=jnp.float32
            )
        )
    down_sum = lax.psum_scatter(
        jnp.stack(terms_list, axis=1).astype(jnp.bfloat16), "row", scatter_dimension=0, tiled=True
    ).astype(jnp.float32)
    grad_piece = grad_pre
    row_ids = up_rows
    terms_list = []
    for slot_index in range(slot_count):
        picked = jnp.take(token_blocks, row_ids[:, slot_index], axis=1)
        terms_list.append(
            jnp.einsum("tja,tjb->jab", picked, grad_piece, preferred_element_type=jnp.float32)
        )
    up_sum = lax.psum_scatter(
        jnp.stack(terms_list, axis=1).astype(jnp.bfloat16), "row", scatter_dimension=0, tiled=True
    ).astype(jnp.float32)
    grad_scale = 1.0 / math.sqrt(tok_rows * lax.axis_size("row"))
    grad_up = (up_sum * grad_scale).astype(jnp.bfloat16)
    grad_down = (down_sum * grad_scale).astype(jnp.bfloat16)
    return (layer_out, grad_tokens, grad_up, grad_down)


def solution(mesh):
    return jax.shard_map(
        per_device,
        mesh=mesh,
        in_specs=(
            P("row", "col"),
            P(("col", "row"), None, None, None),
            P("col", None),
            P(("col", "row"), None, None, None),
            P("col", None),
            P("row", "col"),
        ),
        out_specs=(
            P("row", "col"),
            P("row", "col"),
            P(("col", "row"), None, None, None),
            P(("col", "row"), None, None, None),
        ),
        check_vma=False,
    )
```

profile of v0, /device:TPU:1, one launch (start us, length us, event | category | flops | bytes accessed | tf_op | source)
XLA Modules:
  0.0 460.6 jit_solution(11785073834474695060)
XLA Ops:
  7.2 1.7 copy.96
  8.9 1.7 copy.108
  16.1 21.2 %all-gather.5.cloned.1.call-done = bf16[128,4096]{0,1:T(8,128)(2,1)} async-done(((bf16[128,512]{0,1:T(8,128)(2,1)}), bf16[128,4096]{0,1:T(8,128)(2,1)}) %all-gather.5.cloned.1.call-update) | async-done | bytes 1048592 | tf_op jit(solution)/shard_map/all_gather | solution.py:60
  37.3 1.6 copy.97
  39.6 1.5 gather_fusion.1
  41.1 1.4 gather_fusion.2
  43.9 1.4 gather_fusion.4
  46.7 1.4 gather_fusion.7
  48.1 14.8 %all-gather.11.cloned.1.call-done = bf16[128,4096]{0,1:T(8,128)(2,1)} async-done(((bf16[128,512]{0,1:T(8,128)(2,1)}), bf16[128,4096]{0,1:T(8,128)(2,1)}) %all-gather.11.cloned.1.call-update) | async-done | bytes 1048592 | tf_op jit(solution)/shard_map/all_gather | solution.py:61
  62.9 1.6 copy.109
  66.6 1.4 gather_fusion.10
  68.0 1.4 gather_fusion.11
  69.4 1.4 gather_fusion.12
  70.8 1.4 gather_fusion.13
  72.2 1.4 gather_fusion.14
  73.6 1.4 gather_fusion.15
  75.1 41.1 %all-gather.7.cloned.1.call-done = bf16[16,8,128,128]{3,2,0,1:T(8,128)(2,1)} async-done(((bf16[1,8,128,128]{3,2,0,1:T(8,128)(2,1)}), bf16[16,8,128,128]{3,2,0,1:T(8,128)(2,1)}) %all-gather.7.cloned.1.call-update) | async-done | bytes 4194320 | tf_op jit(solution)/shard_map/all_gather | solution.py:67
  116.2 1.5 fusion.73
  117.8 1.6 convolution_add_fusion.13
  121.3 1.6 multiply_convert_fusion
  122.9 46.6 %all-gather.9.cloned.1.call-done = bf16[16,8,128,128]{3,2,0,1:T(8,128)(2,1)} async-done(((bf16[1,8,128,128]{3,2,0,1:T(8,128)(2,1)}), bf16[16,8,128,128]{3,2,0,1:T(8,128)(2,1)}) %all-gather.9.cloned.1.call-update) | async-done | bytes 4194320 | tf_op jit(solution)/shard_map/all_gather | solution.py:74
  169.5 2.3 fusion.83
  172.0 2.6 scatter_fusion
  174.6 2.3 fusion.84
  176.9 2.6 scatter_fusion.1
  179.5 2.3 fusion.85
  181.8 2.6 scatter_fusion.2
  184.5 2.3 fusion.86
  186.8 2.6 scatter_fusion.3
  189.4 2.3 fusion.87
  191.7 2.6 scatter_fusion.4
  194.3 2.3 fusion.88
  196.6 2.6 scatter_fusion.5
  199.2 2.3 fusion.89
  201.5 2.8 scatter_fusion.6
  204.3 2.3 fusion.90
  206.6 2.6 scatter_fusion.7
  210.4 1.7 fusion.56
  212.1 1.8 convolution_add_fusion.6
  217.7 2.5 fusion.75
  220.4 2.6 scatter_fusion.8
  223.0 2.5 fusion.76
  225.5 2.6 scatter_fusion.9
  228.1 2.5 fusion.77
  230.6 2.6 scatter_fusion.10
  233.2 2.5 fusion.78
  235.7 2.6 scatter_fusion.11
  238.3 2.5 fusion.79
  240.8 2.6 scatter_fusion.12
  243.4 2.5 fusion.80
  245.9 2.6 scatter_fusion.13
  248.5 2.5 fusion.81
  251.0 2.6 scatter_fusion.14
  253.7 2.5 fusion.82
  256.1 2.8 scatter_fusion.15
  260.1 2.4 fusion.3
  262.5 2.3 fusion.19
  264.8 2.3 fusion.5
  273.4 2.4 fusion.17
  275.8 2.3 fusion.21
  288.3 13.8 %reduce-scatter.11.cloned.1.call-done = bf16[128,4,128]{2,0,1:T(8,128)(2,1)} async-done(((bf16[128,32,128]{2,0,1:T(8,128)(2,1)}), bf16[128,4,128]{2,0,1:T(8,128)(2,1)}) %reduce-scatter.11.cloned.1.call-update) | async-done | bytes 131088 | tf_op jit(solution)/shard_map/reduce_scatter | solution.py:90
  303.9 145.3 %all-reduce.5.cloned.1.call-done = (bf16[16,8,128,128]{3,2,0,1:T(8,128)(2,1)}, bf16[16,8,128,128]{3,2,0,1:T(8,128)(2,1)}) async-done(((bf16[16,8,128,128]{3,2,0,1:T(8,128)(2,1)}, bf16[16,8,128,128]{3,2,0,1:T(8,128)(2,1)}), (bf16[16,8,128,128]{3,2,0,1:T(8,128)(2,1)}, bf16[16,8,128,128]{3,2,0,1:T(8,128)(2,1)})) %all-reduce.5.cloned.1.call-update) | async-done | bytes 8388624
  449.2 2.3 fusion.91
  451.5 2.3 fusion.92
  (122 shorter events, 37.3 us)
Async XLA Ops:
  7.2 30.2 %all-gather.5.cloned.1.call-start = ((), (), s32[]{:S(2)}) async-start(), calls=%async_computation.2 | async-start | bytes 1179648 | tf_op jit(solution)/shard_map/all_gather | solution.py:60
  8.9 54.0 %all-gather.11.cloned.1.call-start = ((), (), s32[]{:S(2)}) async-start(), calls=%async_computation.6 | async-start | bytes 1179648 | tf_op jit(solution)/shard_map/all_gather | solution.py:61
  10.6 105.5 %all-gather.7.cloned.1.call-start = ((), (), s32[]{:S(2)}) async-start(), calls=%async_computation.3 | async-start | bytes 4456448 | tf_op jit(solution)/shard_map/all_gather | solution.py:67
  11.4 158.1 %all-gather.9.cloned.1.call-start = ((), (), s32[]{:S(2)}) async-start(), calls=%async_computation.4 | async-start | bytes 4456448 | tf_op jit(solution)/shard_map/all_gather | solution.py:74
  12.0 274.5 %reduce-scatter.9.cloned.1.call-start = ((), (), s32[]{:S(2)}) async-start(), calls=%async_computation.5 | async-start | bytes 1179648 | tf_op jit(solution)/shard_map/reduce_scatter | solution.py:79
  39.6 76.6 %copy-start.2 = (bf16[16,128,128]{2,1,0:T(8,128)(2,1)}, bf16[16,128,128]{2,1,0:T(8,128)(2,1)S(1)}, u32[]{:S(2)}) copy-start(bf16[16,128,128]{2,1,0:T(8,128)(2,1)S(1)} %gather_fusion) | copy-start | bytes 1572868
  46.0 74.5 %copy-start.16 = (bf16[16,128,128]{2,1,0:T(8,128)(2,1)}, bf16[16,128,128]{2,1,0:T(8,128)(2,1)S(1)}, u32[]{:S(2)}) copy-start(bf16[16,128,128]{2,1,0:T(8,128)(2,1)S(1)} %gather_fusion.5) | copy-start | bytes 1572868
  46.6 74.2 %copy-start.14 = (bf16[16,128,128]{2,1,0:T(8,128)(2,1)}, bf16[16,128,128]{2,1,0:T(8,128)(2,1)S(1)}, u32[]{:S(2)}) copy-start(bf16[16,128,128]{2,1,0:T(8,128)(2,1)S(1)} %gather_fusion.6) | copy-start | bytes 1572868
  65.2 145.2 %copy-start.3 = (bf16[16,128,128]{2,1,0:T(8,128)(2,1)}, bf16[16,128,128]{2,1,0:T(8,128)(2,1)S(1)}, u32[]{:S(2)}) copy-start(bf16[16,128,128]{2,1,0:T(8,128)(2,1)S(1)} %gather_fusion.8) | copy-start | bytes 1572868
  75.1 44.3 %copy-start.22 = (bf16[16,128,128]{2,1,0:T(8,128)(2,1)S(1)}, bf16[16,128,128]{2,1,0:T(8,128)(2,1)}, u32[]{:S(2)}) copy-start(bf16[16,128,128]{2,1,0:T(8,128)(2,1)} %gather_fusion.2) | copy-start | bytes 1572868
  116.2 3.2 copy-start
  116.2 3.6 copy-start.20
  117.7 2.4 copy-start.18
  120.1 1.1 copy-start.26
  210.3 3.6 copy-start.12
  210.3 91.8 %reduce-scatter.11.cloned.1.call-start = ((), (), s32[]{:S(2)}) async-start(), calls=%async_computation.7 | async-start | bytes 1179648 | tf_op jit(solution)/shard_map/reduce_scatter | solution.py:90
  210.4 3.5 copy-start.1
  210.4 4.1 copy-start.10
  212.1 2.9 copy-start.8
  213.9 1.7 copy-start.6
  214.5 1.6 copy-start.4
  215.0 1.6 copy-start.24
  215.1 1.6 copy-start.28
  260.1 8.3 %copy-start.21 = (bf16[16,128,128]{2,1,0:T(8,128)(2,1)S(1)}, bf16[16,128,128]{2,1,0:T(8,128)(2,1)}, u32[]{:S(2)}) copy-start(bf16[16,128,128]{2,1,0:T(8,128)(2,1)} %gather_fusion.3) | copy-start | bytes 1572868
  260.1 7.0 %copy-start.23 = (bf16[16,128,128]{2,1,0:T(8,128)(2,1)S(1)}, bf16[16,128,128]{2,1,0:T(8,128)(2,1)}, u32[]{:S(2)}) copy-start(bf16[16,128,128]{2,1,0:T(8,128)(2,1)} %gather_fusion.2) | copy-start | bytes 1572868
  260.1 9.5 %copy-start.19 = (bf16[16,128,128]{2,1,0:T(8,128)(2,1)S(1)}, bf16[16,128,128]{2,1,0:T(8,128)(2,1)}, u32[]{:S(2)}) copy-start(bf16[16,128,128]{2,1,0:T(8,128)(2,1)} %gather_fusion.4) | copy-start | bytes 1572868
  262.5 8.3 %copy-start.17 = (bf16[16,128,128]{2,1,0:T(8,128)(2,1)S(1)}, bf16[16,128,128]{2,1,0:T(8,128)(2,1)}, u32[]{:S(2)}) copy-start(bf16[16,128,128]{2,1,0:T(8,128)(2,1)} %copy-done.16) | copy-start | bytes 1572868
  264.8 7.3 %copy-start.15 = (bf16[16,128,128]{2,1,0:T(8,128)(2,1)S(1)}, bf16[16,128,128]{2,1,0:T(8,128)(2,1)}, u32[]{:S(2)}) copy-start(bf16[16,128,128]{2,1,0:T(8,128)(2,1)} %copy-done.14) | copy-start | bytes 1572868
  269.6 8.4 %copy-start.13 = (bf16[16,128,128]{2,1,0:T(8,128)(2,1)S(1)}, bf16[16,128,128]{2,1,0:T(8,128)(2,1)}, u32[]{:S(2)}) copy-start(bf16[16,128,128]{2,1,0:T(8,128)(2,1)} %gather_fusion.10) | copy-start | bytes 1572868
  270.9 8.4 %copy-start.11 = (bf16[16,128,128]{2,1,0:T(8,128)(2,1)S(1)}, bf16[16,128,128]{2,1,0:T(8,128)(2,1)}, u32[]{:S(2)}) copy-start(bf16[16,128,128]{2,1,0:T(8,128)(2,1)} %gather_fusion.11) | copy-start | bytes 1572868
  272.1 8.3 %copy-start.9 = (bf16[16,128,128]{2,1,0:T(8,128)(2,1)S(1)}, bf16[16,128,128]{2,1,0:T(8,128)(2,1)}, u32[]{:S(2)}) copy-start(bf16[16,128,128]{2,1,0:T(8,128)(2,1)} %gather_fusion.12) | copy-start | bytes 1572868
  273.4 8.3 %copy-start.7 = (bf16[16,128,128]{2,1,0:T(8,128)(2,1)S(1)}, bf16[16,128,128]{2,1,0:T(8,128)(2,1)}, u32[]{:S(2)}) copy-start(bf16[16,128,128]{2,1,0:T(8,128)(2,1)} %gather_fusion.13) | copy-start | bytes 1572868
  273.4 175.9 %all-reduce.5.cloned.1.call-start = ((), (), s32[]{:S(2)}) async-start(), calls=%async_computation.8 | async-start | bytes 16777216
  275.8 7.1 %copy-start.5 = (bf16[16,128,128]{2,1,0:T(8,128)(2,1)S(1)}, bf16[16,128,128]{2,1,0:T(8,128)(2,1)}, u32[]{:S(2)}) copy-start(bf16[16,128,128]{2,1,0:T(8,128)(2,1)} %gather_fusion.14) | copy-start | bytes 1572868
  278.1 6.0 %copy-start.25 = (bf16[16,128,128]{2,1,0:T(8,128)(2,1)S(1)}, bf16[16,128,128]{2,1,0:T(8,128)(2,1)}, u32[]{:S(2)}) copy-start(bf16[16,128,128]{2,1,0:T(8,128)(2,1)} %gather_fusion.15) | copy-start | bytes 1572868
  285.2 0.7 copy-start.27
Sparse Core Ops, SparseCore 0:
  10.3 26.9 all-gather.4
  39.6 23.2 all-gather.10
  65.0 51.1 all-gather.6
  118.2 51.2 all-gather.8
  210.5 28.6 reduce-scatter.8
  273.5 28.5 reduce-scatter.10
  305.9 143.3 all-reduce.4
where the time goes:
time: 463 us; the launch traced here: 461 us
  waiting for transfers between devices  284 us (61%)
  matrix products  76.9 us (17%)
  other arithmetic  52.9 us (11%)
  local copies, waits for them, and re-layouts  31.5 us (7%)
  between operations  14.8 us (3%)
    unnamed x8, waiting for transfers between devices  147 us
    all_gather x1, waiting for transfers between devices, per_device(): lax.all_gather(down_weight, 'row', axis=0, tiled=True)  46.6 us
    all_gather x1, waiting for transfers between devices, per_device(): lax.all_gather(up_weight, 'row', axis=0, tiled=True)  41.1 us
    all_gather x1, waiting for transfers between devices, per_device(): lax.all_gather(tokens, 'col', axis=1, tiled=True)  21.2 us
    scatter-add x8, other arithmetic, up_transpose(): summed = summed.at[:, row_ids[:, slot_index], :].add(product)  21.1 us
    scatter-add x8, other arithmetic, down_apply(): out_part = out_part.at[:, col_ids[:, slot_index], :].add(product)  21 us
    dot_general x8, matrix products, up_transpose(): jnp.einsum('tjb,jab->tja', grad_piece, panel_blocks[:, slot_index], prefe...  19.9 us
    dot_general x8, matrix products, down_apply(): jnp.einsum('tia,iab->tib', hidden_piece, weight_slot, preferred_element_t...  18.4 us
  transfers between devices with their start and end apart: 7, of which 6 were waited for; matrix products, arithmetic and copies ran while one was open for 25% of the time, Pallas kernels for 0%

commit v1 on v0

v1 whole, which is shorter than its diff:
```python
import functools
import math

import jax
import jax.numpy as jnp
from jax import lax
from jax.experimental import pallas as pl
from jax.experimental.pallas import tpu as pltpu
from jax.sharding import Mesh
from jax.sharding import PartitionSpec as P

RING = 4
BLK = 128
SHIFTS = (1, 3, 2)
GELU_SCALE = math.sqrt(2.0 / math.pi)
GELU_CUBIC = 0.044715


def shift(values, axis, step):
    return lax.ppermute(values, axis, [(i, (i + step) % RING) for i in range(RING)])


def swap(values):
    return lax.ppermute(values, "core", [(0, 1), (1, 0)])


def ring_gather(values, axis):
    slots = {0: values}
    for step in SHIFTS:
        slots[step] = shift(values, axis, step)
    return [slots[step] for step in range(RING)]


def ring_reduce(chunks, axis):
    parts = [chunks[0]]
    for step in SHIFTS:
        parts.append(shift(chunks[step], axis, RING - step))
    return sum(part.astype(jnp.float32) for part in parts)


def layer_kernel(
    core_ref,
    codes_ref,
    t0, t1, t2, t3,
    g0, g1, g2, g3,
    w_hbm,
    o0, o1, o2, o3,
    i0, i1, i2, i3,
    wg_hbm,
    tok, grd, wgt, out_acc, in_acc, out_st, in_st, wg_st, sems,
):
    core = core_ref[0]
    copies = []
    for ys, src in enumerate((t0, t1, t2, t3)):
        for r in range(2):
            copies.append((src.at[:, r], tok.at[ys * 2 + r]))
    for xs, src in enumerate((g0, g1, g2, g3)):
        copies.append((src, grd.at[:, xs]))
    copies.append((w_hbm, wgt))
    copies = [
        pltpu.make_async_copy(src, dst, sems.at[n]) for n, (src, dst) in enumerate(copies)
    ]
    for copy in copies:
        copy.start()
    out_acc[...] = jnp.zeros_like(out_acc)
    in_acc[...] = jnp.zeros_like(in_acc)
    for copy in copies:
        copy.wait()

    def spot(r, which, z, s):
        code = codes_ref[r, which, z, s]
        return code >> 2, pl.ds(pl.multiple_of((code & 3) * BLK, BLK), BLK)

    def body(step, carry):
        z, r = step >> 1, step & 1
        m = z * 2 + (r ^ core)
        up_spots = [spot(r, 0, z, s) for s in range(8)]
        down_spots = [spot(r, 1, z, s) for s in range(8)]
        picked = jnp.concatenate(
            [tok[a, :, :, c].reshape(256, BLK) for a, c in up_spots], axis=1
        )
        w_up = wgt[m, 0].reshape(8 * BLK, BLK)
        pre = jnp.dot(picked, w_up, preferred_element_type=jnp.float32)
        inner = GELU_SCALE * (pre + GELU_CUBIC * pre * pre * pre)
        t = jnp.tanh(inner)
        hidden = (0.5 * pre * (1.0 + t)).astype(jnp.bfloat16)
        slope = 0.5 * (1.0 + t) + 0.5 * pre * (1.0 - t * t) * GELU_SCALE * (
            1.0 + 3.0 * GELU_CUBIC * pre * pre
        )
        gpicked = jnp.concatenate(
            [grd[a >> 1, :, a & 1, :, c].reshape(256, BLK) for a, c in down_spots], axis=1
        )
        w_down = jnp.concatenate([wgt[m, 1, s] for s in range(8)], axis=1)
        gh = lax.dot_general(
            gpicked, w_down, (((1,), (1,)), ((), ())), preferred_element_type=jnp.float32
        )
        grad_pre = (gh * slope).astype(jnp.bfloat16)
        out_part = jnp.dot(hidden, w_down, preferred_element_type=jnp.float32)
        for s, (a, c) in enumerate(down_spots):
            out_acc[a, :, c] += out_part[:, s * BLK : (s + 1) * BLK]
        dg = lax.dot_general(
            hidden, gpicked, (((0,), (0,)), ((), ())), preferred_element_type=jnp.float32
        ).astype(jnp.bfloat16)
        for s in range(8):
            wg_st[m, 1, s] = dg[:, s * BLK : (s + 1) * BLK]
        in_part = lax.dot_general(
            grad_pre, w_up, (((1,), (1,)), ((), ())), preferred_element_type=jnp.float32
        )
        for s, (a, c) in enumerate(up_spots):
            in_acc[a, :, c] += in_part[:, s * BLK : (s + 1) * BLK]
        ug = lax.dot_general(
            picked, grad_pre, (((0,), (0,)), ((), ())), preferred_element_type=jnp.float32
        ).astype(jnp.bfloat16)
        wg_st[m, 0] = ug.reshape(8, BLK, BLK)
        return carry

    lax.fori_loop(0, 8, body, 0)

    backs = [pltpu.make_async_copy(wg_st, wg_hbm, sems.at[0])]
    backs[0].start()
    for a in range(8):
        out_st[a >> 1, :, a & 1] = out_acc[a].astype(jnp.bfloat16).reshape(4, 64, 512)
    for ys, dst in enumerate((o0, o1, o2, o3)):
        backs.append(pltpu.make_async_copy(out_st.at[ys], dst, sems.at[1 + ys]))
        backs[-1].start()
    for a in range(8):
        in_st[:, a >> 1, a & 1] = in_acc[a].astype(jnp.bfloat16).reshape(4, 64, 512)
    for xs, dst in enumerate((i0, i1, i2, i3)):
        backs.append(pltpu.make_async_copy(in_st.at[xs], dst, sems.at[5 + xs]))
        backs[-1].start()
    for copy in backs:
        copy.wait()


def layer(core, codes, t_slots, g_slots, weights):
    chunk = jax.ShapeDtypeStruct((4, 2, 64, 512), jnp.bfloat16)
    smem = pl.BlockSpec(memory_space=pltpu.SMEM)
    anywhere = pl.BlockSpec(memory_space=pl.ANY)
    results = pl.pallas_call(
        layer_kernel,
        out_shape=[chunk] * 8 + [jax.ShapeDtypeStruct((8, 2, 8, BLK, BLK), jnp.bfloat16)],
        in_specs=[smem, smem] + [anywhere] * 9,
        out_specs=[anywhere] * 9,
        scratch_shapes=[
            pltpu.VMEM((8, 4, 64, 512), jnp.bfloat16),
            pltpu.VMEM((4, 4, 2, 64, 512), jnp.bfloat16),
            pltpu.VMEM((8, 2, 8, BLK, BLK), jnp.bfloat16),
            pltpu.VMEM((8, 256, 512), jnp.float32),
            pltpu.VMEM((8, 256, 512), jnp.float32),
            pltpu.VMEM((4, 4, 2, 64, 512), jnp.bfloat16),
            pltpu.VMEM((4, 4, 2, 64, 512), jnp.bfloat16),
            pltpu.VMEM((8, 2, 8, BLK, BLK), jnp.bfloat16),
            pltpu.SemaphoreType.DMA((13,)),
        ],
        compiler_params=pltpu.CompilerParams(vmem_limit_bytes=48 << 20),
        cost_estimate=pl.CostEstimate(
            flops=3 * 1024**3, bytes_accessed=16 << 20, transcendentals=1 << 18
        ),
        name="layer",
    )(core, codes, *t_slots, *g_slots, weights)
    return results[:4], results[4:8], results[8]


def per_device(tokens, up_weight, up_rows, down_weight, down_cols, grad_out):
    x_at, y_at = lax.axis_index("x"), lax.axis_index("y")
    core = lax.axis_index("core")

    weights = lax.all_gather(
        jnp.stack([up_weight[0], down_weight[0]])[None], ("z", "core"), axis=0, tiled=True
    )

    both = jnp.stack([tokens, grad_out]).reshape(2, 2, 64, 512)
    kept = lax.dynamic_index_in_dim(both, core, axis=1, keepdims=False)
    sent = lax.dynamic_index_in_dim(both, 1 - core, axis=1, keepdims=False)
    came = swap(sent)
    t_own = jnp.stack([kept[0], came[0]])
    g_own = jnp.stack([kept[1], came[1]])

    ids = jnp.stack([up_rows, down_cols]).reshape(2, 4, 4, 8)
    ids = lax.dynamic_index_in_dim(ids, x_at, axis=2, keepdims=False)
    ids = jnp.stack([ids, swap(ids)])
    place = ((y_at - (ids >> 3)) & 3) * 2 + (((ids >> 2) & 1) ^ core)
    codes = place * 4 + (ids & 3)

    t_x = jnp.stack(ring_gather(t_own, "x"))
    g_y = jnp.stack(ring_gather(g_own, "y"))
    t_slots = ring_gather(t_x, "y")
    g_slots = ring_gather(g_y, "x")

    out_chunks, in_chunks, weight_grads = layer(
        core.reshape(1), codes, t_slots, g_slots, weights
    )

    summed = lax.psum_scatter(weight_grads, ("z", "core"), scatter_dimension=0, tiled=True)
    grad_scale = 1.0 / math.sqrt(tokens.shape[0] * lax.axis_size("z") * lax.axis_size("x"))
    scaled = (summed.astype(jnp.float32) * grad_scale).astype(jnp.bfloat16)

    out_y = ring_reduce(out_chunks, "y").astype(jnp.bfloat16)
    in_x = ring_reduce(in_chunks, "x").astype(jnp.bfloat16)
    out_all = ring_reduce([out_y[n] for n in range(RING)], "x").astype(jnp.bfloat16)
    in_all = ring_reduce([in_x[n] for n in range(RING)], "y").astype(jnp.bfloat16)
    mine = jnp.stack([out_all[0], in_all[0]])
    theirs = swap(jnp.stack([out_all[1], in_all[1]]))
    first = jnp.where(core == 0, mine, theirs)
    second = jnp.where(core == 0, theirs, mine)
    acts = jnp.concatenate([first, second], axis=1)
    return (acts[0], acts[1], scaled[:, 0], scaled[:, 1])


def solution(mesh):
    grid = Mesh(mesh.devices.reshape(4, 4, 4, 2), ("z", "x", "y", "core"))
    row, col = ("z", "x"), ("y", "core")
    acts, ids = P(row, col), P(col, None)
    blocks = P(col + row, None, None, None)
    return jax.shard_map(
        per_device,
        mesh=grid,
        in_specs=(acts, blocks, ids, blocks, ids, acts),
        out_specs=(acts, acts, blocks, blocks),
        check_vma=False,
    )
```

time: 463 us -> 154 us (0.33)
  waiting for transfers between devices: 284 us -> 70.6 us
  matrix products: 76.9 us -> 0 us
  other arithmetic: 52.9 us -> 5.67 us
  starting transfers between devices: 0.28 us -> 41.7 us
  local copies, waits for them, and re-layouts: 31.5 us -> 7.18 us
  Pallas kernels: 0 us -> 14.7 us
    unnamed x8 -> x2, waiting for transfers between devices: 147 us -> 0.03 us
    all_gather x4 -> x1, waiting for transfers between devices: 124 us -> 0.01 us  [per_device(): lax.all_gather(jnp.stack([up_weight[0], down_weight[0]])[None], ('z', 'co...]
    dot_general x48 -> x0, matrix products: 76.9 us -> none  [the longest x8 19.9 us: up_transpose(): jnp.einsum('tjb,jab->tja', grad_piece, panel_blocks[:, slot_index], prefe...]
    ppermute x0 -> x27, waiting for transfers between devices: none -> 70.5 us  [the longest x24 68.6 us: shift(): lax.ppermute(values, axis, [(i, (i + step) % RING) for i in range(RING)])]
    scatter-add x16 -> x0, other arithmetic: 42 us -> none  [the longest x8 21.1 us: up_transpose(): summed = summed.at[:, row_ids[:, slot_index], :].add(product)]
    ppermute x0 -> x27, starting transfers between devices: none -> 41.6 us  [the longest x24 32.2 us: shift(): lax.ppermute(values, axis, [(i, (i + step) % RING) for i in range(RING)])]
    gather x16 -> x0, local copies, waits for them, and re-layouts: 19.6 us -> none  [the longest x8 10.5 us: down_apply(): picked = jnp.take(grad_blocks, col_ids[:, slot_index], axis=1)]
    pallas_call x0 -> x1, Pallas kernels: none -> 14.7 us  [layer(): pl.pallas_call(layer_kernel, out_shape=[chunk] * 8 + [jax.ShapeDtypeStruc...]
  transfers between devices with their start and end apart: 7 -> 29, of which waited for: 6 -> 15; matrix products, arithmetic and copies ran while one was open for 25% -> 2% of each run, Pallas kernels for 0% -> 0%
where the time goes in v1:
time: 154 us
  waiting for transfers between devices  70.6 us (46%)
  starting transfers between devices  41.7 us (27%)
  Pallas kernels  14.7 us (10%)
  between operations  14.2 us (9%)
  local copies, waits for them, and re-layouts  7.18 us (5%)
  other arithmetic  5.67 us (4%)
    ppermute x24, waiting for transfers between devices, shift(): lax.ppermute(values, axis, [(i, (i + step) % RING) for i in range(RING)])  68.6 us
    ppermute x24, starting transfers between devices, shift(): lax.ppermute(values, axis, [(i, (i + step) % RING) for i in range(RING)])  32.2 us
    pallas_call x1, Pallas kernels, layer(): pl.pallas_call(layer_kernel, out_shape=[chunk] * 8 + [jax.ShapeDtypeStruc...  14.7 us
    ppermute x3, starting transfers between devices, swap(): return lax.ppermute(values, 'core', [(0, 1), (1, 0)])  9.39 us
    unnamed x26, local copies, waits for them, and re-layouts  6.25 us
  transfers between devices with their start and end apart: 29, of which 15 were waited for; matrix products, arithmetic and copies ran while one was open for 2% of the time, Pallas kernels for 0%

profile of v1, /device:TPU:1, one launch (start us, length us, event | category | flops | bytes accessed | tf_op | source)
XLA Modules:
  0.0 154.1 jit_solution(15003147735354527586)
XLA Ops:
  7.2 0.0 all-gather.3.cloned.1.call-start
  7.2 1.9 %pad_maximum_fusion.2 = bf16[2,8,128,128]{3,2,1,0:T(8,128)(2,1)} fusion(bf16[1,8,128,128]{3,2,1,0:T(8,128)(2,1)} %param.9, bf16[1,8,128,128]{3,2,1,0:T(8,128)(2,1)} %param.7), kind=kLoop, calls=%fused_computation.5 | loop fusion | flops 262144 | bytes 1048576 | tf_op jit(solution)/shard_map/stack | solution.py:169
  9.1 0.0 all-gather.3.cloned.1.call-update
  9.1 0.0 reduce-scatter.2.cloned.1.call-start
  9.2 1.0 fusion.10
  10.2 1.5 collective-permute-start.1
  11.7 1.0 collective-permute-done.1
  12.7 1.4 collective-permute-start.8
  14.1 2.6 %collective-permute-start.9 = (bf16[2,64,512]{2,1,0:T(8,128)(2,1)S(1)}, bf16[2,64,512]{2,1,0:T(8,128)(2,1)S(1)}, u32[]{:S(2)}, u32[]{:S(2)}) collective-permute-start(bf16[2,64,512]{2,1,0:T(8,128)(2,1)S(1)} %get-tuple-element.41), channel_id=1, source_target_pairs={{0,4},{2,6},{4,0},{6,2},{1,5},{3,7},{5,1},{7,3},{8,12},{10,14},{12... | collective-permute-start | bytes 393224 | tf_op jit(solution)/shard_map/ppermute | solution.py:20
  16.8 1.1 collective-permute-start.10
  17.8 1.2 collective-permute-done.8
  19.0 3.8 %collective-permute-done.9 = bf16[2,64,512]{2,1,0:T(8,128)(2,1)S(1)} collective-permute-done((bf16[2,64,512]{2,1,0:T(8,128)(2,1)S(1)}, bf16[2,64,512]{2,1,0:T(8,128)(2,1)S(1)}, u32[]{:S(2)}, u32[]{:S(2)}) %collective-permute-start.9) | collective-permute-done | bytes 131104 | tf_op jit(solution)/shard_map/ppermute | solution.py:20
  22.8 0.1 pad_maximum_fusion.1.g0
  22.9 1.3 collective-permute-start.11
  24.2 1.3 collective-permute-start.2
  25.5 1.4 collective-permute-start.3
  26.9 1.9 %collective-permute-start.4 = (bf16[2,64,512]{2,1,0:T(8,128)(2,1)S(1)}, bf16[2,64,512]{2,1,0:T(8,128)(2,1)S(1)}, u32[]{:S(2)}, u32[]{:S(2)}) collective-permute-start(bf16[2,64,512]{2,1,0:T(8,128)(2,1)S(1)} %get-tuple-element.47), channel_id=1, source_target_pairs={{0,24},{8,0},{16,8},{24,16},{1,25},{9,1},{17,9},{25,17},{2,26},{10... | collective-permute-start | bytes 393224 | tf_op jit(solution)/shard_map/ppermute | solution.py:20
  28.8 0.1 copy.12
  28.9 0.1 copy.13
  29.0 2.4 %collective-permute-start = (s32[2,4,8]{2,1,0:T(4,128)S(1)}, s32[2,4,8]{2,1,0:T(4,128)S(1)}, u32[]{:S(2)}, u32[]{:S(2)}) collective-permute-start(s32[2,4,8]{2,1,0:T(4,128)S(1)} %bitcast.65), channel_id=1, source_target_pairs={{0,1},{1,0},{2,3},{3,2},{4,5},{5,4},{6,7},{7,6},{8,9},{9,8},{10,11... | collective-permute-start | bytes 776 | tf_op jit(solution)/shard_map/ppermute | solution.py:24
  31.4 8.0 %collective-permute-done.2 = bf16[2,64,512]{2,1,0:T(8,128)(2,1)S(1)} collective-permute-done((bf16[2,64,512]{2,1,0:T(8,128)(2,1)S(1)}, bf16[2,64,512]{2,1,0:T(8,128)(2,1)S(1)}, u32[]{:S(2)}, u32[]{:S(2)}) %collective-permute-start.2) | collective-permute-done | bytes 131104 | tf_op jit(solution)/shard_map/ppermute | solution.py:20
  39.3 1.6 %collective-permute-start.12 = (bf16[4,2,64,512]{3,2,1,0:T(8,128)(2,1)S(1)}, bf16[4,2,64,512]{3,2,1,0:T(8,128)(2,1)}, u32[]{:S(2)}, u32[]{:S(2)}) collective-permute-start(bf16[4,2,64,512]{3,2,1,0:T(8,128)(2,1)S(1)} %pad_maximum_fusion.1.g0), channel_id=1, source_target_pairs={{0,16},{8,24},{16,0},{24,8},{1,17},{9,25},{17,1},{25,9},{2,18},{10... | collective-permute-start | bytes 1572872 | tf_op jit(solution)/shard_map/ppermute | solution.py:20
  40.9 1.9 %collective-permute-done.3 = bf16[2,64,512]{2,1,0:T(8,128)(2,1)S(1)} collective-permute-done((bf16[2,64,512]{2,1,0:T(8,128)(2,1)S(1)}, bf16[2,64,512]{2,1,0:T(8,128)(2,1)S(1)}, u32[]{:S(2)}, u32[]{:S(2)}) %collective-permute-start.3) | collective-permute-done | bytes 131104 | tf_op jit(solution)/shard_map/ppermute | solution.py:20
  42.8 0.1 pad_maximum_fusion.t0
  42.8 1.0 collective-permute-start.5
  43.8 2.4 %collective-permute-start.6 = (bf16[4,2,64,512]{3,2,1,0:T(8,128)(2,1)S(1)}, bf16[4,2,64,512]{3,2,1,0:T(8,128)(2,1)S(1)}, u32[]{:S(2)}, u32[]{:S(2)}) collective-permute-start(bf16[4,2,64,512]{3,2,1,0:T(8,128)(2,1)S(1)} %pad_maximum_fusion.t0), channel_id=1, source_target_pairs={{0,4},{2,6},{4,0},{6,2},{1,5},{3,7},{5,1},{7,3},{8,12},{10,14},{12... | collective-permute-start | bytes 1572872 | tf_op jit(solution)/shard_map/ppermute | solution.py:20
  46.2 0.5 collective-permute-start.7
  46.8 7.2 %collective-permute-done.12.g2 = bf16[4,2,64,512]{3,2,1,0:T(8,128)(2,1)} collective-permute-done((bf16[4,2,64,512]{3,2,1,0:T(8,128)(2,1)S(1)}, bf16[4,2,64,512]{3,2,1,0:T(8,128)(2,1)}, u32[]{:S(2)}, u32[]{:S(2)}) %collective-permute-start.12) | collective-permute-done | bytes 524320 | tf_op jit(solution)/shard_map/ppermute | solution.py:20
  54.0 9.8 %collective-permute-done.13.g3 = bf16[4,2,64,512]{3,2,1,0:T(8,128)(2,1)} collective-permute-done((bf16[4,2,64,512]{3,2,1,0:T(8,128)(2,1)S(1)}, bf16[4,2,64,512]{3,2,1,0:T(8,128)(2,1)}, u32[]{:S(2)}, u32[]{:S(2)}) %collective-permute-start.13) | collective-permute-done | bytes 524320 | tf_op jit(solution)/shard_map/ppermute | solution.py:20
  63.8 0.8 copy-done
  64.6 1.5 %collective-permute-done.6.t2 = bf16[4,2,64,512]{3,2,1,0:T(8,128)(2,1)S(1)} collective-permute-done((bf16[4,2,64,512]{3,2,1,0:T(8,128)(2,1)S(1)}, bf16[4,2,64,512]{3,2,1,0:T(8,128)(2,1)S(1)}, u32[]{:S(2)}, u32[]{:S(2)}) %collective-permute-start.6) | collective-permute-done | bytes 524320 | tf_op jit(solution)/shard_map/ppermute | solution.py:20
  66.1 0.8 copy-done.4
  66.9 1.8 %collective-permute-done.7.t3 = bf16[4,2,64,512]{3,2,1,0:T(8,128)(2,1)} collective-permute-done((bf16[4,2,64,512]{3,2,1,0:T(8,128)(2,1)S(1)}, bf16[4,2,64,512]{3,2,1,0:T(8,128)(2,1)}, u32[]{:S(2)}, u32[]{:S(2)}) %collective-permute-start.7) | collective-permute-done | bytes 524320 | tf_op jit(solution)/shard_map/ppermute | solution.py:20
  68.8 1.0 copy-done.1
  69.8 1.0 copy-done.5
  70.9 14.7 %layer.1 = (bf16[4,2,64,512]{3,2,1,0:T(8,128)(2,1)S(1)}, bf16[4,2,64,512]{3,2,1,0:T(8,128)(2,1)S(1)}, bf16[4,2,64,512]{3,2,1,0:T(8,128)(2,1)S(1)}, bf16[4,2,64,5...) custom-call(s32[1]{0:T(128)} %bitcast.core_ref, ...), custom_call_target="tpu_custom_call" | custom-call | flops 3221225472 | bytes 16777216 | tf_op jit(solution)/shard_map/layer/pallas_call | solution.py:139
  85.6 0.8 copy-done.2
  86.4 0.8 copy-done.6
  87.2 0.8 copy-done.7
  88.0 0.0 reduce-scatter.2.cloned.1.call-update
  88.0 3.6 %collective-permute-start.14 = (bf16[4,2,64,512]{3,2,1,0:T(8,128)(2,1)}, bf16[4,2,64,512]{3,2,1,0:T(8,128)(2,1)S(1)}, u32[]{:S(2)}, u32[]{:S(2)}) collective-permute-start(bf16[4,2,64,512]{3,2,1,0:T(8,128)(2,1)} %copy-done.7), channel_id=1, source_target_pairs={{0,6},{2,0},{4,2},{6,4},{1,7},{3,1},{5,3},{7,5},{8,14},{10,8},{12,... | collective-permute-start | bytes 1572872 | tf_op jit(solution)/shard_map/ppermute | solution.py:20
  91.6 1.3 collective-permute-start.16
  92.9 1.2 collective-permute-start.20
  94.0 0.3 collective-permute-start.21
  94.4 19.4 %collective-permute-done.14 = bf16[4,2,64,512]{3,2,1,0:T(8,128)(2,1)S(1)} collective-permute-done((bf16[4,2,64,512]{3,2,1,0:T(8,128)(2,1)}, bf16[4,2,64,512]{3,2,1,0:T(8,128)(2,1)S(1)}, u32[]{:S(2)}, u32[]{:S(2)}) %collective-permute-start.14) | collective-permute-done | bytes 524320 | tf_op jit(solution)/shard_map/ppermute | solution.py:20
  113.8 0.9 collective-permute-start.22
  114.7 2.3 %collective-permute-done.15 = bf16[4,2,64,512]{3,2,1,0:T(8,128)(2,1)S(1)} collective-permute-done((bf16[4,2,64,512]{3,2,1,0:T(8,128)(2,1)}, bf16[4,2,64,512]{3,2,1,0:T(8,128)(2,1)S(1)}, u32[]{:S(2)}, u32[]{:S(2)}) %collective-permute-start.15) | collective-permute-done | bytes 524320 | tf_op jit(solution)/shard_map/ppermute | solution.py:20
  117.0 0.3 add_convert_fusion.1
  117.4 1.1 collective-permute-start.17
  118.5 0.5 collective-permute-start.18
  119.1 1.7 %collective-permute-start.19 = (bf16[2,64,512]{2,1,0:T(8,128)(2,1)S(1)}, bf16[2,64,512]{2,1,0:T(8,128)(2,1)S(1)}, u32[]{:S(2)}, u32[]{:S(2)}) collective-permute-start(bf16[2,64,512]{2,1,0:T(8,128)(2,1)S(1)} %get-tuple-element.25), channel_id=1, source_target_pairs={{0,16},{8,24},{16,0},{24,8},{1,17},{9,25},{17,1},{25,9},{2,18},{10... | collective-permute-start | bytes 393224 | tf_op jit(solution)/shard_map/ppermute | solution.py:20
  120.8 6.5 %collective-permute-done.22 = bf16[4,2,64,512]{3,2,1,0:T(8,128)(2,1)S(1)} collective-permute-done((bf16[4,2,64,512]{3,2,1,0:T(8,128)(2,1)S(1)}, bf16[4,2,64,512]{3,2,1,0:T(8,128)(2,1)S(1)}, u32[]{:S(2)}, u32[]{:S(2)}) %collective-permute-start.22) | collective-permute-done | bytes 524320 | tf_op jit(solution)/shard_map/ppermute | solution.py:20
  127.3 0.3 add_convert_fusion
  127.6 3.9 %collective-permute-start.23 = (bf16[2,64,512]{2,1,0:T(8,128)(2,1)S(1)}, bf16[2,64,512]{2,1,0:T(8,128)(2,1)S(1)}, u32[]{:S(2)}, u32[]{:S(2)}) collective-permute-start(bf16[2,64,512]{2,1,0:T(8,128)(2,1)S(1)} %get-tuple-element.27), channel_id=1, source_target_pairs={{0,6},{2,0},{4,2},{6,4},{1,7},{3,1},{5,3},{7,5},{8,14},{10,8},{12,... | collective-permute-start | bytes 393224 | tf_op jit(solution)/shard_map/ppermute | solution.py:20
  131.5 1.3 collective-permute-start.25
  132.7 0.6 collective-permute-done.18
  133.4 0.1 fusion.5
  133.5 4.4 %collective-permute-done.24 = bf16[2,64,512]{2,1,0:T(8,128)(2,1)S(1)} collective-permute-done((bf16[2,64,512]{2,1,0:T(8,128)(2,1)S(1)}, bf16[2,64,512]{2,1,0:T(8,128)(2,1)S(1)}, u32[]{:S(2)}, u32[]{:S(2)}) %collective-permute-start.24) | collective-permute-done | bytes 131104 | tf_op jit(solution)/shard_map/ppermute | solution.py:20
  137.9 0.1 fusion.2
  138.0 5.5 %collective-permute-start.26 = (bf16[2,64,512]{2,1,0:T(8,128)(2,1)S(1)}, bf16[2,64,512]{2,1,0:T(8,128)(2,1)S(1)}, u32[]{:S(2)}, u32[]{:S(2)}) collective-permute-start(bf16[2,64,512]{2,1,0:T(8,128)(2,1)S(1)} %pad_maximum_fusion.7), channel_id=1, source_target_pairs={{0,1},{1,0},{2,3},{3,2},{4,5},{5,4},{6,7},{7,6},{8,9},{9,8},{10,11... | collective-permute-start | bytes 393224 | tf_op jit(solution)/shard_map/ppermute | solution.py:24
  143.5 1.0 collective-permute-done.26
  144.5 0.7 fusion.11
  145.2 1.2 multiply_convert_fusion
  146.4 0.8 slice_bitcast_fusion
  (46 shorter events, 0.3 us)
Async XLA Ops:
  7.2 21.6 %copy-start.9 = (s32[16,8]{0,1:T(8,128)S(1)}, s32[16,8]{0,1:T(8,128)}, u32[]{:S(2)}) copy-start(s32[16,8]{0,1:T(8,128)} %param.8) | copy-start | bytes 1540
  7.2 21.7 %copy-start.10 = (s32[16,8]{0,1:T(8,128)S(1)}, s32[16,8]{0,1:T(8,128)}, u32[]{:S(2)}) copy-start(s32[16,8]{0,1:T(8,128)} %param.10) | copy-start | bytes 1540
  7.2 61.6 %all-gather.3.cloned.1.call-start = ((), (), s32[]{:S(2)}) async-start(), calls=%async_computation.2 | async-start | bytes 4718592 | tf_op jit(solution)/shard_map/all_gather | solution.py:168
  9.1 136.1 %reduce-scatter.2.cloned.1.call-start = ((), (), s32[]{:S(2)}) async-start(), calls=%async_computation.1 | async-start | bytes 4718592 | tf_op jit(solution)/shard_map/reduce_scatter | solution.py:194
  10.2 2.5 %collective-permute-start.1 = (bf16[2,64,512]{2,1,0:T(8,128)(2,1)S(1)}, bf16[2,64,512]{2,1,0:T(8,128)(2,1)S(1)}, u32[]{:S(2)}, u32[]{:S(2)}) collective-permute-start(bf16[2,64,512]{2,1,0:T(8,128)(2,1)S(1)} %get-tuple-element.35), channel_id=1, source_target_pairs={{0,1},{1,0},{2,3},{3,2},{4,5},{5,4},{6,7},{7,6},{8,9},{9,8},{10,11... | collective-permute-start | bytes 393224 | tf_op jit(solution)/shard_map/ppermute | solution.py:24
  12.7 6.3 %collective-permute-start.8 = (bf16[2,64,512]{2,1,0:T(8,128)(2,1)S(1)}, bf16[2,64,512]{2,1,0:T(8,128)(2,1)S(1)}, u32[]{:S(2)}, u32[]{:S(2)}) collective-permute-start(bf16[2,64,512]{2,1,0:T(8,128)(2,1)S(1)} %get-tuple-element.41), channel_id=1, source_target_pairs={{0,2},{2,4},{4,6},{6,0},{1,3},{3,5},{5,7},{7,1},{8,10},{10,12},{12... | collective-permute-start | bytes 393224 | tf_op jit(solution)/shard_map/ppermute | solution.py:20
  14.1 8.7 %collective-permute-start.9 = (bf16[2,64,512]{2,1,0:T(8,128)(2,1)S(1)}, bf16[2,64,512]{2,1,0:T(8,128)(2,1)S(1)}, u32[]{:S(2)}, u32[]{:S(2)}) collective-permute-start(bf16[2,64,512]{2,1,0:T(8,128)(2,1)S(1)} %get-tuple-element.41), channel_id=1, source_target_pairs={{0,4},{2,6},{4,0},{6,2},{1,5},{3,7},{5,1},{7,3},{8,12},{10,14},{12... | collective-permute-start | bytes 393224 | tf_op jit(solution)/shard_map/ppermute | solution.py:20
  16.8 6.1 %collective-permute-start.10 = (bf16[2,64,512]{2,1,0:T(8,128)(2,1)S(1)}, bf16[2,64,512]{2,1,0:T(8,128)(2,1)S(1)}, u32[]{:S(2)}, u32[]{:S(2)}) collective-permute-start(bf16[2,64,512]{2,1,0:T(8,128)(2,1)S(1)} %get-tuple-element.41), channel_id=1, source_target_pairs={{0,6},{2,0},{4,2},{6,4},{1,7},{3,1},{5,3},{7,5},{8,14},{10,8},{12,... | collective-permute-start | bytes 393224 | tf_op jit(solution)/shard_map/ppermute | solution.py:20
  22.9 45.9 %copy-start.8 = (bf16[4,2,64,512]{3,2,1,0:T(8,128)(2,1)}, bf16[4,2,64,512]{3,2,1,0:T(8,128)(2,1)S(1)}, u32[]{:S(2)}) copy-start(bf16[4,2,64,512]{3,2,1,0:T(8,128)(2,1)S(1)} %pad_maximum_fusion.1.g0) | copy-start | bytes 1572868
  22.9 23.3 %collective-permute-start.11 = (bf16[4,2,64,512]{3,2,1,0:T(8,128)(2,1)S(1)}, bf16[4,2,64,512]{3,2,1,0:T(8,128)(2,1)S(1)}, u32[]{:S(2)}, u32[]{:S(2)}) collective-permute-start(bf16[4,2,64,512]{3,2,1,0:T(8,128)(2,1)S(1)} %pad_maximum_fusion.1.g0), channel_id=1, source_target_pairs={{0,8},{8,16},{16,24},{24,0},{1,9},{9,17},{17,25},{25,1},{2,10},{10... | collective-permute-start | bytes 1572872 | tf_op jit(solution)/shard_map/ppermute | solution.py:20
  24.2 15.1 %collective-permute-start.2 = (bf16[2,64,512]{2,1,0:T(8,128)(2,1)S(1)}, bf16[2,64,512]{2,1,0:T(8,128)(2,1)S(1)}, u32[]{:S(2)}, u32[]{:S(2)}) collective-permute-start(bf16[2,64,512]{2,1,0:T(8,128)(2,1)S(1)} %get-tuple-element.47), channel_id=1, source_target_pairs={{0,8},{8,16},{16,24},{24,0},{1,9},{9,17},{17,25},{25,1},{2,10},{10... | collective-permute-start | bytes 393224 | tf_op jit(solution)/shard_map/ppermute | solution.py:20
  25.5 17.3 %collective-permute-start.3 = (bf16[2,64,512]{2,1,0:T(8,128)(2,1)S(1)}, bf16[2,64,512]{2,1,0:T(8,128)(2,1)S(1)}, u32[]{:S(2)}, u32[]{:S(2)}) collective-permute-start(bf16[2,64,512]{2,1,0:T(8,128)(2,1)S(1)} %get-tuple-element.47), channel_id=1, source_target_pairs={{0,16},{8,24},{16,0},{24,8},{1,17},{9,25},{17,1},{25,9},{2,18},{10... | collective-permute-start | bytes 393224 | tf_op jit(solution)/shard_map/ppermute | solution.py:20
  26.9 15.8 %collective-permute-start.4 = (bf16[2,64,512]{2,1,0:T(8,128)(2,1)S(1)}, bf16[2,64,512]{2,1,0:T(8,128)(2,1)S(1)}, u32[]{:S(2)}, u32[]{:S(2)}) collective-permute-start(bf16[2,64,512]{2,1,0:T(8,128)(2,1)S(1)} %get-tuple-element.47), channel_id=1, source_target_pairs={{0,24},{8,0},{16,8},{24,16},{1,25},{9,1},{17,9},{25,17},{2,26},{10... | collective-permute-start | bytes 393224 | tf_op jit(solution)/shard_map/ppermute | solution.py:20
  29.0 14.8 %collective-permute-start = (s32[2,4,8]{2,1,0:T(4,128)S(1)}, s32[2,4,8]{2,1,0:T(4,128)S(1)}, u32[]{:S(2)}, u32[]{:S(2)}) collective-permute-start(s32[2,4,8]{2,1,0:T(4,128)S(1)} %bitcast.65), channel_id=1, source_target_pairs={{0,1},{1,0},{2,3},{3,2},{4,5},{5,4},{6,7},{7,6},{8,9},{9,8},{10,11... | collective-permute-start | bytes 776 | tf_op jit(solution)/shard_map/ppermute | solution.py:24
  39.3 14.7 %collective-permute-start.12 = (bf16[4,2,64,512]{3,2,1,0:T(8,128)(2,1)S(1)}, bf16[4,2,64,512]{3,2,1,0:T(8,128)(2,1)}, u32[]{:S(2)}, u32[]{:S(2)}) collective-permute-start(bf16[4,2,64,512]{3,2,1,0:T(8,128)(2,1)S(1)} %pad_maximum_fusion.1.g0), channel_id=1, source_target_pairs={{0,16},{8,24},{16,0},{24,8},{1,17},{9,25},{17,1},{25,9},{2,18},{10... | collective-permute-start | bytes 1572872 | tf_op jit(solution)/shard_map/ppermute | solution.py:20
  42.8 21.0 %collective-permute-start.13 = (bf16[4,2,64,512]{3,2,1,0:T(8,128)(2,1)S(1)}, bf16[4,2,64,512]{3,2,1,0:T(8,128)(2,1)}, u32[]{:S(2)}, u32[]{:S(2)}) collective-permute-start(bf16[4,2,64,512]{3,2,1,0:T(8,128)(2,1)S(1)} %pad_maximum_fusion.1.g0), channel_id=1, source_target_pairs={{0,24},{8,0},{16,8},{24,16},{1,25},{9,1},{17,9},{25,17},{2,26},{10... | collective-permute-start | bytes 1572872 | tf_op jit(solution)/shard_map/ppermute | solution.py:20
  42.8 20.9 %collective-permute-start.5 = (bf16[4,2,64,512]{3,2,1,0:T(8,128)(2,1)S(1)}, bf16[4,2,64,512]{3,2,1,0:T(8,128)(2,1)S(1)}, u32[]{:S(2)}, u32[]{:S(2)}) collective-permute-start(bf16[4,2,64,512]{3,2,1,0:T(8,128)(2,1)S(1)} %pad_maximum_fusion.t0), channel_id=1, source_target_pairs={{0,2},{2,4},{4,6},{6,0},{1,3},{3,5},{5,7},{7,1},{8,10},{10,12},{12... | collective-permute-start | bytes 1572872 | tf_op jit(solution)/shard_map/ppermute | solution.py:20
  43.8 22.3 %collective-permute-start.6 = (bf16[4,2,64,512]{3,2,1,0:T(8,128)(2,1)S(1)}, bf16[4,2,64,512]{3,2,1,0:T(8,128)(2,1)S(1)}, u32[]{:S(2)}, u32[]{:S(2)}) collective-permute-start(bf16[4,2,64,512]{3,2,1,0:T(8,128)(2,1)S(1)} %pad_maximum_fusion.t0), channel_id=1, source_target_pairs={{0,4},{2,6},{4,0},{6,2},{1,5},{3,7},{5,1},{7,3},{8,12},{10,14},{12... | collective-permute-start | bytes 1572872 | tf_op jit(solution)/shard_map/ppermute | solution.py:20
  46.2 22.6 %copy-start.11 = (bf16[4,2,64,512]{3,2,1,0:T(8,128)(2,1)}, bf16[4,2,64,512]{3,2,1,0:T(8,128)(2,1)S(1)}, u32[]{:S(2)}) copy-start(bf16[4,2,64,512]{3,2,1,0:T(8,128)(2,1)S(1)} %collective-permute-done.11.g1) | copy-start | bytes 1572868
  46.2 22.6 %collective-permute-start.7 = (bf16[4,2,64,512]{3,2,1,0:T(8,128)(2,1)S(1)}, bf16[4,2,64,512]{3,2,1,0:T(8,128)(2,1)}, u32[]{:S(2)}, u32[]{:S(2)}) collective-permute-start(bf16[4,2,64,512]{3,2,1,0:T(8,128)(2,1)S(1)} %pad_maximum_fusion.t0), channel_id=1, source_target_pairs={{0,6},{2,0},{4,2},{6,4},{1,7},{3,1},{5,3},{7,5},{8,14},{10,8},{12,... | collective-permute-start | bytes 1572872 | tf_op jit(solution)/shard_map/ppermute | solution.py:20
  63.8 0.8 copy-start
  66.1 0.8 copy-start.4
  68.8 1.0 copy-start.1
  69.8 1.0 copy-start.5
  85.6 0.8 copy-start.2
  86.4 0.8 copy-start.6
  87.2 0.8 copy-start.7
  88.0 3.6 %copy-start.3 = (bf16[4,2,64,512]{3,2,1,0:T(8,128)(2,1)S(1)}, bf16[4,2,64,512]{3,2,1,0:T(8,128)(2,1)}, u32[]{:S(2)}) copy-start(bf16[4,2,64,512]{3,2,1,0:T(8,128)(2,1)} %copy-done.2) | copy-start | bytes 1572868
  88.0 25.8 %collective-permute-start.14 = (bf16[4,2,64,512]{3,2,1,0:T(8,128)(2,1)}, bf16[4,2,64,512]{3,2,1,0:T(8,128)(2,1)S(1)}, u32[]{:S(2)}, u32[]{:S(2)}) collective-permute-start(bf16[4,2,64,512]{3,2,1,0:T(8,128)(2,1)} %copy-done.7), channel_id=1, source_target_pairs={{0,6},{2,0},{4,2},{6,4},{1,7},{3,1},{5,3},{7,5},{8,14},{10,8},{12,... | collective-permute-start | bytes 1572872 | tf_op jit(solution)/shard_map/ppermute | solution.py:20
  91.6 25.4 %collective-permute-start.15 = (bf16[4,2,64,512]{3,2,1,0:T(8,128)(2,1)}, bf16[4,2,64,512]{3,2,1,0:T(8,128)(2,1)S(1)}, u32[]{:S(2)}, u32[]{:S(2)}) collective-permute-start(bf16[4,2,64,512]{3,2,1,0:T(8,128)(2,1)} %copy-done.6), channel_id=1, source_target_pairs={{0,2},{2,4},{4,6},{6,0},{1,3},{3,5},{5,7},{7,1},{8,10},{10,12},{12... | collective-permute-start | bytes 1572872 | tf_op jit(solution)/shard_map/ppermute | solution.py:20
  91.6 25.4 %collective-permute-start.16 = (bf16[4,2,64,512]{3,2,1,0:T(8,128)(2,1)S(1)}, bf16[4,2,64,512]{3,2,1,0:T(8,128)(2,1)S(1)}, u32[]{:S(2)}, u32[]{:S(2)}) collective-permute-start(bf16[4,2,64,512]{3,2,1,0:T(8,128)(2,1)S(1)} %copy-done.3), channel_id=1, source_target_pairs={{0,4},{2,6},{4,0},{6,2},{1,5},{3,7},{5,1},{7,3},{8,12},{10,14},{12... | collective-permute-start | bytes 1572872 | tf_op jit(solution)/shard_map/ppermute | solution.py:20
  92.9 26.2 %collective-permute-start.20 = (bf16[4,2,64,512]{3,2,1,0:T(8,128)(2,1)S(1)}, bf16[4,2,64,512]{3,2,1,0:T(8,128)(2,1)S(1)}, u32[]{:S(2)}, u32[]{:S(2)}) collective-permute-start(bf16[4,2,64,512]{3,2,1,0:T(8,128)(2,1)S(1)} %get-tuple-element.18), channel_id=1, source_target_pairs={{0,24},{8,0},{16,8},{24,16},{1,25},{9,1},{17,9},{25,17},{2,26},{10... | collective-permute-start | bytes 1572872 | tf_op jit(solution)/shard_map/ppermute | solution.py:20
  94.0 26.7 %collective-permute-start.21 = (bf16[4,2,64,512]{3,2,1,0:T(8,128)(2,1)S(1)}, bf16[4,2,64,512]{3,2,1,0:T(8,128)(2,1)S(1)}, u32[]{:S(2)}, u32[]{:S(2)}) collective-permute-start(bf16[4,2,64,512]{3,2,1,0:T(8,128)(2,1)S(1)} %get-tuple-element.19), channel_id=1, source_target_pairs={{0,8},{8,16},{16,24},{24,0},{1,9},{9,17},{17,25},{25,1},{2,10},{10... | collective-permute-start | bytes 1572872 | tf_op jit(solution)/shard_map/ppermute | solution.py:20
  113.8 13.5 %collective-permute-start.22 = (bf16[4,2,64,512]{3,2,1,0:T(8,128)(2,1)S(1)}, bf16[4,2,64,512]{3,2,1,0:T(8,128)(2,1)S(1)}, u32[]{:S(2)}, u32[]{:S(2)}) collective-permute-start(bf16[4,2,64,512]{3,2,1,0:T(8,128)(2,1)S(1)} %get-tuple-element.20), channel_id=1, source_target_pairs={{0,16},{8,24},{16,0},{24,8},{1,17},{9,25},{17,1},{25,9},{2,18},{10... | collective-permute-start | bytes 1572872 | tf_op jit(solution)/shard_map/ppermute | solution.py:20
  117.4 14.1 %collective-permute-start.17 = (bf16[2,64,512]{2,1,0:T(8,128)(2,1)S(1)}, bf16[2,64,512]{2,1,0:T(8,128)(2,1)S(1)}, u32[]{:S(2)}, u32[]{:S(2)}) collective-permute-start(bf16[2,64,512]{2,1,0:T(8,128)(2,1)S(1)} %get-tuple-element.24), channel_id=1, source_target_pairs={{0,24},{8,0},{16,8},{24,16},{1,25},{9,1},{17,9},{25,17},{2,26},{10... | collective-permute-start | bytes 393224 | tf_op jit(solution)/shard_map/ppermute | solution.py:20
  118.5 14.9 %collective-permute-start.18 = (bf16[2,64,512]{2,1,0:T(8,128)(2,1)S(1)}, bf16[2,64,512]{2,1,0:T(8,128)(2,1)S(1)}, u32[]{:S(2)}, u32[]{:S(2)}) collective-permute-start(bf16[2,64,512]{2,1,0:T(8,128)(2,1)S(1)} %get-tuple-element.26), channel_id=1, source_target_pairs={{0,8},{8,16},{16,24},{24,0},{1,9},{9,17},{17,25},{25,1},{2,10},{10... | collective-permute-start | bytes 393224 | tf_op jit(solution)/shard_map/ppermute | solution.py:20
  119.1 14.3 %collective-permute-start.19 = (bf16[2,64,512]{2,1,0:T(8,128)(2,1)S(1)}, bf16[2,64,512]{2,1,0:T(8,128)(2,1)S(1)}, u32[]{:S(2)}, u32[]{:S(2)}) collective-permute-start(bf16[2,64,512]{2,1,0:T(8,128)(2,1)S(1)} %get-tuple-element.25), channel_id=1, source_target_pairs={{0,16},{8,24},{16,0},{24,8},{1,17},{9,25},{17,1},{25,9},{2,18},{10... | collective-permute-start | bytes 393224 | tf_op jit(solution)/shard_map/ppermute | solution.py:20
  127.6 5.9 %collective-permute-start.23 = (bf16[2,64,512]{2,1,0:T(8,128)(2,1)S(1)}, bf16[2,64,512]{2,1,0:T(8,128)(2,1)S(1)}, u32[]{:S(2)}, u32[]{:S(2)}) collective-permute-start(bf16[2,64,512]{2,1,0:T(8,128)(2,1)S(1)} %get-tuple-element.27), channel_id=1, source_target_pairs={{0,6},{2,0},{4,2},{6,4},{1,7},{3,1},{5,3},{7,5},{8,14},{10,8},{12,... | collective-permute-start | bytes 393224 | tf_op jit(solution)/shard_map/ppermute | solution.py:20
  131.5 6.4 %collective-permute-start.24 = (bf16[2,64,512]{2,1,0:T(8,128)(2,1)S(1)}, bf16[2,64,512]{2,1,0:T(8,128)(2,1)S(1)}, u32[]{:S(2)}, u32[]{:S(2)}) collective-permute-start(bf16[2,64,512]{2,1,0:T(8,128)(2,1)S(1)} %get-tuple-element.29), channel_id=1, source_target_pairs={{0,2},{2,4},{4,6},{6,0},{1,3},{3,5},{5,7},{7,1},{8,10},{10,12},{12... | collective-permute-start | bytes 393224 | tf_op jit(solution)/shard_map/ppermute | solution.py:20
  131.5 6.4 %collective-permute-start.25 = (bf16[2,64,512]{2,1,0:T(8,128)(2,1)S(1)}, bf16[2,64,512]{2,1,0:T(8,128)(2,1)S(1)}, u32[]{:S(2)}, u32[]{:S(2)}) collective-permute-start(bf16[2,64,512]{2,1,0:T(8,128)(2,1)S(1)} %get-tuple-element.28), channel_id=1, source_target_pairs={{0,4},{2,6},{4,0},{6,2},{1,5},{3,7},{5,1},{7,3},{8,12},{10,14},{12... | collective-permute-start | bytes 393224 | tf_op jit(solution)/shard_map/ppermute | solution.py:20
  138.0 6.5 %collective-permute-start.26 = (bf16[2,64,512]{2,1,0:T(8,128)(2,1)S(1)}, bf16[2,64,512]{2,1,0:T(8,128)(2,1)S(1)}, u32[]{:S(2)}, u32[]{:S(2)}) collective-permute-start(bf16[2,64,512]{2,1,0:T(8,128)(2,1)S(1)} %pad_maximum_fusion.7), channel_id=1, source_target_pairs={{0,1},{1,0},{2,3},{3,2},{4,5},{5,4},{6,7},{7,6},{8,9},{9,8},{10,11... | collective-permute-start | bytes 393224 | tf_op jit(solution)/shard_map/ppermute | solution.py:24
Sparse Core Ops, SparseCore 0:
  9.7 35.9 all-gather.2
  88.2 36.9 reduce-scatter.1

commit v2 on v1

v2 whole, which is shorter than its diff:
```python
import math

import jax
import jax.numpy as jnp
from jax import lax
from jax.experimental import pallas as pl
from jax.experimental.pallas import tpu as pltpu
from jax.sharding import Mesh
from jax.sharding import PartitionSpec as P

RING = 4
BLK = 128
STEPS = (1, 3, 2)
GELU_SCALE = math.sqrt(2.0 / math.pi)
GELU_CUBIC = 0.044715
MIXED = ("x", "y", "core")


def place(x, y, core):
    return (x % RING * RING + y % RING) * 2 + core


def mixed_pairs(step, first):
    pairs = []
    for x in range(RING):
        for y in range(RING):
            for core in range(2):
                dx, dy = (step, 0) if (core == 0) == first else (0, step)
                pairs.append((place(x, y, core), place(x + dx, y + dy, core)))
    return pairs


def mixed_shift(values, step, first):
    return lax.ppermute(values, MIXED, mixed_pairs(step, first))


def z_shift(values, step):
    return lax.ppermute(values, "z", [(i, (i + step) % RING) for i in range(RING)])


def swap(values):
    return lax.ppermute(values, "core", [(0, 1), (1, 0)])


def gather(values, shift):
    slots = {0: values}
    for step in STEPS:
        slots[step] = shift(values, step)
    return [slots[step] for step in range(RING)]


def reduce(chunks, shift):
    parts = [chunks[0]]
    for step in STEPS:
        parts.append(shift(chunks[step], RING - step))
    return sum(part.astype(jnp.float32) for part in parts)


def load(acts_refs, weight_refs, acts, weights, sems):
    copies = [(src, acts.at[n]) for n, src in enumerate(acts_refs)]
    copies += [(src, weights.at[n]) for n, src in enumerate(weight_refs)]
    copies = [
        pltpu.make_async_copy(src, dst, sems.at[n]) for n, (src, dst) in enumerate(copies)
    ]
    for copy in copies:
        copy.start()
    return copies


def spots(where_ref, codes_ref, d, r):
    core, z = where_ref[0], where_ref[1]
    out = []
    for s in range(8):
        code = codes_ref[r, (z - d) & 3, s]
        slot = code >> 3
        first = jnp.where(core == 0, slot * 4, slot)
        cols = pl.ds(pl.multiple_of((code & 3) * BLK, BLK), BLK)
        out.append((first, (code >> 2) & 1, cols))
    return out, jnp.where(core == 0, 1, 4)


def pick(acts, picked, places, stride):
    for s, (first, half, cols) in enumerate(places):
        for q in range(RING):
            picked[q * BLK : (q + 1) * BLK, s * BLK : (s + 1) * BLK] = acts[
                (first + q * stride) >> 2, (first + q * stride) & 3, half, :, cols
            ]


def enter_kernel(
    where_ref, codes_ref, a0, a1, a2, a3, w0, w1, w2, w3, out, acts, weights, picked, sems
):
    core = where_ref[0]
    for copy in load((a0, a1, a2, a3), (w0, w1, w2, w3), acts, weights, sems):
        copy.wait()

    def body(step, carry):
        d, r = step >> 1, step & 1
        places, stride = spots(where_ref, codes_ref, d, r)
        pick(acts, picked, places, stride)

        @pl.when(core == 0)
        def _():
            out[step ^ core] = jnp.dot(
                picked[...],
                weights[d, r].reshape(8 * BLK, BLK),
                preferred_element_type=jnp.float32,
            )

        @pl.when(core == 1)
        def _():
            flat = jnp.concatenate([weights[d, r, s] for s in range(8)], axis=1)
            out[step ^ core] = lax.dot_general(
                picked[...], flat, (((1,), (1,)), ((), ())), preferred_element_type=jnp.float32
            )

        return carry

    lax.fori_loop(0, 8, body, 0)


def leave_kernel(
    where_ref, codes_ref, left, a0, a1, a2, a3, w0, w1, w2, w3,
    o0, o1, o2, o3, g0, g1, g2, g3,
    acts, weights, picked, acc, out, grads, sems,
):
    core = where_ref[0]
    copies = load((a0, a1, a2, a3), (w0, w1, w2, w3), acts, weights, sems)
    acc[...] = jnp.zeros_like(acc)
    for copy in copies:
        copy.wait()

    def body(step, carry):
        d, r = step >> 1, step & 1
        places, stride = spots(where_ref, codes_ref, d, r)
        pick(acts, picked, places, stride)
        mine = left[step ^ core]

        def scatter(s, product):
            for n in range(2):
                first, half, cols = places[s + n]
                for q in range(RING):
                    at = first + q * stride
                    acc[at >> 2, at & 3, half, :, cols] += product[
                        q * BLK : (q + 1) * BLK, n * BLK : (n + 1) * BLK
                    ]

        @pl.when(core == 0)
        def _():
            for s in range(0, 8, 2):
                pair = weights[d, r, s : s + 2].reshape(2 * BLK, BLK)
                scatter(
                    s,
                    lax.dot_general(
                        mine, pair, (((1,), (1,)), ((), ())), preferred_element_type=jnp.float32
                    ),
                )
            grad = lax.dot_general(
                picked[...], mine, (((0,), (0,)), ((), ())), preferred_element_type=jnp.float32
            )
            grads[d, r] = grad.astype(jnp.bfloat16).reshape(8, BLK, BLK)

        @pl.when(core == 1)
        def _():
            for s in range(0, 8, 2):
                pair = jnp.concatenate([weights[d, r, s], weights[d, r, s + 1]], axis=1)
                scatter(s, jnp.dot(mine, pair, preferred_element_type=jnp.float32))
            grad = lax.dot_general(
                mine, picked[...], (((0,), (0,)), ((), ())), preferred_element_type=jnp.float32
            ).astype(jnp.bfloat16)
            for s in range(8):
                grads[d, r, s] = grad[:, s * BLK : (s + 1) * BLK]

        return carry

    lax.fori_loop(0, 8, body, 0)
    backs = []
    for n, dst in enumerate((g0, g1, g2, g3)):
        backs.append(pltpu.make_async_copy(grads.at[n], dst, sems.at[n]))
        backs[-1].start()
    for n, dst in enumerate((o0, o1, o2, o3)):
        out[n] = acc[n].astype(jnp.bfloat16)
        backs.append(pltpu.make_async_copy(out.at[n], dst, sems.at[4 + n]))
        backs[-1].start()
    for copy in backs:
        copy.wait()


SMEM = pl.BlockSpec(memory_space=pltpu.SMEM)
VMEM = pl.BlockSpec(memory_space=pltpu.VMEM)
ANY = pl.BlockSpec(memory_space=pl.ANY)
ACTS = (RING, RING, 2, BLK, 512)
WEIGHTS = (RING, 2, 8, BLK, BLK)


def enter(where, codes, acts, weights):
    return pl.pallas_call(
        enter_kernel,
        out_shape=jax.ShapeDtypeStruct((8, 512, BLK), jnp.float32),
        in_specs=[SMEM, SMEM] + [ANY] * 8,
        out_specs=VMEM,
        scratch_shapes=[
            pltpu.VMEM(ACTS, jnp.bfloat16),
            pltpu.VMEM(WEIGHTS, jnp.bfloat16),
            pltpu.VMEM((512, 8 * BLK), jnp.bfloat16),
            pltpu.SemaphoreType.DMA((8,)),
        ],
        compiler_params=pltpu.CompilerParams(vmem_limit_bytes=20 << 20),
        cost_estimate=pl.CostEstimate(
            flops=1 << 30, bytes_accessed=8 << 20, transcendentals=0
        ),
        name="enter",
    )(where, codes, *acts, *weights)


def leave(where, codes, left, acts, weights):
    chunk = jax.ShapeDtypeStruct(ACTS[1:], jnp.bfloat16)
    grad = jax.ShapeDtypeStruct(WEIGHTS[1:], jnp.bfloat16)
    results = pl.pallas_call(
        leave_kernel,
        out_shape=[chunk] * 4 + [grad] * 4,
        in_specs=[SMEM, SMEM, VMEM] + [ANY] * 8,
        out_specs=[ANY] * 8,
        scratch_shapes=[
            pltpu.VMEM(ACTS, jnp.bfloat16),
            pltpu.VMEM(WEIGHTS, jnp.bfloat16),
            pltpu.VMEM((512, 8 * BLK), jnp.bfloat16),
            pltpu.VMEM(ACTS, jnp.float32),
            pltpu.VMEM(ACTS, jnp.bfloat16),
            pltpu.VMEM(WEIGHTS, jnp.bfloat16),
            pltpu.SemaphoreType.DMA((8,)),
        ],
        compiler_params=pltpu.CompilerParams(vmem_limit_bytes=32 << 20),
        cost_estimate=pl.CostEstimate(
            flops=2 << 30, bytes_accessed=12 << 20, transcendentals=0
        ),
        name="leave",
    )(where, codes, left, *acts, *weights)
    return results[:4], results[4:]


def per_device(tokens, up_weight, up_rows, down_weight, down_cols, grad_out):
    x, y, z = (lax.axis_index(name) for name in ("x", "y", "z"))
    core = lax.axis_index("core")
    up = core == 0

    def first(stage):
        return lambda values, step: mixed_shift(values, step, stage)

    kept = jnp.where(up, tokens, grad_out)
    acts = jnp.stack([kept, swap(jnp.where(up, grad_out, tokens))])
    kept = jnp.where(up, up_weight[0], down_weight[0])
    weights = jnp.stack([kept, swap(jnp.where(up, down_weight[0], up_weight[0]))])

    up_ids = lax.dynamic_index_in_dim(up_rows.reshape(4, 4, 8), x, axis=1, keepdims=False)
    down_ids = lax.dynamic_index_in_dim(down_cols.reshape(4, 4, 8), x, axis=1, keepdims=False)
    ids = jnp.stack([jnp.where(up, up_ids, down_ids), swap(jnp.where(up, down_ids, up_ids))])
    codes = ((y - (ids >> 3)) & 3) * 8 + (((ids >> 2) & 1) ^ core) * 4 + (ids & 3)
    where = jnp.stack([core, z])

    acts = gather(jnp.stack(gather(acts, first(True))), first(False))
    weights = gather(weights, z_shift)

    entered = enter(where, codes, acts, weights)
    pre = lax.ppermute(entered, "core", [(0, 1)])
    t = jnp.tanh(GELU_SCALE * (pre + GELU_CUBIC * pre * pre * pre))
    hidden = (0.5 * pre * (1.0 + t)).astype(jnp.bfloat16)
    slope = 0.5 * (1.0 + t) + 0.5 * pre * (1.0 - t * t) * GELU_SCALE * (
        1.0 + 3.0 * GELU_CUBIC * pre * pre
    )
    grad_pre = lax.ppermute((entered * slope).astype(jnp.bfloat16), "core", [(1, 0)])
    chunks, grads = leave(where, codes, jnp.where(up, grad_pre, hidden), acts, weights)

    summed = reduce(chunks, first(False)).astype(jnp.bfloat16)
    final = reduce([summed[n] for n in range(RING)], first(True)).astype(jnp.bfloat16)
    grad_scale = 1.0 / math.sqrt(tokens.shape[0] * lax.axis_size("z") * lax.axis_size("x"))
    scaled = (reduce(grads, z_shift) * grad_scale).astype(jnp.bfloat16)
    came = swap(final[1])
    came_grad = swap(scaled[1])
    layer_out = jnp.where(up, came, final[0])
    grad_tokens = jnp.where(up, final[0], came)
    grad_up = jnp.where(up, scaled[0], came_grad)
    grad_down = jnp.where(up, came_grad, scaled[0])
    return (layer_out, grad_tokens, grad_up[None], grad_down[None])


def solution(mesh):
    grid = Mesh(mesh.devices.reshape(4, 4, 4, 2), ("z", "x", "y", "core"))
    row, col = ("z", "x"), ("y", "core")
    acts, ids = P(row, col), P(col, None)
    blocks = P(col + row, None, None, None)
    return jax.shard_map(
        per_device,
        mesh=grid,
        in_specs=(acts, blocks, ids, blocks, ids, acts),
        out_specs=(acts, acts, blocks, blocks),
        check_vma=False,
    )
```

time: 154 us -> 131 us (0.85)
  between operations: 14.2 us -> 0.79 us
  waiting for transfers between devices: 70.6 us -> 57.9 us
  local copies, waits for them, and re-layouts: 7.18 us -> 0.26 us
  Pallas kernels: 14.7 us -> 20.8 us
  starting transfers between devices: 41.7 us -> 43.9 us
    ppermute x24 -> x20, waiting for transfers between devices: 68.6 us -> 56.9 us  [the longest x6 27.9 us: z_shift(): lax.ppermute(values, 'z', [(i, (i + step) % RING) for i in range(RING)])]
    pallas_call x1 -> x2, Pallas kernels: 14.7 us -> 20.8 us  [the longest x1 12.1 us: leave(): pl.pallas_call(leave_kernel, out_shape=[chunk] * 4 + [grad] * 4, in_specs...]
    unnamed x26 -> x6, local copies, waits for them, and re-layouts: 6.25 us -> 0.15 us
    select_n x1 -> x4, other arithmetic: 0.02 us -> 2.61 us  [the longest x1 1.07 us: per_device(): kept = jnp.where(up, up_weight[0], down_weight[0])]
    ppermute x3 -> x5, starting transfers between devices: 9.39 us -> 11.8 us  [swap(): return lax.ppermute(values, 'core', [(0, 1), (1, 0)])]
    another operation x8 -> x5, other arithmetic: 3.04 us -> 1.28 us  [the longest x1 0.99 us: per_device(): acts = jnp.stack([kept, swap(jnp.where(up, grad_out, tokens))])]
    ppermute x24 -> x20, starting transfers between devices: 32.2 us -> 32.1 us  [the longest x12 17 us: mixed_shift(): return lax.ppermute(values, MIXED, mixed_pairs(step, first))]
  transfers between devices with their start and end apart: 29 -> 25, of which waited for: 15 -> 11; matrix products, arithmetic and copies ran while one was open for 2% -> 3% of each run, Pallas kernels for 0% -> 0%
where the time goes in v2:
time: 131 us
  waiting for transfers between devices  57.9 us (44%)
  starting transfers between devices  43.9 us (34%)
  Pallas kernels  20.8 us (16%)
  other arithmetic  7.17 us (5%)
    ppermute x6, waiting for transfers between devices, z_shift(): lax.ppermute(values, 'z', [(i, (i + step) % RING) for i in range(RING)])  27.9 us
    ppermute x12, waiting for transfers between devices, mixed_shift(): return lax.ppermute(values, MIXED, mixed_pairs(step, first))  22.1 us
    ppermute x12, starting transfers between devices, mixed_shift(): return lax.ppermute(values, MIXED, mixed_pairs(step, first))  17 us
    pallas_call x1, Pallas kernels, leave(): pl.pallas_call(leave_kernel, out_shape=[chunk] * 4 + [grad] * 4, in_specs...  12.1 us
    ppermute x5, starting transfers between devices, swap(): return lax.ppermute(values, 'core', [(0, 1), (1, 0)])  11.8 us
    ppermute x6, starting transfers between devices, z_shift(): lax.ppermute(values, 'z', [(i, (i + step) % RING) for i in range(RING)])  11.7 us
    pallas_call x1, Pallas kernels, enter(): pl.pallas_call(enter_kernel, out_shape=jax.ShapeDtypeStruct((8, 512, BLK)...  8.71 us
    ppermute x1, waiting for transfers between devices, per_device(): pre = lax.ppermute(entered, 'core', [(0, 1)])  4.75 us
  transfers between devices with their start and end apart: 25, of which 11 were waited for; matrix products, arithmetic and copies ran while one was open for 3% of the time, Pallas kernels for 0%

profile of v2, /device:TPU:1, one launch (start us, length us, event | category | flops | bytes accessed | tf_op | source)
XLA Modules:
  0.0 130.8 jit_solution(3794446106947728513)
XLA Ops:
  0.6 1.0 select_bitcast_fusion.3
  1.6 1.5 %collective-permute-start.1 = (bf16[128,512]{1,0:T(8,128)(2,1)S(1)}, bf16[128,512]{1,0:T(8,128)(2,1)S(1)}, u32[]{:S(2)}, u32[]{:S(2)}) collective-permute-start(bf16[128,512]{1,0:T(8,128)(2,1)S(1)} %get-tuple-element.32), channel_id=1, source_target_pairs={{0,1},{1,0},{2,3},{3,2},{4,5},{5,4},{6,7},{7,6},{8,9},{9,8},{10,11... | collective-permute-start | bytes 393224 | tf_op jit(solution)/shard_map/ppermute | solution.py:42
  3.1 1.1 broadcast_select_fusion
  4.2 0.0 copy-start
  4.2 0.0 copy-start.1
  4.2 0.1 collective-permute-start.8
  4.3 0.0 collective-permute-done.1
  4.4 3.1 %collective-permute-start.3 = (bf16[2,128,512]{2,1,0:T(8,128)(2,1)S(1)}, bf16[2,128,512]{2,1,0:T(8,128)(2,1)S(1)}, u32[]{:S(2)}, u32[]{:S(2)}) collective-permute-start(bf16[2,128,512]{2,1,0:T(8,128)(2,1)S(1)} %get-tuple-element.30), channel_id=1, source_target_pairs={{0,16},{1,5},{2,18},{3,7},{4,20},{5,1},{6,22},{7,3},{8,24},{9,13},... | collective-permute-start | bytes 786440 | tf_op jit(solution)/shard_map/ppermute | solution.py:34
  7.5 0.4 collective-permute-start.2
  7.9 2.3 %collective-permute-start.4 = (bf16[2,128,512]{2,1,0:T(8,128)(2,1)S(1)}, bf16[2,128,512]{2,1,0:T(8,128)(2,1)S(1)}, u32[]{:S(2)}, u32[]{:S(2)}) collective-permute-start(bf16[2,128,512]{2,1,0:T(8,128)(2,1)S(1)} %get-tuple-element.30), channel_id=1, source_target_pairs={{0,24},{1,7},{2,26},{3,1},{4,28},{5,3},{6,30},{7,5},{8,0},{9,15},{... | collective-permute-start | bytes 786440 | tf_op jit(solution)/shard_map/ppermute | solution.py:34
  10.1 0.0 collective-permute-done.8
  10.1 0.1 pad_maximum_fusion.1.w0
  10.2 3.8 %collective-permute-start.11 = (bf16[2,8,128,128]{3,2,1,0:T(8,128)(2,1)S(1)}, bf16[2,8,128,128]{3,2,1,0:T(8,128)(2,1)S(1)}, u32[]{:S(2)}, u32[]{:S(2)}) collective-permute-start(bf16[2,8,128,128]{3,2,1,0:T(8,128)(2,1)S(1)} %pad_maximum_fusion.1.w0), channel_id=1, source_target_pairs={{0,96},{32,0},{64,32},{96,64},{1,97},{33,1},{65,33},{97,65},{2,98}... | collective-permute-start | bytes 1572872 | tf_op jit(solution)/shard_map/ppermute | solution.py:38
  14.0 0.3 collective-permute-done.2
  14.3 0.4 collective-permute-done.4
  14.7 0.1 pad_maximum_fusion.a0
  14.8 2.5 %collective-permute-start.7 = (bf16[4,2,128,512]{3,2,1,0:T(8,128)(2,1)S(1)}, bf16[4,2,128,512]{3,2,1,0:T(8,128)(2,1)S(1)}, u32[]{:S(2)}, u32[]{:S(2)}) collective-permute-start(bf16[4,2,128,512]{3,2,1,0:T(8,128)(2,1)S(1)} %pad_maximum_fusion.a0), channel_id=1, source_target_pairs={{0,6},{1,25},{2,0},{3,27},{4,2},{5,29},{6,4},{7,31},{8,14},{9,1},{... | collective-permute-start | bytes 3145736 | tf_op jit(solution)/shard_map/ppermute | solution.py:34
  17.4 0.5 collective-permute-start.6
  17.9 0.6 collective-permute-start.5
  18.5 0.1 copy.10
  18.6 0.1 copy.11
  18.7 2.2 %collective-permute-start = (s32[4,8]{1,0:T(4,128)S(1)}, s32[4,8]{1,0:T(4,128)S(1)}, u32[]{:S(2)}, u32[]{:S(2)}) collective-permute-start(s32[4,8]{1,0:T(4,128)S(1)} %bitcast.58), channel_id=1, source_target_pairs={{0,1},{1,0},{2,3},{3,2},{4,5},{5,4},{6,7},{7,6},{8,9},{9,8},{10,11... | collective-permute-start | bytes 392 | tf_op jit(solution)/shard_map/ppermute | solution.py:42
  20.9 0.8 collective-permute-done
  21.7 3.6 %collective-permute-start.10 = (bf16[2,8,128,128]{3,2,1,0:T(8,128)(2,1)S(1)}, bf16[2,8,128,128]{3,2,1,0:T(8,128)(2,1)}, u32[]{:S(2)}, u32[]{:S(2)}) collective-permute-start(bf16[2,8,128,128]{3,2,1,0:T(8,128)(2,1)S(1)} %pad_maximum_fusion.1.w0), channel_id=1, source_target_pairs={{0,64},{32,96},{64,0},{96,32},{1,65},{33,97},{65,1},{97,33},{2,66}... | collective-permute-start | bytes 1572872 | tf_op jit(solution)/shard_map/ppermute | solution.py:38
  25.3 0.0 collective-permute-done.11.w3
  25.3 0.7 collective-permute-start.9
  26.0 0.1 pad_add_fusion.1.where_ref
  26.1 11.4 %collective-permute-done.10.w2 = bf16[2,8,128,128]{3,2,1,0:T(8,128)(2,1)} collective-permute-done((bf16[2,8,128,128]{3,2,1,0:T(8,128)(2,1)S(1)}, bf16[2,8,128,128]{3,2,1,0:T(8,128)(2,1)}, u32[]{:S(2)}, u32[]{:S(2)}) %collective-permute-start.10) | collective-permute-done | bytes 524320 | tf_op jit(solution)/shard_map/ppermute | solution.py:38
  37.5 11.5 %collective-permute-done.9.w1 = bf16[2,8,128,128]{3,2,1,0:T(8,128)(2,1)} collective-permute-done((bf16[2,8,128,128]{3,2,1,0:T(8,128)(2,1)S(1)}, bf16[2,8,128,128]{3,2,1,0:T(8,128)(2,1)}, u32[]{:S(2)}, u32[]{:S(2)}) %collective-permute-start.9) | collective-permute-done | bytes 524320 | tf_op jit(solution)/shard_map/ppermute | solution.py:38
  49.0 0.0 collective-permute-done.7.a3
  49.0 0.0 collective-permute-done.6.a2
  49.0 8.7 %enter.1 = f32[8,512,128]{2,1,0:T(8,128)S(1)} custom-call(s32[2]{0:T(128)S(1)} %pad_add_fusion.1.where_ref, s32[2,4,8]{2,1,0:T(4,128)S(1)} %and_add_fusion.codes_ref, bf16[4,2,128,512]{3,2,1,0:T(8,128)(2,1)S(1)} %pad_maximum_fusion.a0, bf16[4,2,128,512]{3,2,1,0:T(8,128)(2,1)} %collective-permute-done.5.a1, ...), custom_call_target="tpu_custom_call" | custom-call | flops 1073741824 | bytes 8388608 | tf_op jit(solution)/shard_map/enter/pallas_call | solution.py:197
  57.7 1.3 collective-permute-start.12
  59.0 4.8 %collective-permute-done.12 = f32[8,512,128]{2,1,0:T(8,128)S(1)} collective-permute-done((f32[8,512,128]{2,1,0:T(8,128)S(1)}, f32[8,512,128]{2,1,0:T(8,128)S(1)}, u32[]{:S(2)}, u32[]{:S(2)}) %collective-permute-start.12) | collective-permute-done | bytes 2097184 | tf_op jit(solution)/shard_map/ppermute | solution.py:265
  63.8 1.4 %fusion.6 = bf16[8,512,128]{2,1,0:T(8,128)(2,1)S(1)} fusion(f32[8,512,128]{2,1,0:T(8,128)S(1)} %enter.1, f32[8,512,128]{2,1,0:T(8,128)S(1)} %collective-permute-done.12), kind=kLoop, calls=%fused_computation.8 | loop fusion | flops 9961472 | bytes 5242880 | tf_op jit(solution)/shard_map/convert_element_type | solution.py:271
  65.1 2.1 %collective-permute-start.13 = (bf16[8,512,128]{2,1,0:T(8,128)(2,1)S(1)}, bf16[8,512,128]{2,1,0:T(8,128)(2,1)S(1)}, u32[]{:S(2)}, u32[]{:S(2)}) collective-permute-start(bf16[8,512,128]{2,1,0:T(8,128)(2,1)S(1)} %fusion.6), channel_id=1, source_target_pairs={{1,0},{3,2},{5,4},{7,6},{9,8},{11,10},{13,12},{15,14},{17,16},{19,... | collective-permute-start | bytes 3145736 | tf_op jit(solution)/shard_map/ppermute | solution.py:271
  67.3 2.2 %collective-permute-done.13 = bf16[8,512,128]{2,1,0:T(8,128)(2,1)S(1)} collective-permute-done((bf16[8,512,128]{2,1,0:T(8,128)(2,1)S(1)}, bf16[8,512,128]{2,1,0:T(8,128)(2,1)S(1)}, u32[]{:S(2)}, u32[]{:S(2)}) %collective-permute-start.13) | collective-permute-done | bytes 1048608 | tf_op jit(solution)/shard_map/ppermute | solution.py:271
  69.5 0.8 fusion.7.left
  70.3 12.1 %leave.1 = (bf16[4,2,128,512]{3,2,1,0:T(8,128)(2,1)S(1)}, bf16[4,2,128,512]{3,2,1,0:T(8,128)(2,1)S(1)}, bf16[4,2,128,512]{3,2,1,0:T(8,128)(2,1)S(1)}, bf16[4,2,1...) custom-call(s32[2]{0:T(128)S(1)} %pad_add_fusion.1.where_ref, ...), custom_call_target="tpu_custom_call" | custom-call | flops 2147483648 | bytes 12582912 | tf_op jit(solution)/shard_map/leave/pallas_call | solution.py:219
  82.4 2.8 %collective-permute-start.14 = (bf16[4,2,128,512]{3,2,1,0:T(8,128)(2,1)S(1)}, bf16[4,2,128,512]{3,2,1,0:T(8,128)(2,1)S(1)}, u32[]{:S(2)}, u32[]{:S(2)}) collective-permute-start(bf16[4,2,128,512]{3,2,1,0:T(8,128)(2,1)S(1)} %get-tuple-element.13), channel_id=1, source_target_pairs={{0,6},{1,25},{2,0},{3,27},{4,2},{5,29},{6,4},{7,31},{8,14},{9,1},{... | collective-permute-start | bytes 3145736 | tf_op jit(solution)/shard_map/ppermute | solution.py:34
  85.2 0.0 collective-permute-start.15
  85.2 1.4 %collective-permute-start.16 = (bf16[4,2,128,512]{3,2,1,0:T(8,128)(2,1)S(1)}, bf16[4,2,128,512]{3,2,1,0:T(8,128)(2,1)S(1)}, u32[]{:S(2)}, u32[]{:S(2)}) collective-permute-start(bf16[4,2,128,512]{3,2,1,0:T(8,128)(2,1)S(1)} %get-tuple-element.15), channel_id=1, source_target_pairs={{0,4},{1,17},{2,6},{3,19},{4,0},{5,21},{6,2},{7,23},{8,12},{9,25},... | collective-permute-start | bytes 3145736 | tf_op jit(solution)/shard_map/ppermute | solution.py:34
  86.7 0.3 collective-permute-start.21
  87.0 1.2 collective-permute-start.22
  88.1 20.1 %collective-permute-done.14 = bf16[4,2,128,512]{3,2,1,0:T(8,128)(2,1)S(1)} collective-permute-done((bf16[4,2,128,512]{3,2,1,0:T(8,128)(2,1)S(1)}, bf16[4,2,128,512]{3,2,1,0:T(8,128)(2,1)S(1)}, u32[]{:S(2)}, u32[]{:S(2)}) %collective-permute-start.14) | collective-permute-done | bytes 1048608 | tf_op jit(solution)/shard_map/ppermute | solution.py:34
  108.2 2.1 %collective-permute-start.23 = (bf16[2,8,128,128]{3,2,1,0:T(8,128)(2,1)S(1)}, bf16[2,8,128,128]{3,2,1,0:T(8,128)(2,1)S(1)}, u32[]{:S(2)}, u32[]{:S(2)}) collective-permute-start(bf16[2,8,128,128]{3,2,1,0:T(8,128)(2,1)S(1)} %get-tuple-element.19), channel_id=1, source_target_pairs={{0,64},{32,96},{64,0},{96,32},{1,65},{33,97},{65,1},{97,33},{2,66}... | collective-permute-start | bytes 1572872 | tf_op jit(solution)/shard_map/ppermute | solution.py:38
  110.3 1.3 collective-permute-done.15
  111.6 0.0 collective-permute-done.16
  111.6 0.6 add_convert_fusion
  112.2 0.1 slice_bitcast_fusion.4
  112.3 2.1 %collective-permute-start.17 = (bf16[2,128,512]{2,1,0:T(8,128)(2,1)S(1)}, bf16[2,128,512]{2,1,0:T(8,128)(2,1)S(1)}, u32[]{:S(2)}, u32[]{:S(2)}) collective-permute-start(bf16[2,128,512]{2,1,0:T(8,128)(2,1)S(1)} %get-tuple-element.20), channel_id=1, source_target_pairs={{0,24},{1,7},{2,26},{3,1},{4,28},{5,3},{6,30},{7,5},{8,0},{9,15},{... | collective-permute-start | bytes 786440 | tf_op jit(solution)/shard_map/ppermute | solution.py:34
  114.3 1.2 collective-permute-start.19
  115.6 0.0 collective-permute-start.18
  115.6 0.0 collective-permute-done.22
  115.6 5.0 %collective-permute-done.23 = bf16[2,8,128,128]{3,2,1,0:T(8,128)(2,1)S(1)} collective-permute-done((bf16[2,8,128,128]{3,2,1,0:T(8,128)(2,1)S(1)}, bf16[2,8,128,128]{3,2,1,0:T(8,128)(2,1)S(1)}, u32[]{:S(2)}, u32[]{:S(2)}) %collective-permute-start.23) | collective-permute-done | bytes 524320 | tf_op jit(solution)/shard_map/ppermute | solution.py:38
  120.5 0.3 multiply_convert_fusion.1
  120.9 3.6 %collective-permute-start.24 = (bf16[8,128,128]{2,1,0:T(8,128)(2,1)S(1)}, bf16[8,128,128]{2,1,0:T(8,128)(2,1)S(1)}, u32[]{:S(2)}, u32[]{:S(2)}) collective-permute-start(bf16[8,128,128]{2,1,0:T(8,128)(2,1)S(1)} %slice_bitcast_fusion), channel_id=1, source_target_pairs={{0,1},{1,0},{2,3},{3,2},{4,5},{5,4},{6,7},{7,6},{8,9},{9,8},{10,11... | collective-permute-start | bytes 786440 | tf_op jit(solution)/shard_map/ppermute | solution.py:42
  124.5 0.0 collective-permute-done.17
  124.5 0.0 collective-permute-done.19
  124.5 0.1 fusion.10
  124.7 4.4 %collective-permute-start.20 = (bf16[128,512]{1,0:T(8,128)(2,1)S(1)}, bf16[128,512]{1,0:T(8,128)(2,1)S(1)}, u32[]{:S(2)}, u32[]{:S(2)}) collective-permute-start(bf16[128,512]{1,0:T(8,128)(2,1)S(1)} %slice_bitcast_fusion.7), channel_id=1, source_target_pairs={{0,1},{1,0},{2,3},{3,2},{4,5},{5,4},{6,7},{7,6},{8,9},{9,8},{10,11... | collective-permute-start | bytes 393224 | tf_op jit(solution)/shard_map/ppermute | solution.py:42
  129.1 0.8 select_bitcast_fusion
  129.9 0.2 collective-permute-done.20
  130.1 0.7 broadcast_select_fusion.1
  (12 shorter events, 0.1 us)
Async XLA Ops:
  1.6 2.7 %collective-permute-start.1 = (bf16[128,512]{1,0:T(8,128)(2,1)S(1)}, bf16[128,512]{1,0:T(8,128)(2,1)S(1)}, u32[]{:S(2)}, u32[]{:S(2)}) collective-permute-start(bf16[128,512]{1,0:T(8,128)(2,1)S(1)} %get-tuple-element.32), channel_id=1, source_target_pairs={{0,1},{1,0},{2,3},{3,2},{4,5},{5,4},{6,7},{7,6},{8,9},{9,8},{10,11... | collective-permute-start | bytes 393224 | tf_op jit(solution)/shard_map/ppermute | solution.py:42
  4.2 14.3 %copy-start = (s32[16,8]{0,1:T(8,128)S(1)}, s32[16,8]{0,1:T(8,128)}, u32[]{:S(2)}) copy-start(s32[16,8]{0,1:T(8,128)} %param.8) | copy-start | bytes 1540
  4.2 14.4 %copy-start.1 = (s32[16,8]{0,1:T(8,128)S(1)}, s32[16,8]{0,1:T(8,128)}, u32[]{:S(2)}) copy-start(s32[16,8]{0,1:T(8,128)} %param.10) | copy-start | bytes 1540
  4.2 5.9 %collective-permute-start.8 = (bf16[8,128,128]{2,1,0:T(8,128)(2,1)S(1)}, bf16[8,128,128]{2,1,0:T(8,128)(2,1)S(1)}, u32[]{:S(2)}, u32[]{:S(2)}) collective-permute-start(bf16[8,128,128]{2,1,0:T(8,128)(2,1)S(1)} %get-tuple-element.26), channel_id=1, source_target_pairs={{0,1},{1,0},{2,3},{3,2},{4,5},{5,4},{6,7},{7,6},{8,9},{9,8},{10,11... | collective-permute-start | bytes 786440 | tf_op jit(solution)/shard_map/ppermute | solution.py:42
  4.4 9.6 %collective-permute-start.3 = (bf16[2,128,512]{2,1,0:T(8,128)(2,1)S(1)}, bf16[2,128,512]{2,1,0:T(8,128)(2,1)S(1)}, u32[]{:S(2)}, u32[]{:S(2)}) collective-permute-start(bf16[2,128,512]{2,1,0:T(8,128)(2,1)S(1)} %get-tuple-element.30), channel_id=1, source_target_pairs={{0,16},{1,5},{2,18},{3,7},{4,20},{5,1},{6,22},{7,3},{8,24},{9,13},... | collective-permute-start | bytes 786440 | tf_op jit(solution)/shard_map/ppermute | solution.py:34
  7.5 6.9 %collective-permute-start.2 = (bf16[2,128,512]{2,1,0:T(8,128)(2,1)S(1)}, bf16[2,128,512]{2,1,0:T(8,128)(2,1)S(1)}, u32[]{:S(2)}, u32[]{:S(2)}) collective-permute-start(bf16[2,128,512]{2,1,0:T(8,128)(2,1)S(1)} %get-tuple-element.30), channel_id=1, source_target_pairs={{0,8},{1,3},{2,10},{3,5},{4,12},{5,7},{6,14},{7,1},{8,16},{9,11},{... | collective-permute-start | bytes 786440 | tf_op jit(solution)/shard_map/ppermute | solution.py:34
  7.9 6.9 %collective-permute-start.4 = (bf16[2,128,512]{2,1,0:T(8,128)(2,1)S(1)}, bf16[2,128,512]{2,1,0:T(8,128)(2,1)S(1)}, u32[]{:S(2)}, u32[]{:S(2)}) collective-permute-start(bf16[2,128,512]{2,1,0:T(8,128)(2,1)S(1)} %get-tuple-element.30), channel_id=1, source_target_pairs={{0,24},{1,7},{2,26},{3,1},{4,28},{5,3},{6,30},{7,5},{8,0},{9,15},{... | collective-permute-start | bytes 786440 | tf_op jit(solution)/shard_map/ppermute | solution.py:34
  10.2 15.1 %collective-permute-start.11 = (bf16[2,8,128,128]{3,2,1,0:T(8,128)(2,1)S(1)}, bf16[2,8,128,128]{3,2,1,0:T(8,128)(2,1)S(1)}, u32[]{:S(2)}, u32[]{:S(2)}) collective-permute-start(bf16[2,8,128,128]{3,2,1,0:T(8,128)(2,1)S(1)} %pad_maximum_fusion.1.w0), channel_id=1, source_target_pairs={{0,96},{32,0},{64,32},{96,64},{1,97},{33,1},{65,33},{97,65},{2,98}... | collective-permute-start | bytes 1572872 | tf_op jit(solution)/shard_map/ppermute | solution.py:38
  14.8 34.2 %collective-permute-start.7 = (bf16[4,2,128,512]{3,2,1,0:T(8,128)(2,1)S(1)}, bf16[4,2,128,512]{3,2,1,0:T(8,128)(2,1)S(1)}, u32[]{:S(2)}, u32[]{:S(2)}) collective-permute-start(bf16[4,2,128,512]{3,2,1,0:T(8,128)(2,1)S(1)} %pad_maximum_fusion.a0), channel_id=1, source_target_pairs={{0,6},{1,25},{2,0},{3,27},{4,2},{5,29},{6,4},{7,31},{8,14},{9,1},{... | collective-permute-start | bytes 3145736 | tf_op jit(solution)/shard_map/ppermute | solution.py:34
  17.4 31.6 %collective-permute-start.6 = (bf16[4,2,128,512]{3,2,1,0:T(8,128)(2,1)S(1)}, bf16[4,2,128,512]{3,2,1,0:T(8,128)(2,1)}, u32[]{:S(2)}, u32[]{:S(2)}) collective-permute-start(bf16[4,2,128,512]{3,2,1,0:T(8,128)(2,1)S(1)} %pad_maximum_fusion.a0), channel_id=1, source_target_pairs={{0,4},{1,17},{2,6},{3,19},{4,0},{5,21},{6,2},{7,23},{8,12},{9,25},... | collective-permute-start | bytes 3145736 | tf_op jit(solution)/shard_map/ppermute | solution.py:34
  17.9 31.1 %collective-permute-start.5 = (bf16[4,2,128,512]{3,2,1,0:T(8,128)(2,1)S(1)}, bf16[4,2,128,512]{3,2,1,0:T(8,128)(2,1)}, u32[]{:S(2)}, u32[]{:S(2)}) collective-permute-start(bf16[4,2,128,512]{3,2,1,0:T(8,128)(2,1)S(1)} %pad_maximum_fusion.a0), channel_id=1, source_target_pairs={{0,2},{1,9},{2,4},{3,11},{4,6},{5,13},{6,0},{7,15},{8,10},{9,17},{... | collective-permute-start | bytes 3145736 | tf_op jit(solution)/shard_map/ppermute | solution.py:34
  18.7 3.0 %collective-permute-start = (s32[4,8]{1,0:T(4,128)S(1)}, s32[4,8]{1,0:T(4,128)S(1)}, u32[]{:S(2)}, u32[]{:S(2)}) collective-permute-start(s32[4,8]{1,0:T(4,128)S(1)} %bitcast.58), channel_id=1, source_target_pairs={{0,1},{1,0},{2,3},{3,2},{4,5},{5,4},{6,7},{7,6},{8,9},{9,8},{10,11... | collective-permute-start | bytes 392 | tf_op jit(solution)/shard_map/ppermute | solution.py:42
  21.7 15.8 %collective-permute-start.10 = (bf16[2,8,128,128]{3,2,1,0:T(8,128)(2,1)S(1)}, bf16[2,8,128,128]{3,2,1,0:T(8,128)(2,1)}, u32[]{:S(2)}, u32[]{:S(2)}) collective-permute-start(bf16[2,8,128,128]{3,2,1,0:T(8,128)(2,1)S(1)} %pad_maximum_fusion.1.w0), channel_id=1, source_target_pairs={{0,64},{32,96},{64,0},{96,32},{1,65},{33,97},{65,1},{97,33},{2,66}... | collective-permute-start | bytes 1572872 | tf_op jit(solution)/shard_map/ppermute | solution.py:38
  25.3 23.7 %collective-permute-start.9 = (bf16[2,8,128,128]{3,2,1,0:T(8,128)(2,1)S(1)}, bf16[2,8,128,128]{3,2,1,0:T(8,128)(2,1)}, u32[]{:S(2)}, u32[]{:S(2)}) collective-permute-start(bf16[2,8,128,128]{3,2,1,0:T(8,128)(2,1)S(1)} %pad_maximum_fusion.1.w0), channel_id=1, source_target_pairs={{0,32},{32,64},{64,96},{96,0},{1,33},{33,65},{65,97},{97,1},{2,34}... | collective-permute-start | bytes 1572872 | tf_op jit(solution)/shard_map/ppermute | solution.py:38
  57.7 6.1 %collective-permute-start.12 = (f32[8,512,128]{2,1,0:T(8,128)S(1)}, f32[8,512,128]{2,1,0:T(8,128)S(1)}, u32[]{:S(2)}, u32[]{:S(2)}) collective-permute-start(f32[8,512,128]{2,1,0:T(8,128)S(1)} %enter.1), channel_id=1, source_target_pairs={{0,1},{2,3},{4,5},{6,7},{8,9},{10,11},{12,13},{14,15},{16,17},{18,... | collective-permute-start | bytes 6291464 | tf_op jit(solution)/shard_map/ppermute | solution.py:265
  65.1 4.3 %collective-permute-start.13 = (bf16[8,512,128]{2,1,0:T(8,128)(2,1)S(1)}, bf16[8,512,128]{2,1,0:T(8,128)(2,1)S(1)}, u32[]{:S(2)}, u32[]{:S(2)}) collective-permute-start(bf16[8,512,128]{2,1,0:T(8,128)(2,1)S(1)} %fusion.6), channel_id=1, source_target_pairs={{1,0},{3,2},{5,4},{7,6},{9,8},{11,10},{13,12},{15,14},{17,16},{19,... | collective-permute-start | bytes 3145736 | tf_op jit(solution)/shard_map/ppermute | solution.py:271
  82.4 25.8 %collective-permute-start.14 = (bf16[4,2,128,512]{3,2,1,0:T(8,128)(2,1)S(1)}, bf16[4,2,128,512]{3,2,1,0:T(8,128)(2,1)S(1)}, u32[]{:S(2)}, u32[]{:S(2)}) collective-permute-start(bf16[4,2,128,512]{3,2,1,0:T(8,128)(2,1)S(1)} %get-tuple-element.13), channel_id=1, source_target_pairs={{0,6},{1,25},{2,0},{3,27},{4,2},{5,29},{6,4},{7,31},{8,14},{9,1},{... | collective-permute-start | bytes 3145736 | tf_op jit(solution)/shard_map/ppermute | solution.py:34
  85.2 26.4 %collective-permute-start.15 = (bf16[4,2,128,512]{3,2,1,0:T(8,128)(2,1)S(1)}, bf16[4,2,128,512]{3,2,1,0:T(8,128)(2,1)S(1)}, u32[]{:S(2)}, u32[]{:S(2)}) collective-permute-start(bf16[4,2,128,512]{3,2,1,0:T(8,128)(2,1)S(1)} %get-tuple-element.14), channel_id=1, source_target_pairs={{0,2},{1,9},{2,4},{3,11},{4,6},{5,13},{6,0},{7,15},{8,10},{9,17},{... | collective-permute-start | bytes 3145736 | tf_op jit(solution)/shard_map/ppermute | solution.py:34
  85.2 26.4 %collective-permute-start.16 = (bf16[4,2,128,512]{3,2,1,0:T(8,128)(2,1)S(1)}, bf16[4,2,128,512]{3,2,1,0:T(8,128)(2,1)S(1)}, u32[]{:S(2)}, u32[]{:S(2)}) collective-permute-start(bf16[4,2,128,512]{3,2,1,0:T(8,128)(2,1)S(1)} %get-tuple-element.15), channel_id=1, source_target_pairs={{0,4},{1,17},{2,6},{3,19},{4,0},{5,21},{6,2},{7,23},{8,12},{9,25},... | collective-permute-start | bytes 3145736 | tf_op jit(solution)/shard_map/ppermute | solution.py:34
  86.7 28.9 %collective-permute-start.21 = (bf16[2,8,128,128]{3,2,1,0:T(8,128)(2,1)S(1)}, bf16[2,8,128,128]{3,2,1,0:T(8,128)(2,1)S(1)}, u32[]{:S(2)}, u32[]{:S(2)}) collective-permute-start(bf16[2,8,128,128]{3,2,1,0:T(8,128)(2,1)S(1)} %get-tuple-element.17), channel_id=1, source_target_pairs={{0,96},{32,0},{64,32},{96,64},{1,97},{33,1},{65,33},{97,65},{2,98}... | collective-permute-start | bytes 1572872 | tf_op jit(solution)/shard_map/ppermute | solution.py:38
  87.0 28.6 %collective-permute-start.22 = (bf16[2,8,128,128]{3,2,1,0:T(8,128)(2,1)S(1)}, bf16[2,8,128,128]{3,2,1,0:T(8,128)(2,1)S(1)}, u32[]{:S(2)}, u32[]{:S(2)}) collective-permute-start(bf16[2,8,128,128]{3,2,1,0:T(8,128)(2,1)S(1)} %get-tuple-element.18), channel_id=1, source_target_pairs={{0,32},{32,64},{64,96},{96,0},{1,33},{33,65},{65,97},{97,1},{2,34}... | collective-permute-start | bytes 1572872 | tf_op jit(solution)/shard_map/ppermute | solution.py:38
  108.2 12.4 %collective-permute-start.23 = (bf16[2,8,128,128]{3,2,1,0:T(8,128)(2,1)S(1)}, bf16[2,8,128,128]{3,2,1,0:T(8,128)(2,1)S(1)}, u32[]{:S(2)}, u32[]{:S(2)}) collective-permute-start(bf16[2,8,128,128]{3,2,1,0:T(8,128)(2,1)S(1)} %get-tuple-element.19), channel_id=1, source_target_pairs={{0,64},{32,96},{64,0},{96,32},{1,65},{33,97},{65,1},{97,33},{2,66}... | collective-permute-start | bytes 1572872 | tf_op jit(solution)/shard_map/ppermute | solution.py:38
  112.3 12.2 %collective-permute-start.17 = (bf16[2,128,512]{2,1,0:T(8,128)(2,1)S(1)}, bf16[2,128,512]{2,1,0:T(8,128)(2,1)S(1)}, u32[]{:S(2)}, u32[]{:S(2)}) collective-permute-start(bf16[2,128,512]{2,1,0:T(8,128)(2,1)S(1)} %get-tuple-element.20), channel_id=1, source_target_pairs={{0,24},{1,7},{2,26},{3,1},{4,28},{5,3},{6,30},{7,5},{8,0},{9,15},{... | collective-permute-start | bytes 786440 | tf_op jit(solution)/shard_map/ppermute | solution.py:34
  114.3 10.1 %collective-permute-start.19 = (bf16[2,128,512]{2,1,0:T(8,128)(2,1)S(1)}, bf16[2,128,512]{2,1,0:T(8,128)(2,1)S(1)}, u32[]{:S(2)}, u32[]{:S(2)}) collective-permute-start(bf16[2,128,512]{2,1,0:T(8,128)(2,1)S(1)} %get-tuple-element.21), channel_id=1, source_target_pairs={{0,16},{1,5},{2,18},{3,7},{4,20},{5,1},{6,22},{7,3},{8,24},{9,13},... | collective-permute-start | bytes 786440 | tf_op jit(solution)/shard_map/ppermute | solution.py:34
  115.6 8.9 %collective-permute-start.18 = (bf16[2,128,512]{2,1,0:T(8,128)(2,1)S(1)}, bf16[2,128,512]{2,1,0:T(8,128)(2,1)S(1)}, u32[]{:S(2)}, u32[]{:S(2)}) collective-permute-start(bf16[2,128,512]{2,1,0:T(8,128)(2,1)S(1)} %get-tuple-element.22), channel_id=1, source_target_pairs={{0,8},{1,3},{2,10},{3,5},{4,12},{5,7},{6,14},{7,1},{8,16},{9,11},{... | collective-permute-start | bytes 786440 | tf_op jit(solution)/shard_map/ppermute | solution.py:34
  120.9 8.2 %collective-permute-start.24 = (bf16[8,128,128]{2,1,0:T(8,128)(2,1)S(1)}, bf16[8,128,128]{2,1,0:T(8,128)(2,1)S(1)}, u32[]{:S(2)}, u32[]{:S(2)}) collective-permute-start(bf16[8,128,128]{2,1,0:T(8,128)(2,1)S(1)} %slice_bitcast_fusion), channel_id=1, source_target_pairs={{0,1},{1,0},{2,3},{3,2},{4,5},{5,4},{6,7},{7,6},{8,9},{9,8},{10,11... | collective-permute-start | bytes 786440 | tf_op jit(solution)/shard_map/ppermute | solution.py:42
  124.7 5.4 %collective-permute-start.20 = (bf16[128,512]{1,0:T(8,128)(2,1)S(1)}, bf16[128,512]{1,0:T(8,128)(2,1)S(1)}, u32[]{:S(2)}, u32[]{:S(2)}) collective-permute-start(bf16[128,512]{1,0:T(8,128)(2,1)S(1)} %slice_bitcast_fusion.7), channel_id=1, source_target_pairs={{0,1},{1,0},{2,3},{3,2},{4,5},{5,4},{6,7},{7,6},{8,9},{9,8},{10,11... | collective-permute-start | bytes 393224 | tf_op jit(solution)/shard_map/ppermute | solution.py:42

commit v3 on v2

--- a/solution.py
+++ b/solution.py
@@ -88,7 +88,8 @@
 
 
 def enter_kernel(
-    where_ref, codes_ref, a0, a1, a2, a3, w0, w1, w2, w3, out, acts, weights, picked, sems
+    where_ref, codes_ref, a0, a1, a2, a3, w0, w1, w2, w3,
+    acts, weights, sent, slope, picked, sems,
 ):
     core = where_ref[0]
     for copy in load((a0, a1, a2, a3), (w0, w1, w2, w3), acts, weights, sems):
@@ -101,40 +102,40 @@
 
         @pl.when(core == 0)
         def _():
-            out[step ^ core] = jnp.dot(
+            pre = jnp.dot(
                 picked[...],
                 weights[d, r].reshape(8 * BLK, BLK),
                 preferred_element_type=jnp.float32,
             )
+            t = jnp.tanh(GELU_SCALE * (pre + GELU_CUBIC * pre * pre * pre))
+            sent[step] = (0.5 * pre * (1.0 + t)).astype(jnp.bfloat16)
+            slope[step] = 0.5 * (1.0 + t) + 0.5 * pre * (1.0 - t * t) * GELU_SCALE * (
+                1.0 + 3.0 * GELU_CUBIC * pre * pre
+            )
 
         @pl.when(core == 1)
         def _():
             flat = jnp.concatenate([weights[d, r, s] for s in range(8)], axis=1)
-            out[step ^ core] = lax.dot_general(
+            sent[step ^ 1] = lax.dot_general(
                 picked[...], flat, (((1,), (1,)), ((), ())), preferred_element_type=jnp.float32
-            )
+            ).astype(jnp.bfloat16)
 
         return carry
 
     lax.fori_loop(0, 8, body, 0)
 
 
-def leave_kernel(
-    where_ref, codes_ref, left, a0, a1, a2, a3, w0, w1, w2, w3,
-    o0, o1, o2, o3, g0, g1, g2, g3,
-    acts, weights, picked, acc, out, grads, sems,
-):
+def pulled(came, slope, step):
+    return (came[step].astype(jnp.float32) * slope[step]).astype(jnp.bfloat16)
+
+
+def sums_kernel(where_ref, codes_ref, weights, came, slope, o0, o1, o2, o3, acc):
     core = where_ref[0]
-    copies = load((a0, a1, a2, a3), (w0, w1, w2, w3), acts, weights, sems)
     acc[...] = jnp.zeros_like(acc)
-    for copy in copies:
-        copy.wait()
 
     def body(step, carry):
         d, r = step >> 1, step & 1
         places, stride = spots(where_ref, codes_ref, d, r)
-        pick(acts, picked, places, stride)
-        mine = left[step ^ core]
 
         def scatter(s, product):
             for n in range(2):
@@ -147,6 +148,7 @@
 
         @pl.when(core == 0)
         def _():
+            mine = pulled(came, slope, step)
             for s in range(0, 8, 2):
                 pair = weights[d, r, s : s + 2].reshape(2 * BLK, BLK)
                 scatter(
@@ -155,35 +157,54 @@
                         mine, pair, (((1,), (1,)), ((), ())), preferred_element_type=jnp.float32
                     ),
                 )
-            grad = lax.dot_general(
-                picked[...], mine, (((0,), (0,)), ((), ())), preferred_element_type=jnp.float32
-            )
-            grads[d, r] = grad.astype(jnp.bfloat16).reshape(8, BLK, BLK)
 
         @pl.when(core == 1)
         def _():
+            mine = came[step ^ 1]
             for s in range(0, 8, 2):
                 pair = jnp.concatenate([weights[d, r, s], weights[d, r, s + 1]], axis=1)
                 scatter(s, jnp.dot(mine, pair, preferred_element_type=jnp.float32))
-            grad = lax.dot_general(
-                mine, picked[...], (((0,), (0,)), ((), ())), preferred_element_type=jnp.float32
-            ).astype(jnp.bfloat16)
-            for s in range(8):
-                grads[d, r, s] = grad[:, s * BLK : (s + 1) * BLK]
 
         return carry
 
     lax.fori_loop(0, 8, body, 0)
-    backs = []
-    for n, dst in enumerate((g0, g1, g2, g3)):
-        backs.append(pltpu.make_async_copy(grads.at[n], dst, sems.at[n]))
-        backs[-1].start()
-    for n, dst in enumerate((o0, o1, o2, o3)):
-        out[n] = acc[n].astype(jnp.bfloat16)
-        backs.append(pltpu.make_async_copy(out.at[n], dst, sems.at[4 + n]))
-        backs[-1].start()
-    for copy in backs:
-        copy.wait()
+    for n, out in enumerate((o0, o1, o2, o3)):
+        out[...] = acc[n].astype(jnp.bfloat16)
+
+
+def grads_kernel(where_ref, codes_ref, acts, came, slope, g0, g1, g2, g3, picked):
+    core = where_ref[0]
+    for d, grads in enumerate((g0, g1, g2, g3)):
+
+        def body(r, carry):
+            step = d * 2 + r
+            places, stride = spots(where_ref, codes_ref, d, r)
+            pick(acts, picked, places, stride)
+
+            @pl.when(core == 0)
+            def _():
+                grad = lax.dot_general(
+                    picked[...],
+                    pulled(came, slope, step),
+                    (((0,), (0,)), ((), ())),
+                    preferred_element_type=jnp.float32,
+                )
+                grads[r] = grad.astype(jnp.bfloat16).reshape(8, BLK, BLK)
+
+            @pl.when(core == 1)
+            def _():
+                grad = lax.dot_general(
+                    came[step ^ 1],
+                    picked[...],
+                    (((0,), (0,)), ((), ())),
+                    preferred_element_type=jnp.float32,
+                ).astype(jnp.bfloat16)
+                for s in range(8):
+                    grads[r, s] = grad[:, s * BLK : (s + 1) * BLK]
+
+            return carry
+
+        lax.fori_loop(0, 2, body, 0)
 
 
 SMEM = pl.BlockSpec(memory_space=pltpu.SMEM)
@@ -193,50 +214,60 @@
 WEIGHTS = (RING, 2, 8, BLK, BLK)
 
 
+CHUNK = jax.ShapeDtypeStruct(ACTS[1:], jnp.bfloat16)
+GRAD = jax.ShapeDtypeStruct(WEIGHTS[1:], jnp.bfloat16)
+HIDDEN = (8, 512, BLK)
+
+
+def cost(flops, moved):
+    return pl.CostEstimate(flops=flops, bytes_accessed=moved, transcendentals=0)
+
+
 def enter(where, codes, acts, weights):
     return pl.pallas_call(
         enter_kernel,
-        out_shape=jax.ShapeDtypeStruct((8, 512, BLK), jnp.float32),
+        out_shape=[
+            jax.ShapeDtypeStruct(ACTS, jnp.bfloat16),
+            jax.ShapeDtypeStruct(WEIGHTS, jnp.bfloat16),
+            jax.ShapeDtypeStruct(HIDDEN, jnp.bfloat16),
+            jax.ShapeDtypeStruct(HIDDEN, jnp.float32),
+        ],
         in_specs=[SMEM, SMEM] + [ANY] * 8,
-        out_specs=VMEM,
+        out_specs=[VMEM] * 4,
         scratch_shapes=[
-            pltpu.VMEM(ACTS, jnp.bfloat16),
-            pltpu.VMEM(WEIGHTS, jnp.bfloat16),
             pltpu.VMEM((512, 8 * BLK), jnp.bfloat16),
             pltpu.SemaphoreType.DMA((8,)),
         ],
-        compiler_params=pltpu.CompilerParams(vmem_limit_bytes=20 << 20),
-        cost_estimate=pl.CostEstimate(
-            flops=1 << 30, bytes_accessed=8 << 20, transcendentals=0
-        ),
+        compiler_params=pltpu.CompilerParams(vmem_limit_bytes=16 << 20),
+        cost_estimate=cost(1 << 30, 8 << 20),
         name="enter",
     )(where, codes, *acts, *weights)
 
 
-def leave(where, codes, left, acts, weights):
-    chunk = jax.ShapeDtypeStruct(ACTS[1:], jnp.bfloat16)
-    grad = jax.ShapeDtypeStruct(WEIGHTS[1:], jnp.bfloat16)
-    results = pl.pallas_call(
-        leave_kernel,
-        out_shape=[chunk] * 4 + [grad] * 4,
-        in_specs=[SMEM, SMEM, VMEM] + [ANY] * 8,
-        out_specs=[ANY] * 8,
-        scratch_shapes=[
-            pltpu.VMEM(ACTS, jnp.bfloat16),
-            pltpu.VMEM(WEIGHTS, jnp.bfloat16),
-            pltpu.VMEM((512, 8 * BLK), jnp.bfloat16),
-            pltpu.VMEM(ACTS, jnp.float32),
-            pltpu.VMEM(ACTS, jnp.bfloat16),
-            pltpu.VMEM(WEIGHTS, jnp.bfloat16),
-            pltpu.SemaphoreType.DMA((8,)),
-        ],
-        compiler_params=pltpu.CompilerParams(vmem_limit_bytes=32 << 20),
-        cost_estimate=pl.CostEstimate(
-            flops=2 << 30, bytes_accessed=12 << 20, transcendentals=0
-        ),
-        name="leave",
-    )(where, codes, left, *acts, *weights)
-    return results[:4], results[4:]
+def sums(where, codes, weights, came, slope):
+    return pl.pallas_call(
+        sums_kernel,
+        out_shape=[CHUNK] * 4,
+        in_specs=[SMEM, SMEM] + [VMEM] * 3,
+        out_specs=[VMEM] * 4,
+        scratch_shapes=[pltpu.VMEM(ACTS, jnp.float32)],
+        compiler_params=pltpu.CompilerParams(vmem_limit_bytes=24 << 20),
+        cost_estimate=cost(1 << 30, 8 << 20),
+        name="sums",
+    )(where, codes, weights, came, slope)
+
+
+def block_grads(where, codes, acts, came, slope):
+    return pl.pallas_call(
+        grads_kernel,
+        out_shape=[GRAD] * 4,
+        in_specs=[SMEM, SMEM] + [VMEM] * 3,
+        out_specs=[VMEM] * 4,
+        scratch_shapes=[pltpu.VMEM((512, 8 * BLK), jnp.bfloat16)],
+        compiler_params=pltpu.CompilerParams(vmem_limit_bytes=16 << 20),
+        cost_estimate=cost(1 << 30, 8 << 20),
+        name="grads",
+    )(where, codes, acts, came, slope)
 
 
 def per_device(tokens, up_weight, up_rows, down_weight, down_cols, grad_out):
@@ -261,24 +292,19 @@
     acts = gather(jnp.stack(gather(acts, first(True))), first(False))
     weights = gather(weights, z_shift)
 
-    entered = enter(where, codes, acts, weights)
-    pre = lax.ppermute(entered, "core", [(0, 1)])
-    t = jnp.tanh(GELU_SCALE * (pre + GELU_CUBIC * pre * pre * pre))
-    hidden = (0.5 * pre * (1.0 + t)).astype(jnp.bfloat16)
-    slope = 0.5 * (1.0 + t) + 0.5 * pre * (1.0 - t * t) * GELU_SCALE * (
-        1.0 + 3.0 * GELU_CUBIC * pre * pre
-    )
-    grad_pre = lax.ppermute((entered * slope).astype(jnp.bfloat16), "core", [(1, 0)])
-    chunks, grads = leave(where, codes, jnp.where(up, grad_pre, hidden), acts, weights)
+    acts, weights, sent, slope = enter(where, codes, acts, weights)
+    came = swap(sent)
+    chunks = sums(where, codes, weights, came, slope)
+    grads = block_grads(where, codes, acts, came, slope)
 
     summed = reduce(chunks, first(False)).astype(jnp.bfloat16)
     final = reduce([summed[n] for n in range(RING)], first(True)).astype(jnp.bfloat16)
     grad_scale = 1.0 / math.sqrt(tokens.shape[0] * lax.axis_size("z") * lax.axis_size("x"))
     scaled = (reduce(grads, z_shift) * grad_scale).astype(jnp.bfloat16)
-    came = swap(final[1])
+    came_act = swap(final[1])
     came_grad = swap(scaled[1])
-    layer_out = jnp.where(up, came, final[0])
-    grad_tokens = jnp.where(up, final[0], came)
+    layer_out = jnp.where(up, came_act, final[0])
+    grad_tokens = jnp.where(up, final[0], came_act)
     grad_up = jnp.where(up, scaled[0], came_grad)
     grad_down = jnp.where(up, came_grad, scaled[0])
     return (layer_out, grad_tokens, grad_up[None], grad_down[None])

time: 131 us -> 115 us (0.88)
  waiting for transfers between devices: 57.9 us -> 48.8 us
  starting transfers between devices: 43.9 us -> 38.2 us
  other arithmetic: 7.17 us -> 5.01 us
    ppermute x2 -> x0, waiting for transfers between devices: 6.96 us -> none  [the longest x1 4.75 us: per_device(): pre = lax.ppermute(entered, 'core', [(0, 1)])]
    ppermute x12, waiting for transfers between devices: 22.1 us -> 15.7 us  [mixed_shift(): return lax.ppermute(values, MIXED, mixed_pairs(step, first))]
    ppermute x2 -> x0, starting transfers between devices: 3.4 us -> none  [the longest x1 2.11 us: per_device(): lax.ppermute((entered * slope).astype(jnp.bfloat16), 'core', [(1, 0)])]
    ppermute x5 -> x6, starting transfers between devices: 11.8 us -> 9.05 us  [swap(): return lax.ppermute(values, 'core', [(0, 1), (1, 0)])]
    ppermute x5 -> x6, waiting for transfers between devices: 0.98 us -> 3.27 us  [swap(): return lax.ppermute(values, 'core', [(0, 1), (1, 0)])]
    ppermute x6, waiting for transfers between devices: 27.9 us -> 29.9 us  [z_shift(): lax.ppermute(values, 'z', [(i, (i + step) % RING) for i in range(RING)])]
    convert_element_type x1 -> x0, other arithmetic: 1.36 us -> none  [per_device(): (entered * slope).astype(jnp.bfloat16)]
    pallas_call x2 -> x3, Pallas kernels: 20.8 us -> 21.7 us  [the longest x1 8.72 us: enter(): pl.pallas_call(enter_kernel, out_shape=[jax.ShapeDtypeStruct(ACTS, jnp.bf...]
  transfers between devices with their start and end apart: 25 -> 24, of which waited for: 11 -> 10; matrix products, arithmetic and copies ran while one was open for 3% -> 3% of each run, Pallas kernels for 0% -> 5%
where the time goes in v3:
time: 115 us
  waiting for transfers between devices  48.8 us (42%)
  starting transfers between devices  38.2 us (33%)
  Pallas kernels  21.7 us (19%)
  other arithmetic  5.01 us (4%)
    ppermute x6, waiting for transfers between devices, z_shift(): lax.ppermute(values, 'z', [(i, (i + step) % RING) for i in range(RING)])  29.9 us
    ppermute x12, starting transfers between devices, mixed_shift(): return lax.ppermute(values, MIXED, mixed_pairs(step, first))  16.8 us
    ppermute x12, waiting for transfers between devices, mixed_shift(): return lax.ppermute(values, MIXED, mixed_pairs(step, first))  15.7 us
    ppermute x6, starting transfers between devices, z_shift(): lax.ppermute(values, 'z', [(i, (i + step) % RING) for i in range(RING)])  12.4 us
    ppermute x6, starting transfers between devices, swap(): return lax.ppermute(values, 'core', [(0, 1), (1, 0)])  9.05 us
    pallas_call x1, Pallas kernels, enter(): pl.pallas_call(enter_kernel, out_shape=[jax.ShapeDtypeStruct(ACTS, jnp.bf...  8.72 us
    pallas_call x1, Pallas kernels, sums(): pl.pallas_call(sums_kernel, out_shape=[CHUNK] * 4, in_specs=[SMEM, SMEM]...  7.09 us
    pallas_call x1, Pallas kernels, block_grads(): pl.pallas_call(grads_kernel, out_shape=[GRAD] * 4, in_specs=[SMEM, SMEM]...  5.93 us
  transfers between devices with their start and end apart: 24, of which 10 were waited for; matrix products, arithmetic and copies ran while one was open for 3% of the time, Pallas kernels for 5%

profile of v3, /device:TPU:1, one launch (start us, length us, event | category | flops | bytes accessed | tf_op | source)
XLA Modules:
  0.0 114.8 jit_solution(10855429095847334174)
XLA Ops:
  0.6 1.0 select_bitcast_fusion.3
  1.6 1.5 %collective-permute-start.1 = (bf16[128,512]{1,0:T(8,128)(2,1)S(1)}, bf16[128,512]{1,0:T(8,128)(2,1)S(1)}, u32[]{:S(2)}, u32[]{:S(2)}) collective-permute-start(bf16[128,512]{1,0:T(8,128)(2,1)S(1)} %get-tuple-element.40), channel_id=1, source_target_pairs={{0,1},{1,0},{2,3},{3,2},{4,5},{5,4},{6,7},{7,6},{8,9},{9,8},{10,11... | collective-permute-start | bytes 393224 | tf_op jit(solution)/shard_map/ppermute | solution.py:42
  3.1 1.1 broadcast_select_fusion
  4.2 0.0 copy-start
  4.2 0.0 copy-start.1
  4.2 0.1 collective-permute-start.8
  4.3 0.0 collective-permute-done.1
  4.4 3.1 %collective-permute-start.3 = (bf16[2,128,512]{2,1,0:T(8,128)(2,1)S(1)}, bf16[2,128,512]{2,1,0:T(8,128)(2,1)S(1)}, u32[]{:S(2)}, u32[]{:S(2)}) collective-permute-start(bf16[2,128,512]{2,1,0:T(8,128)(2,1)S(1)} %get-tuple-element.38), channel_id=1, source_target_pairs={{0,16},{1,5},{2,18},{3,7},{4,20},{5,1},{6,22},{7,3},{8,24},{9,13},... | collective-permute-start | bytes 786440 | tf_op jit(solution)/shard_map/ppermute | solution.py:34
  7.5 0.4 collective-permute-start.2
  7.9 2.3 %collective-permute-start.4 = (bf16[2,128,512]{2,1,0:T(8,128)(2,1)S(1)}, bf16[2,128,512]{2,1,0:T(8,128)(2,1)S(1)}, u32[]{:S(2)}, u32[]{:S(2)}) collective-permute-start(bf16[2,128,512]{2,1,0:T(8,128)(2,1)S(1)} %get-tuple-element.38), channel_id=1, source_target_pairs={{0,24},{1,7},{2,26},{3,1},{4,28},{5,3},{6,30},{7,5},{8,0},{9,15},{... | collective-permute-start | bytes 786440 | tf_op jit(solution)/shard_map/ppermute | solution.py:34
  10.1 0.0 collective-permute-done.8
  10.1 0.1 pad_maximum_fusion.1.w0
  10.2 3.8 %collective-permute-start.11 = (bf16[2,8,128,128]{3,2,1,0:T(8,128)(2,1)S(1)}, bf16[2,8,128,128]{3,2,1,0:T(8,128)(2,1)S(1)}, u32[]{:S(2)}, u32[]{:S(2)}) collective-permute-start(bf16[2,8,128,128]{3,2,1,0:T(8,128)(2,1)S(1)} %pad_maximum_fusion.1.w0), channel_id=1, source_target_pairs={{0,96},{32,0},{64,32},{96,64},{1,97},{33,1},{65,33},{97,65},{2,98}... | collective-permute-start | bytes 1572872 | tf_op jit(solution)/shard_map/ppermute | solution.py:38
  14.0 0.0 collective-permute-done.3
  14.0 0.3 collective-permute-done.2
  14.3 0.4 collective-permute-done.4
  14.7 0.1 pad_maximum_fusion.a0
  14.8 2.5 %collective-permute-start.7 = (bf16[4,2,128,512]{3,2,1,0:T(8,128)(2,1)S(1)}, bf16[4,2,128,512]{3,2,1,0:T(8,128)(2,1)S(1)}, u32[]{:S(2)}, u32[]{:S(2)}) collective-permute-start(bf16[4,2,128,512]{3,2,1,0:T(8,128)(2,1)S(1)} %pad_maximum_fusion.a0), channel_id=1, source_target_pairs={{0,6},{1,25},{2,0},{3,27},{4,2},{5,29},{6,4},{7,31},{8,14},{9,1},{... | collective-permute-start | bytes 3145736 | tf_op jit(solution)/shard_map/ppermute | solution.py:34
  17.4 0.5 collective-permute-start.6
  17.9 0.6 collective-permute-start.5
  18.5 0.1 copy.10
  18.6 0.1 copy.11
  18.7 2.2 %collective-permute-start = (s32[4,8]{1,0:T(4,128)S(1)}, s32[4,8]{1,0:T(4,128)S(1)}, u32[]{:S(2)}, u32[]{:S(2)}) collective-permute-start(s32[4,8]{1,0:T(4,128)S(1)} %bitcast.58), channel_id=1, source_target_pairs={{0,1},{1,0},{2,3},{3,2},{4,5},{5,4},{6,7},{7,6},{8,9},{9,8},{10,11... | collective-permute-start | bytes 392 | tf_op jit(solution)/shard_map/ppermute | solution.py:42
  20.9 0.8 collective-permute-done
  21.7 3.6 %collective-permute-start.10 = (bf16[2,8,128,128]{3,2,1,0:T(8,128)(2,1)S(1)}, bf16[2,8,128,128]{3,2,1,0:T(8,128)(2,1)}, u32[]{:S(2)}, u32[]{:S(2)}) collective-permute-start(bf16[2,8,128,128]{3,2,1,0:T(8,128)(2,1)S(1)} %pad_maximum_fusion.1.w0), channel_id=1, source_target_pairs={{0,64},{32,96},{64,0},{96,32},{1,65},{33,97},{65,1},{97,33},{2,66}... | collective-permute-start | bytes 1572872 | tf_op jit(solution)/shard_map/ppermute | solution.py:38
  25.3 0.0 collective-permute-done.11.w3
  25.3 0.7 collective-permute-start.9
  26.0 0.1 pad_add_fusion.1.where_ref
  26.1 11.4 %collective-permute-done.10.w2 = bf16[2,8,128,128]{3,2,1,0:T(8,128)(2,1)} collective-permute-done((bf16[2,8,128,128]{3,2,1,0:T(8,128)(2,1)S(1)}, bf16[2,8,128,128]{3,2,1,0:T(8,128)(2,1)}, u32[]{:S(2)}, u32[]{:S(2)}) %collective-permute-start.10) | collective-permute-done | bytes 524320 | tf_op jit(solution)/shard_map/ppermute | solution.py:38
  37.5 11.5 %collective-permute-done.9.w1 = bf16[2,8,128,128]{3,2,1,0:T(8,128)(2,1)} collective-permute-done((bf16[2,8,128,128]{3,2,1,0:T(8,128)(2,1)S(1)}, bf16[2,8,128,128]{3,2,1,0:T(8,128)(2,1)}, u32[]{:S(2)}, u32[]{:S(2)}) %collective-permute-start.9) | collective-permute-done | bytes 524320 | tf_op jit(solution)/shard_map/ppermute | solution.py:38
  49.0 0.0 collective-permute-done.7.a3
  49.0 0.0 collective-permute-done.6.a2
  49.0 0.0 collective-permute-done.5.a1
  49.0 8.7 %enter.1 = (bf16[4,4,2,128,512]{4,3,2,1,0:T(8,128)(2,1)S(1)}, bf16[4,2,8,128,128]{4,3,2,1,0:T(8,128)(2,1)S(1)}, bf16[8,512,128]{2,1,0:T(8,128)(2,1)S(1)}, f32[8,512,128]{2,1,0:T(8,128)S(1)}) custom-call(s32[2]{0:T(128)S(1)} %pad_add_fusion.1.where_ref, s32[2,4,8]{2,1,0:T(4,128)S(1)} %and_add_fusion.codes_ref, ...), custom_call_target="tpu_custom_call" | custom-call | flops 1073741824 | bytes 8388608 | tf_op jit(solution)/shard_map/enter/pallas_call | solution.py:227
  57.7 1.0 collective-permute-start.12
  58.8 2.3 %collective-permute-done.12.came = bf16[8,512,128]{2,1,0:T(8,128)(2,1)S(1)} collective-permute-done((bf16[8,512,128]{2,1,0:T(8,128)(2,1)S(1)}, bf16[8,512,128]{2,1,0:T(8,128)(2,1)S(1)}, u32[]{:S(2)}, u32[]{:S(2)}) %collective-permute-start.12) | collective-permute-done | bytes 1048608 | tf_op jit(solution)/shard_map/ppermute | solution.py:42
  61.1 7.1 %sums.1 = (bf16[4,2,128,512]{3,2,1,0:T(8,128)(2,1)S(1)}, bf16[4,2,128,512]{3,2,1,0:T(8,128)(2,1)S(1)}, bf16[4,2,128,512]{3,2,1,0:T(8,128)(2,1)S(1)}, bf16[4,2,128,512]{3,2,1,0:T(8,128)(2,1)S(1)}) custom-call(s32[2]{0:T(128)S(1)} %pad_add_fusion.1.where_ref, s32[2,4,8]{2,1,0:T(4,128)S(1)} %and_add_fusion.codes_ref, ...), custom_call_target="tpu_custom_call" | custom-call | flops 1073741824 | bytes 8388608 | tf_op jit(solution)/shard_map/sums/pallas_call | solution.py:248
  68.2 2.9 %collective-permute-start.13 = (bf16[4,2,128,512]{3,2,1,0:T(8,128)(2,1)S(1)}, bf16[4,2,128,512]{3,2,1,0:T(8,128)(2,1)S(1)}, u32[]{:S(2)}, u32[]{:S(2)}) collective-permute-start(bf16[4,2,128,512]{3,2,1,0:T(8,128)(2,1)S(1)} %get-tuple-element.20), channel_id=1, source_target_pairs={{0,6},{1,25},{2,0},{3,27},{4,2},{5,29},{6,4},{7,31},{8,14},{9,1},{... | collective-permute-start | bytes 3145736 | tf_op jit(solution)/shard_map/ppermute | solution.py:34
  71.0 0.0 collective-permute-start.14
  71.0 1.3 %collective-permute-start.15 = (bf16[4,2,128,512]{3,2,1,0:T(8,128)(2,1)S(1)}, bf16[4,2,128,512]{3,2,1,0:T(8,128)(2,1)S(1)}, u32[]{:S(2)}, u32[]{:S(2)}) collective-permute-start(bf16[4,2,128,512]{3,2,1,0:T(8,128)(2,1)S(1)} %get-tuple-element.22), channel_id=1, source_target_pairs={{0,4},{1,17},{2,6},{3,19},{4,0},{5,21},{6,2},{7,23},{8,12},{9,25},... | collective-permute-start | bytes 3145736 | tf_op jit(solution)/shard_map/ppermute | solution.py:34
  72.3 5.9 %grads.1 = (bf16[2,8,128,128]{3,2,1,0:T(8,128)(2,1)S(1)}, bf16[2,8,128,128]{3,2,1,0:T(8,128)(2,1)S(1)}, bf16[2,8,128,128]{3,2,1,0:T(8,128)(2,1)S(1)}, bf16[2,8,128,128]{3,2,1,0:T(8,128)(2,1)S(1)}) custom-call(s32[2]{0:T(128)S(1)} %pad_add_fusion.1.where_ref, s32[2,4,8]{2,1,0:T(4,128)S(1)} %and_add_fusion.codes_ref, ...), custom_call_target="tpu_custom_call" | custom-call | flops 1073741824 | bytes 8388608 | tf_op jit(solution)/shard_map/grads/pallas_call | solution.py:261
  78.2 1.0 collective-permute-start.20
  79.2 0.7 collective-permute-start.21
  79.9 14.1 %collective-permute-done.13 = bf16[4,2,128,512]{3,2,1,0:T(8,128)(2,1)S(1)} collective-permute-done((bf16[4,2,128,512]{3,2,1,0:T(8,128)(2,1)S(1)}, bf16[4,2,128,512]{3,2,1,0:T(8,128)(2,1)S(1)}, u32[]{:S(2)}, u32[]{:S(2)}) %collective-permute-start.13) | collective-permute-done | bytes 1048608 | tf_op jit(solution)/shard_map/ppermute | solution.py:34
  94.0 2.5 %collective-permute-start.22 = (bf16[2,8,128,128]{3,2,1,0:T(8,128)(2,1)S(1)}, bf16[2,8,128,128]{3,2,1,0:T(8,128)(2,1)S(1)}, u32[]{:S(2)}, u32[]{:S(2)}) collective-permute-start(bf16[2,8,128,128]{3,2,1,0:T(8,128)(2,1)S(1)} %get-tuple-element.27), channel_id=1, source_target_pairs={{0,64},{32,96},{64,0},{96,32},{1,65},{33,97},{65,1},{97,33},{2,66}... | collective-permute-start | bytes 1572872 | tf_op jit(solution)/shard_map/ppermute | solution.py:38
  96.5 0.9 collective-permute-done.14
  97.4 0.0 collective-permute-done.15
  97.4 0.6 add_convert_fusion
  98.0 0.1 slice_bitcast_fusion.4
  98.1 1.8 %collective-permute-start.16 = (bf16[2,128,512]{2,1,0:T(8,128)(2,1)S(1)}, bf16[2,128,512]{2,1,0:T(8,128)(2,1)S(1)}, u32[]{:S(2)}, u32[]{:S(2)}) collective-permute-start(bf16[2,128,512]{2,1,0:T(8,128)(2,1)S(1)} %get-tuple-element.28), channel_id=1, source_target_pairs={{0,24},{1,7},{2,26},{3,1},{4,28},{5,3},{6,30},{7,5},{8,0},{9,15},{... | collective-permute-start | bytes 786440 | tf_op jit(solution)/shard_map/ppermute | solution.py:34
  99.9 1.4 %collective-permute-start.18 = (bf16[2,128,512]{2,1,0:T(8,128)(2,1)S(1)}, bf16[2,128,512]{2,1,0:T(8,128)(2,1)S(1)}, u32[]{:S(2)}, u32[]{:S(2)}) collective-permute-start(bf16[2,128,512]{2,1,0:T(8,128)(2,1)S(1)} %get-tuple-element.29), channel_id=1, source_target_pairs={{0,16},{1,5},{2,18},{3,7},{4,20},{5,1},{6,22},{7,3},{8,24},{9,13},... | collective-permute-start | bytes 786440 | tf_op jit(solution)/shard_map/ppermute | solution.py:34
  101.3 0.0 collective-permute-done.20
  101.3 0.0 collective-permute-start.17
  101.3 0.0 collective-permute-done.21
  101.3 7.0 %collective-permute-done.22 = bf16[2,8,128,128]{3,2,1,0:T(8,128)(2,1)S(1)} collective-permute-done((bf16[2,8,128,128]{3,2,1,0:T(8,128)(2,1)S(1)}, bf16[2,8,128,128]{3,2,1,0:T(8,128)(2,1)S(1)}, u32[]{:S(2)}, u32[]{:S(2)}) %collective-permute-start.22) | collective-permute-done | bytes 524320 | tf_op jit(solution)/shard_map/ppermute | solution.py:38
  108.3 0.3 multiply_convert_fusion
  108.6 1.6 %collective-permute-start.23 = (bf16[8,128,128]{2,1,0:T(8,128)(2,1)S(1)}, bf16[8,128,128]{2,1,0:T(8,128)(2,1)S(1)}, u32[]{:S(2)}, u32[]{:S(2)}) collective-permute-start(bf16[8,128,128]{2,1,0:T(8,128)(2,1)S(1)} %slice_bitcast_fusion), channel_id=1, source_target_pairs={{0,1},{1,0},{2,3},{3,2},{4,5},{5,4},{6,7},{7,6},{8,9},{9,8},{10,11... | collective-permute-start | bytes 786440 | tf_op jit(solution)/shard_map/ppermute | solution.py:42
  110.3 0.0 collective-permute-done.18
  110.3 0.0 collective-permute-done.17
  110.3 0.1 fusion.2
  110.5 2.6 %collective-permute-start.19 = (bf16[128,512]{1,0:T(8,128)(2,1)S(1)}, bf16[128,512]{1,0:T(8,128)(2,1)S(1)}, u32[]{:S(2)}, u32[]{:S(2)}) collective-permute-start(bf16[128,512]{1,0:T(8,128)(2,1)S(1)} %slice_bitcast_fusion.7), channel_id=1, source_target_pairs={{0,1},{1,0},{2,3},{3,2},{4,5},{5,4},{6,7},{7,6},{8,9},{9,8},{10,11... | collective-permute-start | bytes 393224 | tf_op jit(solution)/shard_map/ppermute | solution.py:42
  113.1 0.8 select_bitcast_fusion
  113.9 0.2 collective-permute-done.19
  114.1 0.7 broadcast_select_fusion.1
  (9 shorter events, 0.1 us)
Async XLA Ops:
  1.6 2.7 %collective-permute-start.1 = (bf16[128,512]{1,0:T(8,128)(2,1)S(1)}, bf16[128,512]{1,0:T(8,128)(2,1)S(1)}, u32[]{:S(2)}, u32[]{:S(2)}) collective-permute-start(bf16[128,512]{1,0:T(8,128)(2,1)S(1)} %get-tuple-element.40), channel_id=1, source_target_pairs={{0,1},{1,0},{2,3},{3,2},{4,5},{5,4},{6,7},{7,6},{8,9},{9,8},{10,11... | collective-permute-start | bytes 393224 | tf_op jit(solution)/shard_map/ppermute | solution.py:42
  4.2 14.3 %copy-start = (s32[16,8]{0,1:T(8,128)S(1)}, s32[16,8]{0,1:T(8,128)}, u32[]{:S(2)}) copy-start(s32[16,8]{0,1:T(8,128)} %param.8) | copy-start | bytes 1540
  4.2 14.4 %copy-start.1 = (s32[16,8]{0,1:T(8,128)S(1)}, s32[16,8]{0,1:T(8,128)}, u32[]{:S(2)}) copy-start(s32[16,8]{0,1:T(8,128)} %param.10) | copy-start | bytes 1540
  4.2 5.9 %collective-permute-start.8 = (bf16[8,128,128]{2,1,0:T(8,128)(2,1)S(1)}, bf16[8,128,128]{2,1,0:T(8,128)(2,1)S(1)}, u32[]{:S(2)}, u32[]{:S(2)}) collective-permute-start(bf16[8,128,128]{2,1,0:T(8,128)(2,1)S(1)} %get-tuple-element.34), channel_id=1, source_target_pairs={{0,1},{1,0},{2,3},{3,2},{4,5},{5,4},{6,7},{7,6},{8,9},{9,8},{10,11... | collective-permute-start | bytes 786440 | tf_op jit(solution)/shard_map/ppermute | solution.py:42
  4.4 9.6 %collective-permute-start.3 = (bf16[2,128,512]{2,1,0:T(8,128)(2,1)S(1)}, bf16[2,128,512]{2,1,0:T(8,128)(2,1)S(1)}, u32[]{:S(2)}, u32[]{:S(2)}) collective-permute-start(bf16[2,128,512]{2,1,0:T(8,128)(2,1)S(1)} %get-tuple-element.38), channel_id=1, source_target_pairs={{0,16},{1,5},{2,18},{3,7},{4,20},{5,1},{6,22},{7,3},{8,24},{9,13},... | collective-permute-start | bytes 786440 | tf_op jit(solution)/shard_map/ppermute | solution.py:34
  7.5 6.9 %collective-permute-start.2 = (bf16[2,128,512]{2,1,0:T(8,128)(2,1)S(1)}, bf16[2,128,512]{2,1,0:T(8,128)(2,1)S(1)}, u32[]{:S(2)}, u32[]{:S(2)}) collective-permute-start(bf16[2,128,512]{2,1,0:T(8,128)(2,1)S(1)} %get-tuple-element.38), channel_id=1, source_target_pairs={{0,8},{1,3},{2,10},{3,5},{4,12},{5,7},{6,14},{7,1},{8,16},{9,11},{... | collective-permute-start | bytes 786440 | tf_op jit(solution)/shard_map/ppermute | solution.py:34
  7.9 6.9 %collective-permute-start.4 = (bf16[2,128,512]{2,1,0:T(8,128)(2,1)S(1)}, bf16[2,128,512]{2,1,0:T(8,128)(2,1)S(1)}, u32[]{:S(2)}, u32[]{:S(2)}) collective-permute-start(bf16[2,128,512]{2,1,0:T(8,128)(2,1)S(1)} %get-tuple-element.38), channel_id=1, source_target_pairs={{0,24},{1,7},{2,26},{3,1},{4,28},{5,3},{6,30},{7,5},{8,0},{9,15},{... | collective-permute-start | bytes 786440 | tf_op jit(solution)/shard_map/ppermute | solution.py:34
  10.2 15.1 %collective-permute-start.11 = (bf16[2,8,128,128]{3,2,1,0:T(8,128)(2,1)S(1)}, bf16[2,8,128,128]{3,2,1,0:T(8,128)(2,1)S(1)}, u32[]{:S(2)}, u32[]{:S(2)}) collective-permute-start(bf16[2,8,128,128]{3,2,1,0:T(8,128)(2,1)S(1)} %pad_maximum_fusion.1.w0), channel_id=1, source_target_pairs={{0,96},{32,0},{64,32},{96,64},{1,97},{33,1},{65,33},{97,65},{2,98}... | collective-permute-start | bytes 1572872 | tf_op jit(solution)/shard_map/ppermute | solution.py:38
  14.8 34.2 %collective-permute-start.7 = (bf16[4,2,128,512]{3,2,1,0:T(8,128)(2,1)S(1)}, bf16[4,2,128,512]{3,2,1,0:T(8,128)(2,1)S(1)}, u32[]{:S(2)}, u32[]{:S(2)}) collective-permute-start(bf16[4,2,128,512]{3,2,1,0:T(8,128)(2,1)S(1)} %pad_maximum_fusion.a0), channel_id=1, source_target_pairs={{0,6},{1,25},{2,0},{3,27},{4,2},{5,29},{6,4},{7,31},{8,14},{9,1},{... | collective-permute-start | bytes 3145736 | tf_op jit(solution)/shard_map/ppermute | solution.py:34
  17.4 31.6 %collective-permute-start.6 = (bf16[4,2,128,512]{3,2,1,0:T(8,128)(2,1)S(1)}, bf16[4,2,128,512]{3,2,1,0:T(8,128)(2,1)}, u32[]{:S(2)}, u32[]{:S(2)}) collective-permute-start(bf16[4,2,128,512]{3,2,1,0:T(8,128)(2,1)S(1)} %pad_maximum_fusion.a0), channel_id=1, source_target_pairs={{0,4},{1,17},{2,6},{3,19},{4,0},{5,21},{6,2},{7,23},{8,12},{9,25},... | collective-permute-start | bytes 3145736 | tf_op jit(solution)/shard_map/ppermute | solution.py:34
  17.9 31.1 %collective-permute-start.5 = (bf16[4,2,128,512]{3,2,1,0:T(8,128)(2,1)S(1)}, bf16[4,2,128,512]{3,2,1,0:T(8,128)(2,1)}, u32[]{:S(2)}, u32[]{:S(2)}) collective-permute-start(bf16[4,2,128,512]{3,2,1,0:T(8,128)(2,1)S(1)} %pad_maximum_fusion.a0), channel_id=1, source_target_pairs={{0,2},{1,9},{2,4},{3,11},{4,6},{5,13},{6,0},{7,15},{8,10},{9,17},{... | collective-permute-start | bytes 3145736 | tf_op jit(solution)/shard_map/ppermute | solution.py:34
  18.7 3.0 %collective-permute-start = (s32[4,8]{1,0:T(4,128)S(1)}, s32[4,8]{1,0:T(4,128)S(1)}, u32[]{:S(2)}, u32[]{:S(2)}) collective-permute-start(s32[4,8]{1,0:T(4,128)S(1)} %bitcast.58), channel_id=1, source_target_pairs={{0,1},{1,0},{2,3},{3,2},{4,5},{5,4},{6,7},{7,6},{8,9},{9,8},{10,11... | collective-permute-start | bytes 392 | tf_op jit(solution)/shard_map/ppermute | solution.py:42
  21.7 15.8 %collective-permute-start.10 = (bf16[2,8,128,128]{3,2,1,0:T(8,128)(2,1)S(1)}, bf16[2,8,128,128]{3,2,1,0:T(8,128)(2,1)}, u32[]{:S(2)}, u32[]{:S(2)}) collective-permute-start(bf16[2,8,128,128]{3,2,1,0:T(8,128)(2,1)S(1)} %pad_maximum_fusion.1.w0), channel_id=1, source_target_pairs={{0,64},{32,96},{64,0},{96,32},{1,65},{33,97},{65,1},{97,33},{2,66}... | collective-permute-start | bytes 1572872 | tf_op jit(solution)/shard_map/ppermute | solution.py:38
  25.3 23.7 %collective-permute-start.9 = (bf16[2,8,128,128]{3,2,1,0:T(8,128)(2,1)S(1)}, bf16[2,8,128,128]{3,2,1,0:T(8,128)(2,1)}, u32[]{:S(2)}, u32[]{:S(2)}) collective-permute-start(bf16[2,8,128,128]{3,2,1,0:T(8,128)(2,1)S(1)} %pad_maximum_fusion.1.w0), channel_id=1, source_target_pairs={{0,32},{32,64},{64,96},{96,0},{1,33},{33,65},{65,97},{97,1},{2,34}... | collective-permute-start | bytes 1572872 | tf_op jit(solution)/shard_map/ppermute | solution.py:38
  57.7 3.3 %collective-permute-start.12 = (bf16[8,512,128]{2,1,0:T(8,128)(2,1)S(1)}, bf16[8,512,128]{2,1,0:T(8,128)(2,1)S(1)}, u32[]{:S(2)}, u32[]{:S(2)}) collective-permute-start(bf16[8,512,128]{2,1,0:T(8,128)(2,1)S(1)} %get-tuple-element.17), channel_id=1, source_target_pairs={{0,1},{1,0},{2,3},{3,2},{4,5},{5,4},{6,7},{7,6},{8,9},{9,8},{10,11... | collective-permute-start | bytes 3145736 | tf_op jit(solution)/shard_map/ppermute | solution.py:42
  68.2 25.8 %collective-permute-start.13 = (bf16[4,2,128,512]{3,2,1,0:T(8,128)(2,1)S(1)}, bf16[4,2,128,512]{3,2,1,0:T(8,128)(2,1)S(1)}, u32[]{:S(2)}, u32[]{:S(2)}) collective-permute-start(bf16[4,2,128,512]{3,2,1,0:T(8,128)(2,1)S(1)} %get-tuple-element.20), channel_id=1, source_target_pairs={{0,6},{1,25},{2,0},{3,27},{4,2},{5,29},{6,4},{7,31},{8,14},{9,1},{... | collective-permute-start | bytes 3145736 | tf_op jit(solution)/shard_map/ppermute | solution.py:34
  71.0 26.4 %collective-permute-start.14 = (bf16[4,2,128,512]{3,2,1,0:T(8,128)(2,1)S(1)}, bf16[4,2,128,512]{3,2,1,0:T(8,128)(2,1)S(1)}, u32[]{:S(2)}, u32[]{:S(2)}) collective-permute-start(bf16[4,2,128,512]{3,2,1,0:T(8,128)(2,1)S(1)} %get-tuple-element.21), channel_id=1, source_target_pairs={{0,2},{1,9},{2,4},{3,11},{4,6},{5,13},{6,0},{7,15},{8,10},{9,17},{... | collective-permute-start | bytes 3145736 | tf_op jit(solution)/shard_map/ppermute | solution.py:34
  71.0 26.4 %collective-permute-start.15 = (bf16[4,2,128,512]{3,2,1,0:T(8,128)(2,1)S(1)}, bf16[4,2,128,512]{3,2,1,0:T(8,128)(2,1)S(1)}, u32[]{:S(2)}, u32[]{:S(2)}) collective-permute-start(bf16[4,2,128,512]{3,2,1,0:T(8,128)(2,1)S(1)} %get-tuple-element.22), channel_id=1, source_target_pairs={{0,4},{1,17},{2,6},{3,19},{4,0},{5,21},{6,2},{7,23},{8,12},{9,25},... | collective-permute-start | bytes 3145736 | tf_op jit(solution)/shard_map/ppermute | solution.py:34
  78.2 23.1 %collective-permute-start.20 = (bf16[2,8,128,128]{3,2,1,0:T(8,128)(2,1)S(1)}, bf16[2,8,128,128]{3,2,1,0:T(8,128)(2,1)S(1)}, u32[]{:S(2)}, u32[]{:S(2)}) collective-permute-start(bf16[2,8,128,128]{3,2,1,0:T(8,128)(2,1)S(1)} %get-tuple-element.25), channel_id=1, source_target_pairs={{0,96},{32,0},{64,32},{96,64},{1,97},{33,1},{65,33},{97,65},{2,98}... | collective-permute-start | bytes 1572872 | tf_op jit(solution)/shard_map/ppermute | solution.py:38
  79.2 22.1 %collective-permute-start.21 = (bf16[2,8,128,128]{3,2,1,0:T(8,128)(2,1)S(1)}, bf16[2,8,128,128]{3,2,1,0:T(8,128)(2,1)S(1)}, u32[]{:S(2)}, u32[]{:S(2)}) collective-permute-start(bf16[2,8,128,128]{3,2,1,0:T(8,128)(2,1)S(1)} %get-tuple-element.26), channel_id=1, source_target_pairs={{0,32},{32,64},{64,96},{96,0},{1,33},{33,65},{65,97},{97,1},{2,34}... | collective-permute-start | bytes 1572872 | tf_op jit(solution)/shard_map/ppermute | solution.py:38
  94.0 14.3 %collective-permute-start.22 = (bf16[2,8,128,128]{3,2,1,0:T(8,128)(2,1)S(1)}, bf16[2,8,128,128]{3,2,1,0:T(8,128)(2,1)S(1)}, u32[]{:S(2)}, u32[]{:S(2)}) collective-permute-start(bf16[2,8,128,128]{3,2,1,0:T(8,128)(2,1)S(1)} %get-tuple-element.27), channel_id=1, source_target_pairs={{0,64},{32,96},{64,0},{96,32},{1,65},{33,97},{65,1},{97,33},{2,66}... | collective-permute-start | bytes 1572872 | tf_op jit(solution)/shard_map/ppermute | solution.py:38
  98.1 12.2 %collective-permute-start.16 = (bf16[2,128,512]{2,1,0:T(8,128)(2,1)S(1)}, bf16[2,128,512]{2,1,0:T(8,128)(2,1)S(1)}, u32[]{:S(2)}, u32[]{:S(2)}) collective-permute-start(bf16[2,128,512]{2,1,0:T(8,128)(2,1)S(1)} %get-tuple-element.28), channel_id=1, source_target_pairs={{0,24},{1,7},{2,26},{3,1},{4,28},{5,3},{6,30},{7,5},{8,0},{9,15},{... | collective-permute-start | bytes 786440 | tf_op jit(solution)/shard_map/ppermute | solution.py:34
  99.9 10.4 %collective-permute-start.18 = (bf16[2,128,512]{2,1,0:T(8,128)(2,1)S(1)}, bf16[2,128,512]{2,1,0:T(8,128)(2,1)S(1)}, u32[]{:S(2)}, u32[]{:S(2)}) collective-permute-start(bf16[2,128,512]{2,1,0:T(8,128)(2,1)S(1)} %get-tuple-element.29), channel_id=1, source_target_pairs={{0,16},{1,5},{2,18},{3,7},{4,20},{5,1},{6,22},{7,3},{8,24},{9,13},... | collective-permute-start | bytes 786440 | tf_op jit(solution)/shard_map/ppermute | solution.py:34
  101.3 9.0 %collective-permute-start.17 = (bf16[2,128,512]{2,1,0:T(8,128)(2,1)S(1)}, bf16[2,128,512]{2,1,0:T(8,128)(2,1)S(1)}, u32[]{:S(2)}, u32[]{:S(2)}) collective-permute-start(bf16[2,128,512]{2,1,0:T(8,128)(2,1)S(1)} %get-tuple-element.30), channel_id=1, source_target_pairs={{0,8},{1,3},{2,10},{3,5},{4,12},{5,7},{6,14},{7,1},{8,16},{9,11},{... | collective-permute-start | bytes 786440 | tf_op jit(solution)/shard_map/ppermute | solution.py:34
  108.6 4.4 %collective-permute-start.23 = (bf16[8,128,128]{2,1,0:T(8,128)(2,1)S(1)}, bf16[8,128,128]{2,1,0:T(8,128)(2,1)S(1)}, u32[]{:S(2)}, u32[]{:S(2)}) collective-permute-start(bf16[8,128,128]{2,1,0:T(8,128)(2,1)S(1)} %slice_bitcast_fusion), channel_id=1, source_target_pairs={{0,1},{1,0},{2,3},{3,2},{4,5},{5,4},{6,7},{7,6},{8,9},{9,8},{10,11... | collective-permute-start | bytes 786440 | tf_op jit(solution)/shard_map/ppermute | solution.py:42
  110.5 3.6 %collective-permute-start.19 = (bf16[128,512]{1,0:T(8,128)(2,1)S(1)}, bf16[128,512]{1,0:T(8,128)(2,1)S(1)}, u32[]{:S(2)}, u32[]{:S(2)}) collective-permute-start(bf16[128,512]{1,0:T(8,128)(2,1)S(1)} %slice_bitcast_fusion.7), channel_id=1, source_target_pairs={{0,1},{1,0},{2,3},{3,2},{4,5},{5,4},{6,7},{7,6},{8,9},{9,8},{10,11... | collective-permute-start | bytes 393224 | tf_op jit(solution)/shard_map/ppermute | solution.py:42

commit v4 on v3

--- a/solution.py
+++ b/solution.py
@@ -1,3 +1,4 @@
+import functools
 import math
 
 import jax
@@ -35,7 +36,9 @@
 
 
 def z_shift(values, step):
-    return lax.ppermute(values, "z", [(i, (i + step) % RING) for i in range(RING)])
+    pairs = [(i * 2, (i + step) % RING * 2) for i in range(RING)]
+    pairs += [(i * 2 + 1, (i - step) % RING * 2 + 1) for i in range(RING)]
+    return lax.ppermute(values, ("z", "core"), pairs)
 
 
 def swap(values):
@@ -67,11 +70,20 @@
     return copies
 
 
+def from_z(where_ref, d):
+    return (where_ref[1] + jnp.where(where_ref[0] == 0, -d, d)) & 3
+
+
+def column(where_ref, d, r):
+    return from_z(where_ref, d) * 2 + (r ^ where_ref[0])
+
+
 def spots(where_ref, codes_ref, d, r):
-    core, z = where_ref[0], where_ref[1]
+    core = where_ref[0]
+    z = from_z(where_ref, d)
     out = []
     for s in range(8):
-        code = codes_ref[r, (z - d) & 3, s]
+        code = codes_ref[r, z, s]
         slot = code >> 3
         first = jnp.where(core == 0, slot * 4, slot)
         cols = pl.ds(pl.multiple_of((code & 3) * BLK, BLK), BLK)
@@ -97,6 +109,7 @@
 
     def body(step, carry):
         d, r = step >> 1, step & 1
+        at = column(where_ref, d, r)
         places, stride = spots(where_ref, codes_ref, d, r)
         pick(acts, picked, places, stride)
 
@@ -108,15 +121,15 @@
                 preferred_element_type=jnp.float32,
             )
             t = jnp.tanh(GELU_SCALE * (pre + GELU_CUBIC * pre * pre * pre))
-            sent[step] = (0.5 * pre * (1.0 + t)).astype(jnp.bfloat16)
-            slope[step] = 0.5 * (1.0 + t) + 0.5 * pre * (1.0 - t * t) * GELU_SCALE * (
+            sent[at] = (0.5 * pre * (1.0 + t)).astype(jnp.bfloat16)
+            slope[at] = 0.5 * (1.0 + t) + 0.5 * pre * (1.0 - t * t) * GELU_SCALE * (
                 1.0 + 3.0 * GELU_CUBIC * pre * pre
             )
 
         @pl.when(core == 1)
         def _():
             flat = jnp.concatenate([weights[d, r, s] for s in range(8)], axis=1)
-            sent[step ^ 1] = lax.dot_general(
+            sent[at] = lax.dot_general(
                 picked[...], flat, (((1,), (1,)), ((), ())), preferred_element_type=jnp.float32
             ).astype(jnp.bfloat16)
 
@@ -135,6 +148,7 @@
 
     def body(step, carry):
         d, r = step >> 1, step & 1
+        row = column(where_ref, d, r)
         places, stride = spots(where_ref, codes_ref, d, r)
 
         def scatter(s, product):
@@ -148,7 +162,7 @@
 
         @pl.when(core == 0)
         def _():
-            mine = pulled(came, slope, step)
+            mine = pulled(came, slope, row)
             for s in range(0, 8, 2):
                 pair = weights[d, r, s : s + 2].reshape(2 * BLK, BLK)
                 scatter(
@@ -160,7 +174,7 @@
 
         @pl.when(core == 1)
         def _():
-            mine = came[step ^ 1]
+            mine = came[row]
             for s in range(0, 8, 2):
                 pair = jnp.concatenate([weights[d, r, s], weights[d, r, s + 1]], axis=1)
                 scatter(s, jnp.dot(mine, pair, preferred_element_type=jnp.float32))
@@ -172,12 +186,13 @@
         out[...] = acc[n].astype(jnp.bfloat16)
 
 
-def grads_kernel(where_ref, codes_ref, acts, came, slope, g0, g1, g2, g3, picked):
+def grads_kernel(slots, where_ref, codes_ref, acts, came, slope, *refs):
     core = where_ref[0]
-    for d, grads in enumerate((g0, g1, g2, g3)):
+    picked = refs[-1]
+    for d, grads in zip(slots, refs):
 
         def body(r, carry):
-            step = d * 2 + r
+            row = column(where_ref, d, r)
             places, stride = spots(where_ref, codes_ref, d, r)
             pick(acts, picked, places, stride)
 
@@ -185,7 +200,7 @@
             def _():
                 grad = lax.dot_general(
                     picked[...],
-                    pulled(came, slope, step),
+                    pulled(came, slope, row),
                     (((0,), (0,)), ((), ())),
                     preferred_element_type=jnp.float32,
                 )
@@ -194,7 +209,7 @@
             @pl.when(core == 1)
             def _():
                 grad = lax.dot_general(
-                    came[step ^ 1],
+                    came[row],
                     picked[...],
                     (((0,), (0,)), ((), ())),
                     preferred_element_type=jnp.float32,
@@ -257,15 +272,15 @@
     )(where, codes, weights, came, slope)
 
 
-def block_grads(where, codes, acts, came, slope):
+def block_grads(slots, where, codes, acts, came, slope):
     return pl.pallas_call(
-        grads_kernel,
-        out_shape=[GRAD] * 4,
+        functools.partial(grads_kernel, slots),
+        out_shape=[GRAD] * len(slots),
         in_specs=[SMEM, SMEM] + [VMEM] * 3,
-        out_specs=[VMEM] * 4,
+        out_specs=[VMEM] * len(slots),
         scratch_shapes=[pltpu.VMEM((512, 8 * BLK), jnp.bfloat16)],
         compiler_params=pltpu.CompilerParams(vmem_limit_bytes=16 << 20),
-        cost_estimate=cost(1 << 30, 8 << 20),
+        cost_estimate=cost(1 << 29, 8 << 20),
         name="grads",
     )(where, codes, acts, came, slope)
 
@@ -295,7 +310,9 @@
     acts, weights, sent, slope = enter(where, codes, acts, weights)
     came = swap(sent)
     chunks = sums(where, codes, weights, came, slope)
-    grads = block_grads(where, codes, acts, came, slope)
+    grads_1, grads_3 = block_grads((1, 3), where, codes, acts, came, slope)
+    grads_2, grads_0 = block_grads((2, 0), where, codes, acts, came, slope)
+    grads = [grads_0, grads_1, grads_2, grads_3]
 
     summed = reduce(chunks, first(False)).astype(jnp.bfloat16)
     final = reduce([summed[n] for n in range(RING)], first(True)).astype(jnp.bfloat16)

time: 115 us -> 110 us (0.957)
  waiting for transfers between devices: 48.8 us -> 43.8 us
    ppermute x6, waiting for transfers between devices: 29.9 us -> 22.8 us  [z_shift(): return lax.ppermute(values, ('z', 'core'), pairs)]
    ppermute x12, waiting for transfers between devices: 15.7 us -> 17.7 us  [mixed_shift(): return lax.ppermute(values, MIXED, mixed_pairs(step, first))]
    ppermute x12, starting transfers between devices: 16.8 us -> 15.1 us  [mixed_shift(): return lax.ppermute(values, MIXED, mixed_pairs(step, first))]
    pallas_call x1 -> x2, Pallas kernels: 5.93 us -> 6.61 us  [block_grads(): pl.pallas_call(functools.partial(grads_kernel, slots), out_shape=[GRAD] *...]
  transfers between devices with their start and end apart: 24 -> 24, of which waited for: 10 -> 11; matrix products, arithmetic and copies ran while one was open for 3% -> 3% of each run, Pallas kernels for 5% -> 6%
where the time goes in v4:
time: 110 us
  waiting for transfers between devices  43.8 us (40%)
  starting transfers between devices  38 us (35%)
  Pallas kernels  22.5 us (20%)
  other arithmetic  4.99 us (5%)
    ppermute x6, waiting for transfers between devices, z_shift(): return lax.ppermute(values, ('z', 'core'), pairs)  22.8 us
    ppermute x12, waiting for transfers between devices, mixed_shift(): return lax.ppermute(values, MIXED, mixed_pairs(step, first))  17.7 us
    ppermute x12, starting transfers between devices, mixed_shift(): return lax.ppermute(values, MIXED, mixed_pairs(step, first))  15.1 us
    ppermute x6, starting transfers between devices, z_shift(): return lax.ppermute(values, ('z', 'core'), pairs)  13.4 us
    ppermute x6, starting transfers between devices, swap(): return lax.ppermute(values, 'core', [(0, 1), (1, 0)])  9.49 us
    pallas_call x1, Pallas kernels, enter(): pl.pallas_call(enter_kernel, out_shape=[jax.ShapeDtypeStruct(ACTS, jnp.bf...  8.78 us
    pallas_call x1, Pallas kernels, sums(): pl.pallas_call(sums_kernel, out_shape=[CHUNK] * 4, in_specs=[SMEM, SMEM]...  7.1 us
    pallas_call x2, Pallas kernels, block_grads(): pl.pallas_call(functools.partial(grads_kernel, slots), out_shape=[GRAD] *...  6.61 us
  transfers between devices with their start and end apart: 24, of which 11 were waited for; matrix products, arithmetic and copies ran while one was open for 3% of the time, Pallas kernels for 6%

profile of v4, /device:TPU:1, one launch (start us, length us, event | category | flops | bytes accessed | tf_op | source)
XLA Modules:
  0.0 110.3 jit_solution(269997023014445277)
XLA Ops:
  0.6 1.0 select_bitcast_fusion.3
  1.6 1.5 %collective-permute-start.1 = (bf16[128,512]{1,0:T(8,128)(2,1)S(1)}, bf16[128,512]{1,0:T(8,128)(2,1)S(1)}, u32[]{:S(2)}, u32[]{:S(2)}) collective-permute-start(bf16[128,512]{1,0:T(8,128)(2,1)S(1)} %get-tuple-element.40), channel_id=1, source_target_pairs={{0,1},{1,0},{2,3},{3,2},{4,5},{5,4},{6,7},{7,6},{8,9},{9,8},{10,11... | collective-permute-start | bytes 393224 | tf_op jit(solution)/shard_map/ppermute | solution.py:45
  3.1 1.1 broadcast_select_fusion
  4.2 0.0 copy-start
  4.2 0.0 copy-start.1
  4.2 0.1 collective-permute-start.8
  4.3 0.0 collective-permute-done.1
  4.4 3.1 %collective-permute-start.3 = (bf16[2,128,512]{2,1,0:T(8,128)(2,1)S(1)}, bf16[2,128,512]{2,1,0:T(8,128)(2,1)S(1)}, u32[]{:S(2)}, u32[]{:S(2)}) collective-permute-start(bf16[2,128,512]{2,1,0:T(8,128)(2,1)S(1)} %get-tuple-element.38), channel_id=1, source_target_pairs={{0,16},{1,5},{2,18},{3,7},{4,20},{5,1},{6,22},{7,3},{8,24},{9,13},... | collective-permute-start | bytes 786440 | tf_op jit(solution)/shard_map/ppermute | solution.py:35
  7.5 0.4 collective-permute-start.2
  7.9 2.3 %collective-permute-start.4 = (bf16[2,128,512]{2,1,0:T(8,128)(2,1)S(1)}, bf16[2,128,512]{2,1,0:T(8,128)(2,1)S(1)}, u32[]{:S(2)}, u32[]{:S(2)}) collective-permute-start(bf16[2,128,512]{2,1,0:T(8,128)(2,1)S(1)} %get-tuple-element.38), channel_id=1, source_target_pairs={{0,24},{1,7},{2,26},{3,1},{4,28},{5,3},{6,30},{7,5},{8,0},{9,15},{... | collective-permute-start | bytes 786440 | tf_op jit(solution)/shard_map/ppermute | solution.py:35
  10.1 0.0 collective-permute-done.8
  10.1 0.1 pad_maximum_fusion.1.w0
  10.2 1.7 %collective-permute-start.11 = (bf16[2,8,128,128]{3,2,1,0:T(8,128)(2,1)S(1)}, bf16[2,8,128,128]{3,2,1,0:T(8,128)(2,1)S(1)}, u32[]{:S(2)}, u32[]{:S(2)}) collective-permute-start(bf16[2,8,128,128]{3,2,1,0:T(8,128)(2,1)S(1)} %pad_maximum_fusion.1.w0), channel_id=1, source_target_pairs={{0,96},{32,0},{64,32},{96,64},{1,33},{33,65},{65,97},{97,1},{2,98}... | collective-permute-start | bytes 1572872 | tf_op jit(solution)/shard_map/ppermute | solution.py:41
  11.9 0.0 collective-permute-done.3
  11.9 2.4 %collective-permute-done.2 = bf16[2,128,512]{2,1,0:T(8,128)(2,1)S(1)} collective-permute-done((bf16[2,128,512]{2,1,0:T(8,128)(2,1)S(1)}, bf16[2,128,512]{2,1,0:T(8,128)(2,1)S(1)}, u32[]{:S(2)}, u32[]{:S(2)}) %collective-permute-start.2) | collective-permute-done | bytes 262176 | tf_op jit(solution)/shard_map/ppermute | solution.py:35
  14.3 0.4 collective-permute-done.4
  14.7 0.1 pad_maximum_fusion.a0
  14.8 2.5 %collective-permute-start.7 = (bf16[4,2,128,512]{3,2,1,0:T(8,128)(2,1)S(1)}, bf16[4,2,128,512]{3,2,1,0:T(8,128)(2,1)S(1)}, u32[]{:S(2)}, u32[]{:S(2)}) collective-permute-start(bf16[4,2,128,512]{3,2,1,0:T(8,128)(2,1)S(1)} %pad_maximum_fusion.a0), channel_id=1, source_target_pairs={{0,6},{1,25},{2,0},{3,27},{4,2},{5,29},{6,4},{7,31},{8,14},{9,1},{... | collective-permute-start | bytes 3145736 | tf_op jit(solution)/shard_map/ppermute | solution.py:35
  17.4 0.5 collective-permute-start.6
  17.9 0.6 collective-permute-start.5
  18.5 0.1 copy.10
  18.6 0.1 copy.11
  18.7 2.2 %collective-permute-start = (s32[4,8]{1,0:T(4,128)S(1)}, s32[4,8]{1,0:T(4,128)S(1)}, u32[]{:S(2)}, u32[]{:S(2)}) collective-permute-start(s32[4,8]{1,0:T(4,128)S(1)} %bitcast.58), channel_id=1, source_target_pairs={{0,1},{1,0},{2,3},{3,2},{4,5},{5,4},{6,7},{7,6},{8,9},{9,8},{10,11... | collective-permute-start | bytes 392 | tf_op jit(solution)/shard_map/ppermute | solution.py:45
  20.9 0.8 collective-permute-done
  21.7 3.6 %collective-permute-start.10 = (bf16[2,8,128,128]{3,2,1,0:T(8,128)(2,1)S(1)}, bf16[2,8,128,128]{3,2,1,0:T(8,128)(2,1)}, u32[]{:S(2)}, u32[]{:S(2)}) collective-permute-start(bf16[2,8,128,128]{3,2,1,0:T(8,128)(2,1)S(1)} %pad_maximum_fusion.1.w0), channel_id=1, source_target_pairs={{0,64},{32,96},{64,0},{96,32},{1,65},{33,97},{65,1},{97,33},{2,66}... | collective-permute-start | bytes 1572872 | tf_op jit(solution)/shard_map/ppermute | solution.py:41
  25.3 0.0 collective-permute-done.11.w3
  25.3 0.4 collective-permute-start.9
  25.7 0.1 pad_add_fusion.1.where_ref
  25.8 11.7 %collective-permute-done.10.w2 = bf16[2,8,128,128]{3,2,1,0:T(8,128)(2,1)} collective-permute-done((bf16[2,8,128,128]{3,2,1,0:T(8,128)(2,1)S(1)}, bf16[2,8,128,128]{3,2,1,0:T(8,128)(2,1)}, u32[]{:S(2)}, u32[]{:S(2)}) %collective-permute-start.10) | collective-permute-done | bytes 524320 | tf_op jit(solution)/shard_map/ppermute | solution.py:41
  37.5 6.8 %collective-permute-done.9.w1 = bf16[2,8,128,128]{3,2,1,0:T(8,128)(2,1)} collective-permute-done((bf16[2,8,128,128]{3,2,1,0:T(8,128)(2,1)S(1)}, bf16[2,8,128,128]{3,2,1,0:T(8,128)(2,1)}, u32[]{:S(2)}, u32[]{:S(2)}) %collective-permute-start.9) | collective-permute-done | bytes 524320 | tf_op jit(solution)/shard_map/ppermute | solution.py:41
  44.3 0.0 collective-permute-done.7.a3
  44.3 0.0 collective-permute-done.6.a2
  44.3 0.0 collective-permute-done.5.a1
  44.3 8.8 %enter.1 = (bf16[4,4,2,128,512]{4,3,2,1,0:T(8,128)(2,1)S(1)}, bf16[4,2,8,128,128]{4,3,2,1,0:T(8,128)(2,1)S(1)}, bf16[8,512,128]{2,1,0:T(8,128)(2,1)S(1)}, f32[8,512,128]{2,1,0:T(8,128)S(1)}) custom-call(s32[2]{0:T(128)S(1)} %pad_add_fusion.1.where_ref, s32[2,4,8]{2,1,0:T(4,128)S(1)} %and_add_fusion.codes_ref, ...), custom_call_target="tpu_custom_call" | custom-call | flops 1073741824 | bytes 8388608 | tf_op jit(solution)/shard_map/enter/pallas_call | solution.py:242
  53.1 2.9 %collective-permute-start.12 = (bf16[8,512,128]{2,1,0:T(8,128)(2,1)S(1)}, bf16[8,512,128]{2,1,0:T(8,128)(2,1)S(1)}, u32[]{:S(2)}, u32[]{:S(2)}) collective-permute-start(bf16[8,512,128]{2,1,0:T(8,128)(2,1)S(1)} %get-tuple-element.17), channel_id=1, source_target_pairs={{0,1},{1,0},{2,3},{3,2},{4,5},{5,4},{6,7},{7,6},{8,9},{9,8},{10,11... | collective-permute-start | bytes 3145736 | tf_op jit(solution)/shard_map/ppermute | solution.py:45
  56.0 2.3 %collective-permute-done.12.came = bf16[8,512,128]{2,1,0:T(8,128)(2,1)S(1)} collective-permute-done((bf16[8,512,128]{2,1,0:T(8,128)(2,1)S(1)}, bf16[8,512,128]{2,1,0:T(8,128)(2,1)S(1)}, u32[]{:S(2)}, u32[]{:S(2)}) %collective-permute-start.12) | collective-permute-done | bytes 1048608 | tf_op jit(solution)/shard_map/ppermute | solution.py:45
  58.3 7.1 %sums.1 = (bf16[4,2,128,512]{3,2,1,0:T(8,128)(2,1)S(1)}, bf16[4,2,128,512]{3,2,1,0:T(8,128)(2,1)S(1)}, bf16[4,2,128,512]{3,2,1,0:T(8,128)(2,1)S(1)}, bf16[4,2,128,512]{3,2,1,0:T(8,128)(2,1)S(1)}) custom-call(s32[2]{0:T(128)S(1)} %pad_add_fusion.1.where_ref, s32[2,4,8]{2,1,0:T(4,128)S(1)} %and_add_fusion.codes_ref, ...), custom_call_target="tpu_custom_call" | custom-call | flops 1073741824 | bytes 8388608 | tf_op jit(solution)/shard_map/sums/pallas_call | solution.py:263
  65.4 2.9 %collective-permute-start.13 = (bf16[4,2,128,512]{3,2,1,0:T(8,128)(2,1)S(1)}, bf16[4,2,128,512]{3,2,1,0:T(8,128)(2,1)S(1)}, u32[]{:S(2)}, u32[]{:S(2)}) collective-permute-start(bf16[4,2,128,512]{3,2,1,0:T(8,128)(2,1)S(1)} %get-tuple-element.20), channel_id=1, source_target_pairs={{0,6},{1,25},{2,0},{3,27},{4,2},{5,29},{6,4},{7,31},{8,14},{9,1},{... | collective-permute-start | bytes 3145736 | tf_op jit(solution)/shard_map/ppermute | solution.py:35
  68.2 0.0 collective-permute-start.14
  68.2 1.3 %collective-permute-start.15 = (bf16[4,2,128,512]{3,2,1,0:T(8,128)(2,1)S(1)}, bf16[4,2,128,512]{3,2,1,0:T(8,128)(2,1)S(1)}, u32[]{:S(2)}, u32[]{:S(2)}) collective-permute-start(bf16[4,2,128,512]{3,2,1,0:T(8,128)(2,1)S(1)} %get-tuple-element.22), channel_id=1, source_target_pairs={{0,4},{1,17},{2,6},{3,19},{4,0},{5,21},{6,2},{7,23},{8,12},{9,25},... | collective-permute-start | bytes 3145736 | tf_op jit(solution)/shard_map/ppermute | solution.py:35
  69.5 3.3 %grads.3 = (bf16[2,8,128,128]{3,2,1,0:T(8,128)(2,1)S(1)}, bf16[2,8,128,128]{3,2,1,0:T(8,128)(2,1)S(1)}) custom-call(s32[2]{0:T(128)S(1)} %pad_add_fusion.1.where_ref, s32[2,4,8]{2,1,0:T(4,128)S(1)} %and_add_fusion.codes_ref, bf16[4,4,2,128,512]{4,3,2,1,0:T(8,128)(2,1)S(1)} %get-tuple-element.23.acts, bf16[8,512,128]{2,1,0:T(8,128)(2,1)S(1)} %collective-permute-done.12.came, ...), custom_call_target="tpu_custom_call" | custom-call | flops 536870912 | bytes 8388608 | tf_op jit(solution)/shard_map/grads/pallas_call | solution.py:276
  72.8 1.7 %collective-permute-start.20 = (bf16[2,8,128,128]{3,2,1,0:T(8,128)(2,1)S(1)}, bf16[2,8,128,128]{3,2,1,0:T(8,128)(2,1)S(1)}, u32[]{:S(2)}, u32[]{:S(2)}) collective-permute-start(bf16[2,8,128,128]{3,2,1,0:T(8,128)(2,1)S(1)} %get-tuple-element.25), channel_id=1, source_target_pairs={{0,96},{32,0},{64,32},{96,64},{1,33},{33,65},{65,97},{97,1},{2,98}... | collective-permute-start | bytes 1572872 | tf_op jit(solution)/shard_map/ppermute | solution.py:41
  74.5 2.4 %collective-permute-start.21 = (bf16[2,8,128,128]{3,2,1,0:T(8,128)(2,1)S(1)}, bf16[2,8,128,128]{3,2,1,0:T(8,128)(2,1)S(1)}, u32[]{:S(2)}, u32[]{:S(2)}) collective-permute-start(bf16[2,8,128,128]{3,2,1,0:T(8,128)(2,1)S(1)} %get-tuple-element.26), channel_id=1, source_target_pairs={{0,32},{32,64},{64,96},{96,0},{1,97},{33,1},{65,33},{97,65},{2,34}... | collective-permute-start | bytes 1572872 | tf_op jit(solution)/shard_map/ppermute | solution.py:41
  76.9 3.3 %grads.2 = (bf16[2,8,128,128]{3,2,1,0:T(8,128)(2,1)S(1)}, bf16[2,8,128,128]{3,2,1,0:T(8,128)(2,1)S(1)}) custom-call(s32[2]{0:T(128)S(1)} %pad_add_fusion.1.where_ref, s32[2,4,8]{2,1,0:T(4,128)S(1)} %and_add_fusion.codes_ref, bf16[4,4,2,128,512]{4,3,2,1,0:T(8,128)(2,1)S(1)} %get-tuple-element.23.acts, bf16[8,512,128]{2,1,0:T(8,128)(2,1)S(1)} %collective-permute-done.12.came, ...), custom_call_target="tpu_custom_call" | custom-call | flops 536870912 | bytes 8388608 | tf_op jit(solution)/shard_map/grads/pallas_call | solution.py:276
  80.2 11.0 %collective-permute-done.13 = bf16[4,2,128,512]{3,2,1,0:T(8,128)(2,1)S(1)} collective-permute-done((bf16[4,2,128,512]{3,2,1,0:T(8,128)(2,1)S(1)}, bf16[4,2,128,512]{3,2,1,0:T(8,128)(2,1)S(1)}, u32[]{:S(2)}, u32[]{:S(2)}) %collective-permute-start.13) | collective-permute-done | bytes 1048608 | tf_op jit(solution)/shard_map/ppermute | solution.py:35
  91.2 3.6 %collective-permute-start.22 = (bf16[2,8,128,128]{3,2,1,0:T(8,128)(2,1)S(1)}, bf16[2,8,128,128]{3,2,1,0:T(8,128)(2,1)S(1)}, u32[]{:S(2)}, u32[]{:S(2)}) collective-permute-start(bf16[2,8,128,128]{3,2,1,0:T(8,128)(2,1)S(1)} %get-tuple-element.27), channel_id=1, source_target_pairs={{0,64},{32,96},{64,0},{96,32},{1,65},{33,97},{65,1},{97,33},{2,66}... | collective-permute-start | bytes 1572872 | tf_op jit(solution)/shard_map/ppermute | solution.py:41
  94.8 0.0 collective-permute-done.14
  94.8 0.0 collective-permute-done.15
  94.8 0.6 add_convert_fusion
  95.4 0.1 slice_bitcast_fusion.4
  95.5 0.4 collective-permute-start.16
  95.9 0.3 collective-permute-start.18
  96.2 0.8 collective-permute-start.17
  97.0 0.0 collective-permute-done.21
  97.0 4.3 %collective-permute-done.22 = bf16[2,8,128,128]{3,2,1,0:T(8,128)(2,1)S(1)} collective-permute-done((bf16[2,8,128,128]{3,2,1,0:T(8,128)(2,1)S(1)}, bf16[2,8,128,128]{3,2,1,0:T(8,128)(2,1)S(1)}, u32[]{:S(2)}, u32[]{:S(2)}) %collective-permute-start.22) | collective-permute-done | bytes 524320 | tf_op jit(solution)/shard_map/ppermute | solution.py:41
  101.4 0.3 multiply_convert_fusion
  101.8 0.1 collective-permute-start.23
  101.9 1.1 collective-permute-done.18
  103.0 2.8 %collective-permute-done.17 = bf16[2,128,512]{2,1,0:T(8,128)(2,1)S(1)} collective-permute-done((bf16[2,128,512]{2,1,0:T(8,128)(2,1)S(1)}, bf16[2,128,512]{2,1,0:T(8,128)(2,1)S(1)}, u32[]{:S(2)}, u32[]{:S(2)}) %collective-permute-start.17) | collective-permute-done | bytes 262176 | tf_op jit(solution)/shard_map/ppermute | solution.py:35
  105.7 0.1 fusion.2
  105.9 2.7 %collective-permute-start.19 = (bf16[128,512]{1,0:T(8,128)(2,1)S(1)}, bf16[128,512]{1,0:T(8,128)(2,1)S(1)}, u32[]{:S(2)}, u32[]{:S(2)}) collective-permute-start(bf16[128,512]{1,0:T(8,128)(2,1)S(1)} %slice_bitcast_fusion.7), channel_id=1, source_target_pairs={{0,1},{1,0},{2,3},{3,2},{4,5},{5,4},{6,7},{7,6},{8,9},{9,8},{10,11... | collective-permute-start | bytes 393224 | tf_op jit(solution)/shard_map/ppermute | solution.py:45
  108.6 0.8 select_bitcast_fusion
  109.4 0.2 collective-permute-done.19
  109.6 0.7 broadcast_select_fusion.1
  (10 shorter events, 0.1 us)
Async XLA Ops:
  1.6 2.7 %collective-permute-start.1 = (bf16[128,512]{1,0:T(8,128)(2,1)S(1)}, bf16[128,512]{1,0:T(8,128)(2,1)S(1)}, u32[]{:S(2)}, u32[]{:S(2)}) collective-permute-start(bf16[128,512]{1,0:T(8,128)(2,1)S(1)} %get-tuple-element.40), channel_id=1, source_target_pairs={{0,1},{1,0},{2,3},{3,2},{4,5},{5,4},{6,7},{7,6},{8,9},{9,8},{10,11... | collective-permute-start | bytes 393224 | tf_op jit(solution)/shard_map/ppermute | solution.py:45
  4.2 14.3 %copy-start = (s32[16,8]{0,1:T(8,128)S(1)}, s32[16,8]{0,1:T(8,128)}, u32[]{:S(2)}) copy-start(s32[16,8]{0,1:T(8,128)} %param.8) | copy-start | bytes 1540
  4.2 14.4 %copy-start.1 = (s32[16,8]{0,1:T(8,128)S(1)}, s32[16,8]{0,1:T(8,128)}, u32[]{:S(2)}) copy-start(s32[16,8]{0,1:T(8,128)} %param.10) | copy-start | bytes 1540
  4.2 5.9 %collective-permute-start.8 = (bf16[8,128,128]{2,1,0:T(8,128)(2,1)S(1)}, bf16[8,128,128]{2,1,0:T(8,128)(2,1)S(1)}, u32[]{:S(2)}, u32[]{:S(2)}) collective-permute-start(bf16[8,128,128]{2,1,0:T(8,128)(2,1)S(1)} %get-tuple-element.34), channel_id=1, source_target_pairs={{0,1},{1,0},{2,3},{3,2},{4,5},{5,4},{6,7},{7,6},{8,9},{9,8},{10,11... | collective-permute-start | bytes 786440 | tf_op jit(solution)/shard_map/ppermute | solution.py:45
  4.4 7.5 %collective-permute-start.3 = (bf16[2,128,512]{2,1,0:T(8,128)(2,1)S(1)}, bf16[2,128,512]{2,1,0:T(8,128)(2,1)S(1)}, u32[]{:S(2)}, u32[]{:S(2)}) collective-permute-start(bf16[2,128,512]{2,1,0:T(8,128)(2,1)S(1)} %get-tuple-element.38), channel_id=1, source_target_pairs={{0,16},{1,5},{2,18},{3,7},{4,20},{5,1},{6,22},{7,3},{8,24},{9,13},... | collective-permute-start | bytes 786440 | tf_op jit(solution)/shard_map/ppermute | solution.py:35
  7.5 6.9 %collective-permute-start.2 = (bf16[2,128,512]{2,1,0:T(8,128)(2,1)S(1)}, bf16[2,128,512]{2,1,0:T(8,128)(2,1)S(1)}, u32[]{:S(2)}, u32[]{:S(2)}) collective-permute-start(bf16[2,128,512]{2,1,0:T(8,128)(2,1)S(1)} %get-tuple-element.38), channel_id=1, source_target_pairs={{0,8},{1,3},{2,10},{3,5},{4,12},{5,7},{6,14},{7,1},{8,16},{9,11},{... | collective-permute-start | bytes 786440 | tf_op jit(solution)/shard_map/ppermute | solution.py:35
  7.9 6.9 %collective-permute-start.4 = (bf16[2,128,512]{2,1,0:T(8,128)(2,1)S(1)}, bf16[2,128,512]{2,1,0:T(8,128)(2,1)S(1)}, u32[]{:S(2)}, u32[]{:S(2)}) collective-permute-start(bf16[2,128,512]{2,1,0:T(8,128)(2,1)S(1)} %get-tuple-element.38), channel_id=1, source_target_pairs={{0,24},{1,7},{2,26},{3,1},{4,28},{5,3},{6,30},{7,5},{8,0},{9,15},{... | collective-permute-start | bytes 786440 | tf_op jit(solution)/shard_map/ppermute | solution.py:35
  10.2 15.1 %collective-permute-start.11 = (bf16[2,8,128,128]{3,2,1,0:T(8,128)(2,1)S(1)}, bf16[2,8,128,128]{3,2,1,0:T(8,128)(2,1)S(1)}, u32[]{:S(2)}, u32[]{:S(2)}) collective-permute-start(bf16[2,8,128,128]{3,2,1,0:T(8,128)(2,1)S(1)} %pad_maximum_fusion.1.w0), channel_id=1, source_target_pairs={{0,96},{32,0},{64,32},{96,64},{1,33},{33,65},{65,97},{97,1},{2,98}... | collective-permute-start | bytes 1572872 | tf_op jit(solution)/shard_map/ppermute | solution.py:41
  14.8 29.4 %collective-permute-start.7 = (bf16[4,2,128,512]{3,2,1,0:T(8,128)(2,1)S(1)}, bf16[4,2,128,512]{3,2,1,0:T(8,128)(2,1)S(1)}, u32[]{:S(2)}, u32[]{:S(2)}) collective-permute-start(bf16[4,2,128,512]{3,2,1,0:T(8,128)(2,1)S(1)} %pad_maximum_fusion.a0), channel_id=1, source_target_pairs={{0,6},{1,25},{2,0},{3,27},{4,2},{5,29},{6,4},{7,31},{8,14},{9,1},{... | collective-permute-start | bytes 3145736 | tf_op jit(solution)/shard_map/ppermute | solution.py:35
  17.4 26.9 %collective-permute-start.6 = (bf16[4,2,128,512]{3,2,1,0:T(8,128)(2,1)S(1)}, bf16[4,2,128,512]{3,2,1,0:T(8,128)(2,1)}, u32[]{:S(2)}, u32[]{:S(2)}) collective-permute-start(bf16[4,2,128,512]{3,2,1,0:T(8,128)(2,1)S(1)} %pad_maximum_fusion.a0), channel_id=1, source_target_pairs={{0,4},{1,17},{2,6},{3,19},{4,0},{5,21},{6,2},{7,23},{8,12},{9,25},... | collective-permute-start | bytes 3145736 | tf_op jit(solution)/shard_map/ppermute | solution.py:35
  17.9 26.4 %collective-permute-start.5 = (bf16[4,2,128,512]{3,2,1,0:T(8,128)(2,1)S(1)}, bf16[4,2,128,512]{3,2,1,0:T(8,128)(2,1)}, u32[]{:S(2)}, u32[]{:S(2)}) collective-permute-start(bf16[4,2,128,512]{3,2,1,0:T(8,128)(2,1)S(1)} %pad_maximum_fusion.a0), channel_id=1, source_target_pairs={{0,2},{1,9},{2,4},{3,11},{4,6},{5,13},{6,0},{7,15},{8,10},{9,17},{... | collective-permute-start | bytes 3145736 | tf_op jit(solution)/shard_map/ppermute | solution.py:35
  18.7 3.0 %collective-permute-start = (s32[4,8]{1,0:T(4,128)S(1)}, s32[4,8]{1,0:T(4,128)S(1)}, u32[]{:S(2)}, u32[]{:S(2)}) collective-permute-start(s32[4,8]{1,0:T(4,128)S(1)} %bitcast.58), channel_id=1, source_target_pairs={{0,1},{1,0},{2,3},{3,2},{4,5},{5,4},{6,7},{7,6},{8,9},{9,8},{10,11... | collective-permute-start | bytes 392 | tf_op jit(solution)/shard_map/ppermute | solution.py:45
  21.7 15.8 %collective-permute-start.10 = (bf16[2,8,128,128]{3,2,1,0:T(8,128)(2,1)S(1)}, bf16[2,8,128,128]{3,2,1,0:T(8,128)(2,1)}, u32[]{:S(2)}, u32[]{:S(2)}) collective-permute-start(bf16[2,8,128,128]{3,2,1,0:T(8,128)(2,1)S(1)} %pad_maximum_fusion.1.w0), channel_id=1, source_target_pairs={{0,64},{32,96},{64,0},{96,32},{1,65},{33,97},{65,1},{97,33},{2,66}... | collective-permute-start | bytes 1572872 | tf_op jit(solution)/shard_map/ppermute | solution.py:41
  25.3 19.0 %collective-permute-start.9 = (bf16[2,8,128,128]{3,2,1,0:T(8,128)(2,1)S(1)}, bf16[2,8,128,128]{3,2,1,0:T(8,128)(2,1)}, u32[]{:S(2)}, u32[]{:S(2)}) collective-permute-start(bf16[2,8,128,128]{3,2,1,0:T(8,128)(2,1)S(1)} %pad_maximum_fusion.1.w0), channel_id=1, source_target_pairs={{0,32},{32,64},{64,96},{96,0},{1,97},{33,1},{65,33},{97,65},{2,34}... | collective-permute-start | bytes 1572872 | tf_op jit(solution)/shard_map/ppermute | solution.py:41
  53.1 5.2 %collective-permute-start.12 = (bf16[8,512,128]{2,1,0:T(8,128)(2,1)S(1)}, bf16[8,512,128]{2,1,0:T(8,128)(2,1)S(1)}, u32[]{:S(2)}, u32[]{:S(2)}) collective-permute-start(bf16[8,512,128]{2,1,0:T(8,128)(2,1)S(1)} %get-tuple-element.17), channel_id=1, source_target_pairs={{0,1},{1,0},{2,3},{3,2},{4,5},{5,4},{6,7},{7,6},{8,9},{9,8},{10,11... | collective-permute-start | bytes 3145736 | tf_op jit(solution)/shard_map/ppermute | solution.py:45
  65.4 25.8 %collective-permute-start.13 = (bf16[4,2,128,512]{3,2,1,0:T(8,128)(2,1)S(1)}, bf16[4,2,128,512]{3,2,1,0:T(8,128)(2,1)S(1)}, u32[]{:S(2)}, u32[]{:S(2)}) collective-permute-start(bf16[4,2,128,512]{3,2,1,0:T(8,128)(2,1)S(1)} %get-tuple-element.20), channel_id=1, source_target_pairs={{0,6},{1,25},{2,0},{3,27},{4,2},{5,29},{6,4},{7,31},{8,14},{9,1},{... | collective-permute-start | bytes 3145736 | tf_op jit(solution)/shard_map/ppermute | solution.py:35
  68.2 26.6 %collective-permute-start.14 = (bf16[4,2,128,512]{3,2,1,0:T(8,128)(2,1)S(1)}, bf16[4,2,128,512]{3,2,1,0:T(8,128)(2,1)S(1)}, u32[]{:S(2)}, u32[]{:S(2)}) collective-permute-start(bf16[4,2,128,512]{3,2,1,0:T(8,128)(2,1)S(1)} %get-tuple-element.21), channel_id=1, source_target_pairs={{0,2},{1,9},{2,4},{3,11},{4,6},{5,13},{6,0},{7,15},{8,10},{9,17},{... | collective-permute-start | bytes 3145736 | tf_op jit(solution)/shard_map/ppermute | solution.py:35
  68.2 26.6 %collective-permute-start.15 = (bf16[4,2,128,512]{3,2,1,0:T(8,128)(2,1)S(1)}, bf16[4,2,128,512]{3,2,1,0:T(8,128)(2,1)S(1)}, u32[]{:S(2)}, u32[]{:S(2)}) collective-permute-start(bf16[4,2,128,512]{3,2,1,0:T(8,128)(2,1)S(1)} %get-tuple-element.22), channel_id=1, source_target_pairs={{0,4},{1,17},{2,6},{3,19},{4,0},{5,21},{6,2},{7,23},{8,12},{9,25},... | collective-permute-start | bytes 3145736 | tf_op jit(solution)/shard_map/ppermute | solution.py:35
  72.8 23.4 %collective-permute-start.20 = (bf16[2,8,128,128]{3,2,1,0:T(8,128)(2,1)S(1)}, bf16[2,8,128,128]{3,2,1,0:T(8,128)(2,1)S(1)}, u32[]{:S(2)}, u32[]{:S(2)}) collective-permute-start(bf16[2,8,128,128]{3,2,1,0:T(8,128)(2,1)S(1)} %get-tuple-element.25), channel_id=1, source_target_pairs={{0,96},{32,0},{64,32},{96,64},{1,33},{33,65},{65,97},{97,1},{2,98}... | collective-permute-start | bytes 1572872 | tf_op jit(solution)/shard_map/ppermute | solution.py:41
  74.5 22.5 %collective-permute-start.21 = (bf16[2,8,128,128]{3,2,1,0:T(8,128)(2,1)S(1)}, bf16[2,8,128,128]{3,2,1,0:T(8,128)(2,1)S(1)}, u32[]{:S(2)}, u32[]{:S(2)}) collective-permute-start(bf16[2,8,128,128]{3,2,1,0:T(8,128)(2,1)S(1)} %get-tuple-element.26), channel_id=1, source_target_pairs={{0,32},{32,64},{64,96},{96,0},{1,97},{33,1},{65,33},{97,65},{2,34}... | collective-permute-start | bytes 1572872 | tf_op jit(solution)/shard_map/ppermute | solution.py:41
  91.2 10.2 %collective-permute-start.22 = (bf16[2,8,128,128]{3,2,1,0:T(8,128)(2,1)S(1)}, bf16[2,8,128,128]{3,2,1,0:T(8,128)(2,1)S(1)}, u32[]{:S(2)}, u32[]{:S(2)}) collective-permute-start(bf16[2,8,128,128]{3,2,1,0:T(8,128)(2,1)S(1)} %get-tuple-element.27), channel_id=1, source_target_pairs={{0,64},{32,96},{64,0},{96,32},{1,65},{33,97},{65,1},{97,33},{2,66}... | collective-permute-start | bytes 1572872 | tf_op jit(solution)/shard_map/ppermute | solution.py:41
  95.5 6.4 %collective-permute-start.16 = (bf16[2,128,512]{2,1,0:T(8,128)(2,1)S(1)}, bf16[2,128,512]{2,1,0:T(8,128)(2,1)S(1)}, u32[]{:S(2)}, u32[]{:S(2)}) collective-permute-start(bf16[2,128,512]{2,1,0:T(8,128)(2,1)S(1)} %get-tuple-element.28), channel_id=1, source_target_pairs={{0,24},{1,7},{2,26},{3,1},{4,28},{5,3},{6,30},{7,5},{8,0},{9,15},{... | collective-permute-start | bytes 786440 | tf_op jit(solution)/shard_map/ppermute | solution.py:35
  95.9 7.1 %collective-permute-start.18 = (bf16[2,128,512]{2,1,0:T(8,128)(2,1)S(1)}, bf16[2,128,512]{2,1,0:T(8,128)(2,1)S(1)}, u32[]{:S(2)}, u32[]{:S(2)}) collective-permute-start(bf16[2,128,512]{2,1,0:T(8,128)(2,1)S(1)} %get-tuple-element.29), channel_id=1, source_target_pairs={{0,16},{1,5},{2,18},{3,7},{4,20},{5,1},{6,22},{7,3},{8,24},{9,13},... | collective-permute-start | bytes 786440 | tf_op jit(solution)/shard_map/ppermute | solution.py:35
  96.2 9.5 %collective-permute-start.17 = (bf16[2,128,512]{2,1,0:T(8,128)(2,1)S(1)}, bf16[2,128,512]{2,1,0:T(8,128)(2,1)S(1)}, u32[]{:S(2)}, u32[]{:S(2)}) collective-permute-start(bf16[2,128,512]{2,1,0:T(8,128)(2,1)S(1)} %get-tuple-element.30), channel_id=1, source_target_pairs={{0,8},{1,3},{2,10},{3,5},{4,12},{5,7},{6,14},{7,1},{8,16},{9,11},{... | collective-permute-start | bytes 786440 | tf_op jit(solution)/shard_map/ppermute | solution.py:35
  101.8 6.8 %collective-permute-start.23 = (bf16[8,128,128]{2,1,0:T(8,128)(2,1)S(1)}, bf16[8,128,128]{2,1,0:T(8,128)(2,1)S(1)}, u32[]{:S(2)}, u32[]{:S(2)}) collective-permute-start(bf16[8,128,128]{2,1,0:T(8,128)(2,1)S(1)} %slice_bitcast_fusion), channel_id=1, source_target_pairs={{0,1},{1,0},{2,3},{3,2},{4,5},{5,4},{6,7},{7,6},{8,9},{9,8},{10,11... | collective-permute-start | bytes 786440 | tf_op jit(solution)/shard_map/ppermute | solution.py:45
  105.9 3.7 %collective-permute-start.19 = (bf16[128,512]{1,0:T(8,128)(2,1)S(1)}, bf16[128,512]{1,0:T(8,128)(2,1)S(1)}, u32[]{:S(2)}, u32[]{:S(2)}) collective-permute-start(bf16[128,512]{1,0:T(8,128)(2,1)S(1)} %slice_bitcast_fusion.7), channel_id=1, source_target_pairs={{0,1},{1,0},{2,3},{3,2},{4,5},{5,4},{6,7},{7,6},{8,9},{9,8},{10,11... | collective-permute-start | bytes 393224 | tf_op jit(solution)/shard_map/ppermute | solution.py:45

commit v5 on v4

--- a/solution.py
+++ b/solution.py
@@ -99,127 +99,120 @@
             ]
 
 
+def per_core(where_ref, codes_ref, columns, unroll, for_up, for_down):
+    def run(step_function):
+        def body(turn, carry):
+            for n in range(unroll):
+                step = turn * unroll + n
+                step_function(columns[0] + (step >> 1), step & 1, n)
+            return carry
+
+        lax.fori_loop(0, 2 * len(columns) // unroll, body, 0)
+
+    @pl.when(where_ref[0] == 0)
+    def _():
+        run(for_up)
+
+    @pl.when(where_ref[0] == 1)
+    def _():
+        run(for_down)
+
+
 def enter_kernel(
     where_ref, codes_ref, a0, a1, a2, a3, w0, w1, w2, w3,
     acts, weights, sent, slope, picked, sems,
 ):
-    core = where_ref[0]
     for copy in load((a0, a1, a2, a3), (w0, w1, w2, w3), acts, weights, sems):
         copy.wait()
 
-    def body(step, carry):
-        d, r = step >> 1, step & 1
+    def for_up(d, r, n):
         at = column(where_ref, d, r)
+        pick(acts, picked.at[n], *spots(where_ref, codes_ref, d, r))
+        pre = jnp.dot(
+            picked[n], weights[d, r].reshape(8 * BLK, BLK), preferred_element_type=jnp.float32
+        )
+        square = pre * pre
+        t = jnp.tanh(pre * (GELU_SCALE + GELU_SCALE * GELU_CUBIC * square))
+        half = 0.5 + 0.5 * t
+        sent[at] = (pre * half).astype(jnp.bfloat16)
+        slope[at] = half + pre * (half - half * t) * (
+            GELU_SCALE + 3.0 * GELU_SCALE * GELU_CUBIC * square
+        )
+
+    def for_down(d, r, n):
+        at = column(where_ref, d, r)
+        pick(acts, picked.at[n], *spots(where_ref, codes_ref, d, r))
+        flat = jnp.concatenate([weights[d, r, s] for s in range(8)], axis=1)
+        sent[at] = lax.dot_general(
+            picked[n], flat, (((1,), (1,)), ((), ())), preferred_element_type=jnp.float32
+        ).astype(jnp.bfloat16)
+
+    per_core(where_ref, codes_ref, range(4), 4, for_up, for_down)
+
+
+def pulled(came, slope, row):
+    return (came[row].astype(jnp.float32) * slope[row]).astype(jnp.bfloat16)
+
+
+def sums_kernel(where_ref, codes_ref, weights, came, slope, o0, o1, o2, o3, acc):
+    acc[...] = jnp.zeros_like(acc)
+
+    def scatter(places, stride, s, product):
+        for n in range(2):
+            first, half, cols = places[s + n]
+            for q in range(RING):
+                at = first + q * stride
+                acc[at >> 2, at & 3, half, :, cols] += product[
+                    q * BLK : (q + 1) * BLK, n * BLK : (n + 1) * BLK
+                ]
+
+    def for_up(d, r, n):
+        mine = pulled(came, slope, column(where_ref, d, r))
         places, stride = spots(where_ref, codes_ref, d, r)
-        pick(acts, picked, places, stride)
-
-        @pl.when(core == 0)
-        def _():
-            pre = jnp.dot(
-                picked[...],
-                weights[d, r].reshape(8 * BLK, BLK),
-                preferred_element_type=jnp.float32,
+        for s in range(0, 8, 2):
+            pair = weights[d, r, s : s + 2].reshape(2 * BLK, BLK)
+            product = lax.dot_general(
+                mine, pair, (((1,), (1,)), ((), ())), preferred_element_type=jnp.float32
             )
-            t = jnp.tanh(GELU_SCALE * (pre + GELU_CUBIC * pre * pre * pre))
-            sent[at] = (0.5 * pre * (1.0 + t)).astype(jnp.bfloat16)
-            slope[at] = 0.5 * (1.0 + t) + 0.5 * pre * (1.0 - t * t) * GELU_SCALE * (
-                1.0 + 3.0 * GELU_CUBIC * pre * pre
-            )
-
-        @pl.when(core == 1)
-        def _():
-            flat = jnp.concatenate([weights[d, r, s] for s in range(8)], axis=1)
-            sent[at] = lax.dot_general(
-                picked[...], flat, (((1,), (1,)), ((), ())), preferred_element_type=jnp.float32
-            ).astype(jnp.bfloat16)
-
-        return carry
-
-    lax.fori_loop(0, 8, body, 0)
-
-
-def pulled(came, slope, step):
-    return (came[step].astype(jnp.float32) * slope[step]).astype(jnp.bfloat16)
-
-
-def sums_kernel(where_ref, codes_ref, weights, came, slope, o0, o1, o2, o3, acc):
-    core = where_ref[0]
-    acc[...] = jnp.zeros_like(acc)
-
-    def body(step, carry):
-        d, r = step >> 1, step & 1
-        row = column(where_ref, d, r)
+            scatter(places, stride, s, product)
+
+    def for_down(d, r, n):
+        mine = came[column(where_ref, d, r)]
         places, stride = spots(where_ref, codes_ref, d, r)
-
-        def scatter(s, product):
-            for n in range(2):
-                first, half, cols = places[s + n]
-                for q in range(RING):
-                    at = first + q * stride
-                    acc[at >> 2, at & 3, half, :, cols] += product[
-                        q * BLK : (q + 1) * BLK, n * BLK : (n + 1) * BLK
-                    ]
-
-        @pl.when(core == 0)
-        def _():
-            mine = pulled(came, slope, row)
-            for s in range(0, 8, 2):
-                pair = weights[d, r, s : s + 2].reshape(2 * BLK, BLK)
-                scatter(
-                    s,
-                    lax.dot_general(
-                        mine, pair, (((1,), (1,)), ((), ())), preferred_element_type=jnp.float32
-                    ),
-                )
-
-        @pl.when(core == 1)
-        def _():
-            mine = came[row]
-            for s in range(0, 8, 2):
-                pair = jnp.concatenate([weights[d, r, s], weights[d, r, s + 1]], axis=1)
-                scatter(s, jnp.dot(mine, pair, preferred_element_type=jnp.float32))
-
-        return carry
-
-    lax.fori_loop(0, 8, body, 0)
+        for s in range(0, 8, 2):
+            pair = jnp.concatenate([weights[d, r, s], weights[d, r, s + 1]], axis=1)
+            product = jnp.dot(mine, pair, preferred_element_type=jnp.float32)
+            scatter(places, stride, s, product)
+
+    per_core(where_ref, codes_ref, range(4), 4, for_up, for_down)
     for n, out in enumerate((o0, o1, o2, o3)):
         out[...] = acc[n].astype(jnp.bfloat16)
 
 
 def grads_kernel(slots, where_ref, codes_ref, acts, came, slope, *refs):
-    core = where_ref[0]
     picked = refs[-1]
     for d, grads in zip(slots, refs):
 
-        def body(r, carry):
-            row = column(where_ref, d, r)
-            places, stride = spots(where_ref, codes_ref, d, r)
-            pick(acts, picked, places, stride)
-
-            @pl.when(core == 0)
-            def _():
-                grad = lax.dot_general(
-                    picked[...],
-                    pulled(came, slope, row),
-                    (((0,), (0,)), ((), ())),
-                    preferred_element_type=jnp.float32,
-                )
-                grads[r] = grad.astype(jnp.bfloat16).reshape(8, BLK, BLK)
-
-            @pl.when(core == 1)
-            def _():
-                grad = lax.dot_general(
-                    came[row],
-                    picked[...],
-                    (((0,), (0,)), ((), ())),
-                    preferred_element_type=jnp.float32,
-                ).astype(jnp.bfloat16)
-                for s in range(8):
-                    grads[r, s] = grad[:, s * BLK : (s + 1) * BLK]
-
-            return carry
-
-        lax.fori_loop(0, 2, body, 0)
+        def for_up(d, r, n):
+            pick(acts, picked.at[n], *spots(where_ref, codes_ref, d, r))
+            mine = pulled(came, slope, column(where_ref, d, r))
+            grad = lax.dot_general(
+                picked[n], mine, (((0,), (0,)), ((), ())), preferred_element_type=jnp.float32
+            )
+            grads[r] = grad.astype(jnp.bfloat16).reshape(8, BLK, BLK)
+
+        def for_down(d, r, n):
+            pick(acts, picked.at[n], *spots(where_ref, codes_ref, d, r))
+            grad = lax.dot_general(
+                came[column(where_ref, d, r)],
+                picked[n],
+                (((0,), (0,)), ((), ())),
+                preferred_element_type=jnp.float32,
+            ).astype(jnp.bfloat16)
+            for s in range(8):
+                grads[r, s] = grad[:, s * BLK : (s + 1) * BLK]
+
+        per_core(where_ref, codes_ref, (d,), 2, for_up, for_down)
 
 
 SMEM = pl.BlockSpec(memory_space=pltpu.SMEM)
@@ -250,10 +243,10 @@
         in_specs=[SMEM, SMEM] + [ANY] * 8,
         out_specs=[VMEM] * 4,
         scratch_shapes=[
-            pltpu.VMEM((512, 8 * BLK), jnp.bfloat16),
+            pltpu.VMEM((4, 512, 8 * BLK), jnp.bfloat16),
             pltpu.SemaphoreType.DMA((8,)),
         ],
-        compiler_params=pltpu.CompilerParams(vmem_limit_bytes=16 << 20),
+        compiler_params=pltpu.CompilerParams(vmem_limit_bytes=10 << 20),
         cost_estimate=cost(1 << 30, 8 << 20),
         name="enter",
     )(where, codes, *acts, *weights)
@@ -266,7 +259,7 @@
         in_specs=[SMEM, SMEM] + [VMEM] * 3,
         out_specs=[VMEM] * 4,
         scratch_shapes=[pltpu.VMEM(ACTS, jnp.float32)],
-        compiler_params=pltpu.CompilerParams(vmem_limit_bytes=24 << 20),
+        compiler_params=pltpu.CompilerParams(vmem_limit_bytes=14 << 20),
         cost_estimate=cost(1 << 30, 8 << 20),
         name="sums",
     )(where, codes, weights, came, slope)
@@ -278,8 +271,8 @@
         out_shape=[GRAD] * len(slots),
         in_specs=[SMEM, SMEM] + [VMEM] * 3,
         out_specs=[VMEM] * len(slots),
-        scratch_shapes=[pltpu.VMEM((512, 8 * BLK), jnp.bfloat16)],
-        compiler_params=pltpu.CompilerParams(vmem_limit_bytes=16 << 20),
+        scratch_shapes=[pltpu.VMEM((2, 512, 8 * BLK), jnp.bfloat16)],
+        compiler_params=pltpu.CompilerParams(vmem_limit_bytes=10 << 20),
         cost_estimate=cost(1 << 29, 8 << 20),
         name="grads",
     )(where, codes, acts, came, slope)

time: 110 us -> 106 us (0.964)
  Pallas kernels: 22.5 us -> 16.1 us
  waiting for transfers between devices: 43.8 us -> 46 us
    pallas_call x1, Pallas kernels: 8.78 us -> 5.45 us  [enter(): pl.pallas_call(enter_kernel, out_shape=[jax.ShapeDtypeStruct(ACTS, jnp.bf...]
    ppermute x12, waiting for transfers between devices: 17.7 us -> 19.9 us  [mixed_shift(): return lax.ppermute(values, MIXED, mixed_pairs(step, first))]
    pallas_call x2, Pallas kernels: 6.61 us -> 4.53 us  [block_grads(): pl.pallas_call(functools.partial(grads_kernel, slots), out_shape=[GRAD] *...]
  transfers between devices with their start and end apart: 24 -> 24, of which waited for: 11 -> 11; matrix products, arithmetic and copies ran while one was open for 3% -> 3% of each run, Pallas kernels for 6% -> 4%
where the time goes in v5:
time: 106 us
  waiting for transfers between devices  46 us (43%)
  starting transfers between devices  38.1 us (36%)
  Pallas kernels  16.1 us (15%)
  other arithmetic  5.02 us (5%)
    ppermute x6, waiting for transfers between devices, z_shift(): return lax.ppermute(values, ('z', 'core'), pairs)  22.8 us
    ppermute x12, waiting for transfers between devices, mixed_shift(): return lax.ppermute(values, MIXED, mixed_pairs(step, first))  19.9 us
    ppermute x12, starting transfers between devices, mixed_shift(): return lax.ppermute(values, MIXED, mixed_pairs(step, first))  15.1 us
    ppermute x6, starting transfers between devices, z_shift(): return lax.ppermute(values, ('z', 'core'), pairs)  13.3 us
    ppermute x6, starting transfers between devices, swap(): return lax.ppermute(values, 'core', [(0, 1), (1, 0)])  9.71 us
    pallas_call x1, Pallas kernels, sums(): pl.pallas_call(sums_kernel, out_shape=[CHUNK] * 4, in_specs=[SMEM, SMEM]...  6.14 us
    pallas_call x1, Pallas kernels, enter(): pl.pallas_call(enter_kernel, out_shape=[jax.ShapeDtypeStruct(ACTS, jnp.bf...  5.45 us
    pallas_call x2, Pallas kernels, block_grads(): pl.pallas_call(functools.partial(grads_kernel, slots), out_shape=[GRAD] *...  4.53 us
  transfers between devices with their start and end apart: 24, of which 11 were waited for; matrix products, arithmetic and copies ran while one was open for 3% of the time, Pallas kernels for 4%

profile of v5, /device:TPU:1, one launch (start us, length us, event | category | flops | bytes accessed | tf_op | source)
XLA Modules:
  0.0 106.3 jit_solution(6864074391743276197)
XLA Ops:
  0.6 1.0 select_bitcast_fusion.3
  1.6 1.5 %collective-permute-start.1 = (bf16[128,512]{1,0:T(8,128)(2,1)S(1)}, bf16[128,512]{1,0:T(8,128)(2,1)S(1)}, u32[]{:S(2)}, u32[]{:S(2)}) collective-permute-start(bf16[128,512]{1,0:T(8,128)(2,1)S(1)} %get-tuple-element.40), channel_id=1, source_target_pairs={{0,1},{1,0},{2,3},{3,2},{4,5},{5,4},{6,7},{7,6},{8,9},{9,8},{10,11... | collective-permute-start | bytes 393224 | tf_op jit(solution)/shard_map/ppermute | solution.py:45
  3.1 1.1 %broadcast_select_fusion = (bf16[1,8,128,128]{3,2,1,0:T(8,128)(2,1)S(1)}, bf16[8,128,128]{2,1,0:T(8,128)(2,1)S(1)}) fusion(bf16[1,8,128,128]{3,2,1,0:T(8,128)(2,1)} %param.7, bf16[1,8,128,128]{3,2,1,0:T(8,128)(2,1)} %param.9, pred[]{:T(512)S(6)} %eq.3), kind=kLoop, calls=%fused_computation.18 | loop fusion | flops 262144 | bytes 1048577 | tf_op jit(solution)/shard_map/jit(_where)/select_n | solution.py:291
  4.2 0.0 copy-start
  4.2 0.0 copy-start.1
  4.2 0.1 collective-permute-start.8
  4.3 0.0 collective-permute-done.1
  4.4 3.1 %collective-permute-start.3 = (bf16[2,128,512]{2,1,0:T(8,128)(2,1)S(1)}, bf16[2,128,512]{2,1,0:T(8,128)(2,1)S(1)}, u32[]{:S(2)}, u32[]{:S(2)}) collective-permute-start(bf16[2,128,512]{2,1,0:T(8,128)(2,1)S(1)} %get-tuple-element.38), channel_id=1, source_target_pairs={{0,16},{1,5},{2,18},{3,7},{4,20},{5,1},{6,22},{7,3},{8,24},{9,13},... | collective-permute-start | bytes 786440 | tf_op jit(solution)/shard_map/ppermute | solution.py:35
  7.5 0.4 collective-permute-start.2
  7.9 2.3 %collective-permute-start.4 = (bf16[2,128,512]{2,1,0:T(8,128)(2,1)S(1)}, bf16[2,128,512]{2,1,0:T(8,128)(2,1)S(1)}, u32[]{:S(2)}, u32[]{:S(2)}) collective-permute-start(bf16[2,128,512]{2,1,0:T(8,128)(2,1)S(1)} %get-tuple-element.38), channel_id=1, source_target_pairs={{0,24},{1,7},{2,26},{3,1},{4,28},{5,3},{6,30},{7,5},{8,0},{9,15},{... | collective-permute-start | bytes 786440 | tf_op jit(solution)/shard_map/ppermute | solution.py:35
  10.1 0.0 collective-permute-done.8
  10.1 0.1 pad_maximum_fusion.1.w0
  10.2 1.7 %collective-permute-start.11 = (bf16[2,8,128,128]{3,2,1,0:T(8,128)(2,1)S(1)}, bf16[2,8,128,128]{3,2,1,0:T(8,128)(2,1)S(1)}, u32[]{:S(2)}, u32[]{:S(2)}) collective-permute-start(bf16[2,8,128,128]{3,2,1,0:T(8,128)(2,1)S(1)} %pad_maximum_fusion.1.w0), channel_id=1, source_target_pairs={{0,96},{32,0},{64,32},{96,64},{1,33},{33,65},{65,97},{97,1},{2,98}... | collective-permute-start | bytes 1572872 | tf_op jit(solution)/shard_map/ppermute | solution.py:41
  11.9 0.0 collective-permute-done.3
  11.9 2.4 %collective-permute-done.2 = bf16[2,128,512]{2,1,0:T(8,128)(2,1)S(1)} collective-permute-done((bf16[2,128,512]{2,1,0:T(8,128)(2,1)S(1)}, bf16[2,128,512]{2,1,0:T(8,128)(2,1)S(1)}, u32[]{:S(2)}, u32[]{:S(2)}) %collective-permute-start.2) | collective-permute-done | bytes 262176 | tf_op jit(solution)/shard_map/ppermute | solution.py:35
  14.3 0.4 collective-permute-done.4
  14.7 0.1 pad_maximum_fusion.a0
  14.8 2.5 %collective-permute-start.7 = (bf16[4,2,128,512]{3,2,1,0:T(8,128)(2,1)S(1)}, bf16[4,2,128,512]{3,2,1,0:T(8,128)(2,1)S(1)}, u32[]{:S(2)}, u32[]{:S(2)}) collective-permute-start(bf16[4,2,128,512]{3,2,1,0:T(8,128)(2,1)S(1)} %pad_maximum_fusion.a0), channel_id=1, source_target_pairs={{0,6},{1,25},{2,0},{3,27},{4,2},{5,29},{6,4},{7,31},{8,14},{9,1},{... | collective-permute-start | bytes 3145736 | tf_op jit(solution)/shard_map/ppermute | solution.py:35
  17.4 0.5 collective-permute-start.6
  17.9 0.6 collective-permute-start.5
  18.5 0.1 copy.10
  18.6 0.1 copy.11
  18.7 2.2 %collective-permute-start = (s32[4,8]{1,0:T(4,128)S(1)}, s32[4,8]{1,0:T(4,128)S(1)}, u32[]{:S(2)}, u32[]{:S(2)}) collective-permute-start(s32[4,8]{1,0:T(4,128)S(1)} %bitcast.58), channel_id=1, source_target_pairs={{0,1},{1,0},{2,3},{3,2},{4,5},{5,4},{6,7},{7,6},{8,9},{9,8},{10,11... | collective-permute-start | bytes 392 | tf_op jit(solution)/shard_map/ppermute | solution.py:45
  20.9 0.8 collective-permute-done
  21.7 3.6 %collective-permute-start.10 = (bf16[2,8,128,128]{3,2,1,0:T(8,128)(2,1)S(1)}, bf16[2,8,128,128]{3,2,1,0:T(8,128)(2,1)}, u32[]{:S(2)}, u32[]{:S(2)}) collective-permute-start(bf16[2,8,128,128]{3,2,1,0:T(8,128)(2,1)S(1)} %pad_maximum_fusion.1.w0), channel_id=1, source_target_pairs={{0,64},{32,96},{64,0},{96,32},{1,65},{33,97},{65,1},{97,33},{2,66}... | collective-permute-start | bytes 1572872 | tf_op jit(solution)/shard_map/ppermute | solution.py:41
  25.3 0.0 collective-permute-done.11.w3
  25.3 0.4 collective-permute-start.9
  25.7 0.1 pad_add_fusion.1.where_ref
  25.8 11.7 %collective-permute-done.10.w2 = bf16[2,8,128,128]{3,2,1,0:T(8,128)(2,1)} collective-permute-done((bf16[2,8,128,128]{3,2,1,0:T(8,128)(2,1)S(1)}, bf16[2,8,128,128]{3,2,1,0:T(8,128)(2,1)}, u32[]{:S(2)}, u32[]{:S(2)}) %collective-permute-start.10) | collective-permute-done | bytes 524320 | tf_op jit(solution)/shard_map/ppermute | solution.py:41
  37.5 6.8 %collective-permute-done.9.w1 = bf16[2,8,128,128]{3,2,1,0:T(8,128)(2,1)} collective-permute-done((bf16[2,8,128,128]{3,2,1,0:T(8,128)(2,1)S(1)}, bf16[2,8,128,128]{3,2,1,0:T(8,128)(2,1)}, u32[]{:S(2)}, u32[]{:S(2)}) %collective-permute-start.9) | collective-permute-done | bytes 524320 | tf_op jit(solution)/shard_map/ppermute | solution.py:41
  44.3 0.0 collective-permute-done.7.a3
  44.3 0.0 collective-permute-done.6.a2
  44.3 0.0 collective-permute-done.5.a1
  44.3 5.5 %enter.1 = (bf16[4,4,2,128,512]{4,3,2,1,0:T(8,128)(2,1)S(1)}, bf16[4,2,8,128,128]{4,3,2,1,0:T(8,128)(2,1)S(1)}, bf16[8,512,128]{2,1,0:T(8,128)(2,1)S(1)}, f32[8,512,128]{2,1,0:T(8,128)S(1)}) custom-call(s32[2]{0:T(128)S(1)} %pad_add_fusion.1.where_ref, s32[2,4,8]{2,1,0:T(4,128)S(1)} %and_add_fusion.codes_ref, ...), custom_call_target="tpu_custom_call" | custom-call | flops 1073741824 | bytes 8388608 | tf_op jit(solution)/shard_map/enter/pallas_call | solution.py:235
  49.7 3.2 %collective-permute-start.12 = (bf16[8,512,128]{2,1,0:T(8,128)(2,1)S(1)}, bf16[8,512,128]{2,1,0:T(8,128)(2,1)S(1)}, u32[]{:S(2)}, u32[]{:S(2)}) collective-permute-start(bf16[8,512,128]{2,1,0:T(8,128)(2,1)S(1)} %get-tuple-element.17), channel_id=1, source_target_pairs={{0,1},{1,0},{2,3},{3,2},{4,5},{5,4},{6,7},{7,6},{8,9},{9,8},{10,11... | collective-permute-start | bytes 3145736 | tf_op jit(solution)/shard_map/ppermute | solution.py:45
  52.9 2.3 %collective-permute-done.12.came = bf16[8,512,128]{2,1,0:T(8,128)(2,1)S(1)} collective-permute-done((bf16[8,512,128]{2,1,0:T(8,128)(2,1)S(1)}, bf16[8,512,128]{2,1,0:T(8,128)(2,1)S(1)}, u32[]{:S(2)}, u32[]{:S(2)}) %collective-permute-start.12) | collective-permute-done | bytes 1048608 | tf_op jit(solution)/shard_map/ppermute | solution.py:45
  55.2 6.1 %sums.1 = (bf16[4,2,128,512]{3,2,1,0:T(8,128)(2,1)S(1)}, bf16[4,2,128,512]{3,2,1,0:T(8,128)(2,1)S(1)}, bf16[4,2,128,512]{3,2,1,0:T(8,128)(2,1)S(1)}, bf16[4,2,128,512]{3,2,1,0:T(8,128)(2,1)S(1)}) custom-call(s32[2]{0:T(128)S(1)} %pad_add_fusion.1.where_ref, s32[2,4,8]{2,1,0:T(4,128)S(1)} %and_add_fusion.codes_ref, ...), custom_call_target="tpu_custom_call" | custom-call | flops 1073741824 | bytes 8388608 | tf_op jit(solution)/shard_map/sums/pallas_call | solution.py:256
  61.4 2.9 %collective-permute-start.13 = (bf16[4,2,128,512]{3,2,1,0:T(8,128)(2,1)S(1)}, bf16[4,2,128,512]{3,2,1,0:T(8,128)(2,1)S(1)}, u32[]{:S(2)}, u32[]{:S(2)}) collective-permute-start(bf16[4,2,128,512]{3,2,1,0:T(8,128)(2,1)S(1)} %get-tuple-element.20), channel_id=1, source_target_pairs={{0,6},{1,25},{2,0},{3,27},{4,2},{5,29},{6,4},{7,31},{8,14},{9,1},{... | collective-permute-start | bytes 3145736 | tf_op jit(solution)/shard_map/ppermute | solution.py:35
  64.3 1.3 %collective-permute-start.15 = (bf16[4,2,128,512]{3,2,1,0:T(8,128)(2,1)S(1)}, bf16[4,2,128,512]{3,2,1,0:T(8,128)(2,1)S(1)}, u32[]{:S(2)}, u32[]{:S(2)}) collective-permute-start(bf16[4,2,128,512]{3,2,1,0:T(8,128)(2,1)S(1)} %get-tuple-element.22), channel_id=1, source_target_pairs={{0,4},{1,17},{2,6},{3,19},{4,0},{5,21},{6,2},{7,23},{8,12},{9,25},... | collective-permute-start | bytes 3145736 | tf_op jit(solution)/shard_map/ppermute | solution.py:35
  65.5 2.3 %grads.3 = (bf16[2,8,128,128]{3,2,1,0:T(8,128)(2,1)S(1)}, bf16[2,8,128,128]{3,2,1,0:T(8,128)(2,1)S(1)}) custom-call(s32[2]{0:T(128)S(1)} %pad_add_fusion.1.where_ref, s32[2,4,8]{2,1,0:T(4,128)S(1)} %and_add_fusion.codes_ref, bf16[4,4,2,128,512]{4,3,2,1,0:T(8,128)(2,1)S(1)} %get-tuple-element.23.acts, bf16[8,512,128]{2,1,0:T(8,128)(2,1)S(1)} %collective-permute-done.12.came, ...), custom_call_target="tpu_custom_call" | custom-call | flops 536870912 | bytes 8388608 | tf_op jit(solution)/shard_map/grads/pallas_call | solution.py:269
  67.8 1.7 %collective-permute-start.20 = (bf16[2,8,128,128]{3,2,1,0:T(8,128)(2,1)S(1)}, bf16[2,8,128,128]{3,2,1,0:T(8,128)(2,1)S(1)}, u32[]{:S(2)}, u32[]{:S(2)}) collective-permute-start(bf16[2,8,128,128]{3,2,1,0:T(8,128)(2,1)S(1)} %get-tuple-element.25), channel_id=1, source_target_pairs={{0,96},{32,0},{64,32},{96,64},{1,33},{33,65},{65,97},{97,1},{2,98}... | collective-permute-start | bytes 1572872 | tf_op jit(solution)/shard_map/ppermute | solution.py:41
  69.5 2.2 %collective-permute-start.21 = (bf16[2,8,128,128]{3,2,1,0:T(8,128)(2,1)S(1)}, bf16[2,8,128,128]{3,2,1,0:T(8,128)(2,1)S(1)}, u32[]{:S(2)}, u32[]{:S(2)}) collective-permute-start(bf16[2,8,128,128]{3,2,1,0:T(8,128)(2,1)S(1)} %get-tuple-element.26), channel_id=1, source_target_pairs={{0,32},{32,64},{64,96},{96,0},{1,97},{33,1},{65,33},{97,65},{2,34}... | collective-permute-start | bytes 1572872 | tf_op jit(solution)/shard_map/ppermute | solution.py:41
  71.8 2.3 %grads.2 = (bf16[2,8,128,128]{3,2,1,0:T(8,128)(2,1)S(1)}, bf16[2,8,128,128]{3,2,1,0:T(8,128)(2,1)S(1)}) custom-call(s32[2]{0:T(128)S(1)} %pad_add_fusion.1.where_ref, s32[2,4,8]{2,1,0:T(4,128)S(1)} %and_add_fusion.codes_ref, bf16[4,4,2,128,512]{4,3,2,1,0:T(8,128)(2,1)S(1)} %get-tuple-element.23.acts, bf16[8,512,128]{2,1,0:T(8,128)(2,1)S(1)} %collective-permute-done.12.came, ...), custom_call_target="tpu_custom_call" | custom-call | flops 536870912 | bytes 8388608 | tf_op jit(solution)/shard_map/grads/pallas_call | solution.py:269
  74.0 13.2 %collective-permute-done.13 = bf16[4,2,128,512]{3,2,1,0:T(8,128)(2,1)S(1)} collective-permute-done((bf16[4,2,128,512]{3,2,1,0:T(8,128)(2,1)S(1)}, bf16[4,2,128,512]{3,2,1,0:T(8,128)(2,1)S(1)}, u32[]{:S(2)}, u32[]{:S(2)}) %collective-permute-start.13) | collective-permute-done | bytes 1048608 | tf_op jit(solution)/shard_map/ppermute | solution.py:35
  87.2 3.6 %collective-permute-start.22 = (bf16[2,8,128,128]{3,2,1,0:T(8,128)(2,1)S(1)}, bf16[2,8,128,128]{3,2,1,0:T(8,128)(2,1)S(1)}, u32[]{:S(2)}, u32[]{:S(2)}) collective-permute-start(bf16[2,8,128,128]{3,2,1,0:T(8,128)(2,1)S(1)} %get-tuple-element.27), channel_id=1, source_target_pairs={{0,64},{32,96},{64,0},{96,32},{1,65},{33,97},{65,1},{97,33},{2,66}... | collective-permute-start | bytes 1572872 | tf_op jit(solution)/shard_map/ppermute | solution.py:41
  90.8 0.0 collective-permute-done.14
  90.8 0.0 collective-permute-done.15
  90.8 0.6 add_convert_fusion
  91.4 0.1 slice_bitcast_fusion.4
  91.5 0.4 collective-permute-start.16
  91.9 0.4 collective-permute-start.18
  92.3 0.7 collective-permute-start.17
  93.1 0.0 collective-permute-done.21
  93.1 4.3 %collective-permute-done.22 = bf16[2,8,128,128]{3,2,1,0:T(8,128)(2,1)S(1)} collective-permute-done((bf16[2,8,128,128]{3,2,1,0:T(8,128)(2,1)S(1)}, bf16[2,8,128,128]{3,2,1,0:T(8,128)(2,1)S(1)}, u32[]{:S(2)}, u32[]{:S(2)}) %collective-permute-start.22) | collective-permute-done | bytes 524320 | tf_op jit(solution)/shard_map/ppermute | solution.py:41
  97.4 0.3 multiply_convert_fusion
  97.8 0.1 collective-permute-start.23
  97.9 0.0 collective-permute-done.16
  97.9 1.1 %collective-permute-done.18 = bf16[2,128,512]{2,1,0:T(8,128)(2,1)S(1)} collective-permute-done((bf16[2,128,512]{2,1,0:T(8,128)(2,1)S(1)}, bf16[2,128,512]{2,1,0:T(8,128)(2,1)S(1)}, u32[]{:S(2)}, u32[]{:S(2)}) %collective-permute-start.18) | collective-permute-done | bytes 262176 | tf_op jit(solution)/shard_map/ppermute | solution.py:35
  99.0 2.8 %collective-permute-done.17 = bf16[2,128,512]{2,1,0:T(8,128)(2,1)S(1)} collective-permute-done((bf16[2,128,512]{2,1,0:T(8,128)(2,1)S(1)}, bf16[2,128,512]{2,1,0:T(8,128)(2,1)S(1)}, u32[]{:S(2)}, u32[]{:S(2)}) %collective-permute-start.17) | collective-permute-done | bytes 262176 | tf_op jit(solution)/shard_map/ppermute | solution.py:35
  101.8 0.1 fusion.2
  101.9 2.7 %collective-permute-start.19 = (bf16[128,512]{1,0:T(8,128)(2,1)S(1)}, bf16[128,512]{1,0:T(8,128)(2,1)S(1)}, u32[]{:S(2)}, u32[]{:S(2)}) collective-permute-start(bf16[128,512]{1,0:T(8,128)(2,1)S(1)} %slice_bitcast_fusion.7), channel_id=1, source_target_pairs={{0,1},{1,0},{2,3},{3,2},{4,5},{5,4},{6,7},{7,6},{8,9},{9,8},{10,11... | collective-permute-start | bytes 393224 | tf_op jit(solution)/shard_map/ppermute | solution.py:45
  104.6 0.9 select_bitcast_fusion
  105.4 0.1 collective-permute-done.19
  105.6 0.7 broadcast_select_fusion.1
  (10 shorter events, 0.1 us)
Async XLA Ops:
  1.6 2.7 %collective-permute-start.1 = (bf16[128,512]{1,0:T(8,128)(2,1)S(1)}, bf16[128,512]{1,0:T(8,128)(2,1)S(1)}, u32[]{:S(2)}, u32[]{:S(2)}) collective-permute-start(bf16[128,512]{1,0:T(8,128)(2,1)S(1)} %get-tuple-element.40), channel_id=1, source_target_pairs={{0,1},{1,0},{2,3},{3,2},{4,5},{5,4},{6,7},{7,6},{8,9},{9,8},{10,11... | collective-permute-start | bytes 393224 | tf_op jit(solution)/shard_map/ppermute | solution.py:45
  4.2 14.3 %copy-start = (s32[16,8]{0,1:T(8,128)S(1)}, s32[16,8]{0,1:T(8,128)}, u32[]{:S(2)}) copy-start(s32[16,8]{0,1:T(8,128)} %param.8) | copy-start | bytes 1540
  4.2 14.4 %copy-start.1 = (s32[16,8]{0,1:T(8,128)S(1)}, s32[16,8]{0,1:T(8,128)}, u32[]{:S(2)}) copy-start(s32[16,8]{0,1:T(8,128)} %param.10) | copy-start | bytes 1540
  4.2 5.9 %collective-permute-start.8 = (bf16[8,128,128]{2,1,0:T(8,128)(2,1)S(1)}, bf16[8,128,128]{2,1,0:T(8,128)(2,1)S(1)}, u32[]{:S(2)}, u32[]{:S(2)}) collective-permute-start(bf16[8,128,128]{2,1,0:T(8,128)(2,1)S(1)} %get-tuple-element.34), channel_id=1, source_target_pairs={{0,1},{1,0},{2,3},{3,2},{4,5},{5,4},{6,7},{7,6},{8,9},{9,8},{10,11... | collective-permute-start | bytes 786440 | tf_op jit(solution)/shard_map/ppermute | solution.py:45
  4.4 7.5 %collective-permute-start.3 = (bf16[2,128,512]{2,1,0:T(8,128)(2,1)S(1)}, bf16[2,128,512]{2,1,0:T(8,128)(2,1)S(1)}, u32[]{:S(2)}, u32[]{:S(2)}) collective-permute-start(bf16[2,128,512]{2,1,0:T(8,128)(2,1)S(1)} %get-tuple-element.38), channel_id=1, source_target_pairs={{0,16},{1,5},{2,18},{3,7},{4,20},{5,1},{6,22},{7,3},{8,24},{9,13},... | collective-permute-start | bytes 786440 | tf_op jit(solution)/shard_map/ppermute | solution.py:35
  7.5 6.9 %collective-permute-start.2 = (bf16[2,128,512]{2,1,0:T(8,128)(2,1)S(1)}, bf16[2,128,512]{2,1,0:T(8,128)(2,1)S(1)}, u32[]{:S(2)}, u32[]{:S(2)}) collective-permute-start(bf16[2,128,512]{2,1,0:T(8,128)(2,1)S(1)} %get-tuple-element.38), channel_id=1, source_target_pairs={{0,8},{1,3},{2,10},{3,5},{4,12},{5,7},{6,14},{7,1},{8,16},{9,11},{... | collective-permute-start | bytes 786440 | tf_op jit(solution)/shard_map/ppermute | solution.py:35
  7.9 6.9 %collective-permute-start.4 = (bf16[2,128,512]{2,1,0:T(8,128)(2,1)S(1)}, bf16[2,128,512]{2,1,0:T(8,128)(2,1)S(1)}, u32[]{:S(2)}, u32[]{:S(2)}) collective-permute-start(bf16[2,128,512]{2,1,0:T(8,128)(2,1)S(1)} %get-tuple-element.38), channel_id=1, source_target_pairs={{0,24},{1,7},{2,26},{3,1},{4,28},{5,3},{6,30},{7,5},{8,0},{9,15},{... | collective-permute-start | bytes 786440 | tf_op jit(solution)/shard_map/ppermute | solution.py:35
  10.2 15.1 %collective-permute-start.11 = (bf16[2,8,128,128]{3,2,1,0:T(8,128)(2,1)S(1)}, bf16[2,8,128,128]{3,2,1,0:T(8,128)(2,1)S(1)}, u32[]{:S(2)}, u32[]{:S(2)}) collective-permute-start(bf16[2,8,128,128]{3,2,1,0:T(8,128)(2,1)S(1)} %pad_maximum_fusion.1.w0), channel_id=1, source_target_pairs={{0,96},{32,0},{64,32},{96,64},{1,33},{33,65},{65,97},{97,1},{2,98}... | collective-permute-start | bytes 1572872 | tf_op jit(solution)/shard_map/ppermute | solution.py:41
  14.8 29.4 %collective-permute-start.7 = (bf16[4,2,128,512]{3,2,1,0:T(8,128)(2,1)S(1)}, bf16[4,2,128,512]{3,2,1,0:T(8,128)(2,1)S(1)}, u32[]{:S(2)}, u32[]{:S(2)}) collective-permute-start(bf16[4,2,128,512]{3,2,1,0:T(8,128)(2,1)S(1)} %pad_maximum_fusion.a0), channel_id=1, source_target_pairs={{0,6},{1,25},{2,0},{3,27},{4,2},{5,29},{6,4},{7,31},{8,14},{9,1},{... | collective-permute-start | bytes 3145736 | tf_op jit(solution)/shard_map/ppermute | solution.py:35
  17.4 26.9 %collective-permute-start.6 = (bf16[4,2,128,512]{3,2,1,0:T(8,128)(2,1)S(1)}, bf16[4,2,128,512]{3,2,1,0:T(8,128)(2,1)}, u32[]{:S(2)}, u32[]{:S(2)}) collective-permute-start(bf16[4,2,128,512]{3,2,1,0:T(8,128)(2,1)S(1)} %pad_maximum_fusion.a0), channel_id=1, source_target_pairs={{0,4},{1,17},{2,6},{3,19},{4,0},{5,21},{6,2},{7,23},{8,12},{9,25},... | collective-permute-start | bytes 3145736 | tf_op jit(solution)/shard_map/ppermute | solution.py:35
  17.9 26.4 %collective-permute-start.5 = (bf16[4,2,128,512]{3,2,1,0:T(8,128)(2,1)S(1)}, bf16[4,2,128,512]{3,2,1,0:T(8,128)(2,1)}, u32[]{:S(2)}, u32[]{:S(2)}) collective-permute-start(bf16[4,2,128,512]{3,2,1,0:T(8,128)(2,1)S(1)} %pad_maximum_fusion.a0), channel_id=1, source_target_pairs={{0,2},{1,9},{2,4},{3,11},{4,6},{5,13},{6,0},{7,15},{8,10},{9,17},{... | collective-permute-start | bytes 3145736 | tf_op jit(solution)/shard_map/ppermute | solution.py:35
  18.7 3.0 %collective-permute-start = (s32[4,8]{1,0:T(4,128)S(1)}, s32[4,8]{1,0:T(4,128)S(1)}, u32[]{:S(2)}, u32[]{:S(2)}) collective-permute-start(s32[4,8]{1,0:T(4,128)S(1)} %bitcast.58), channel_id=1, source_target_pairs={{0,1},{1,0},{2,3},{3,2},{4,5},{5,4},{6,7},{7,6},{8,9},{9,8},{10,11... | collective-permute-start | bytes 392 | tf_op jit(solution)/shard_map/ppermute | solution.py:45
  21.7 15.8 %collective-permute-start.10 = (bf16[2,8,128,128]{3,2,1,0:T(8,128)(2,1)S(1)}, bf16[2,8,128,128]{3,2,1,0:T(8,128)(2,1)}, u32[]{:S(2)}, u32[]{:S(2)}) collective-permute-start(bf16[2,8,128,128]{3,2,1,0:T(8,128)(2,1)S(1)} %pad_maximum_fusion.1.w0), channel_id=1, source_target_pairs={{0,64},{32,96},{64,0},{96,32},{1,65},{33,97},{65,1},{97,33},{2,66}... | collective-permute-start | bytes 1572872 | tf_op jit(solution)/shard_map/ppermute | solution.py:41
  25.3 19.0 %collective-permute-start.9 = (bf16[2,8,128,128]{3,2,1,0:T(8,128)(2,1)S(1)}, bf16[2,8,128,128]{3,2,1,0:T(8,128)(2,1)}, u32[]{:S(2)}, u32[]{:S(2)}) collective-permute-start(bf16[2,8,128,128]{3,2,1,0:T(8,128)(2,1)S(1)} %pad_maximum_fusion.1.w0), channel_id=1, source_target_pairs={{0,32},{32,64},{64,96},{96,0},{1,97},{33,1},{65,33},{97,65},{2,34}... | collective-permute-start | bytes 1572872 | tf_op jit(solution)/shard_map/ppermute | solution.py:41
  49.7 5.5 %collective-permute-start.12 = (bf16[8,512,128]{2,1,0:T(8,128)(2,1)S(1)}, bf16[8,512,128]{2,1,0:T(8,128)(2,1)S(1)}, u32[]{:S(2)}, u32[]{:S(2)}) collective-permute-start(bf16[8,512,128]{2,1,0:T(8,128)(2,1)S(1)} %get-tuple-element.17), channel_id=1, source_target_pairs={{0,1},{1,0},{2,3},{3,2},{4,5},{5,4},{6,7},{7,6},{8,9},{9,8},{10,11... | collective-permute-start | bytes 3145736 | tf_op jit(solution)/shard_map/ppermute | solution.py:45
  61.4 25.9 %collective-permute-start.13 = (bf16[4,2,128,512]{3,2,1,0:T(8,128)(2,1)S(1)}, bf16[4,2,128,512]{3,2,1,0:T(8,128)(2,1)S(1)}, u32[]{:S(2)}, u32[]{:S(2)}) collective-permute-start(bf16[4,2,128,512]{3,2,1,0:T(8,128)(2,1)S(1)} %get-tuple-element.20), channel_id=1, source_target_pairs={{0,6},{1,25},{2,0},{3,27},{4,2},{5,29},{6,4},{7,31},{8,14},{9,1},{... | collective-permute-start | bytes 3145736 | tf_op jit(solution)/shard_map/ppermute | solution.py:35
  64.3 26.6 %collective-permute-start.14 = (bf16[4,2,128,512]{3,2,1,0:T(8,128)(2,1)S(1)}, bf16[4,2,128,512]{3,2,1,0:T(8,128)(2,1)S(1)}, u32[]{:S(2)}, u32[]{:S(2)}) collective-permute-start(bf16[4,2,128,512]{3,2,1,0:T(8,128)(2,1)S(1)} %get-tuple-element.21), channel_id=1, source_target_pairs={{0,2},{1,9},{2,4},{3,11},{4,6},{5,13},{6,0},{7,15},{8,10},{9,17},{... | collective-permute-start | bytes 3145736 | tf_op jit(solution)/shard_map/ppermute | solution.py:35
  64.3 26.6 %collective-permute-start.15 = (bf16[4,2,128,512]{3,2,1,0:T(8,128)(2,1)S(1)}, bf16[4,2,128,512]{3,2,1,0:T(8,128)(2,1)S(1)}, u32[]{:S(2)}, u32[]{:S(2)}) collective-permute-start(bf16[4,2,128,512]{3,2,1,0:T(8,128)(2,1)S(1)} %get-tuple-element.22), channel_id=1, source_target_pairs={{0,4},{1,17},{2,6},{3,19},{4,0},{5,21},{6,2},{7,23},{8,12},{9,25},... | collective-permute-start | bytes 3145736 | tf_op jit(solution)/shard_map/ppermute | solution.py:35
  67.8 24.5 %collective-permute-start.20 = (bf16[2,8,128,128]{3,2,1,0:T(8,128)(2,1)S(1)}, bf16[2,8,128,128]{3,2,1,0:T(8,128)(2,1)S(1)}, u32[]{:S(2)}, u32[]{:S(2)}) collective-permute-start(bf16[2,8,128,128]{3,2,1,0:T(8,128)(2,1)S(1)} %get-tuple-element.25), channel_id=1, source_target_pairs={{0,96},{32,0},{64,32},{96,64},{1,33},{33,65},{65,97},{97,1},{2,98}... | collective-permute-start | bytes 1572872 | tf_op jit(solution)/shard_map/ppermute | solution.py:41
  69.5 23.5 %collective-permute-start.21 = (bf16[2,8,128,128]{3,2,1,0:T(8,128)(2,1)S(1)}, bf16[2,8,128,128]{3,2,1,0:T(8,128)(2,1)S(1)}, u32[]{:S(2)}, u32[]{:S(2)}) collective-permute-start(bf16[2,8,128,128]{3,2,1,0:T(8,128)(2,1)S(1)} %get-tuple-element.26), channel_id=1, source_target_pairs={{0,32},{32,64},{64,96},{96,0},{1,97},{33,1},{65,33},{97,65},{2,34}... | collective-permute-start | bytes 1572872 | tf_op jit(solution)/shard_map/ppermute | solution.py:41
  87.2 10.2 %collective-permute-start.22 = (bf16[2,8,128,128]{3,2,1,0:T(8,128)(2,1)S(1)}, bf16[2,8,128,128]{3,2,1,0:T(8,128)(2,1)S(1)}, u32[]{:S(2)}, u32[]{:S(2)}) collective-permute-start(bf16[2,8,128,128]{3,2,1,0:T(8,128)(2,1)S(1)} %get-tuple-element.27), channel_id=1, source_target_pairs={{0,64},{32,96},{64,0},{96,32},{1,65},{33,97},{65,1},{97,33},{2,66}... | collective-permute-start | bytes 1572872 | tf_op jit(solution)/shard_map/ppermute | solution.py:41
  91.5 6.4 %collective-permute-start.16 = (bf16[2,128,512]{2,1,0:T(8,128)(2,1)S(1)}, bf16[2,128,512]{2,1,0:T(8,128)(2,1)S(1)}, u32[]{:S(2)}, u32[]{:S(2)}) collective-permute-start(bf16[2,128,512]{2,1,0:T(8,128)(2,1)S(1)} %get-tuple-element.28), channel_id=1, source_target_pairs={{0,24},{1,7},{2,26},{3,1},{4,28},{5,3},{6,30},{7,5},{8,0},{9,15},{... | collective-permute-start | bytes 786440 | tf_op jit(solution)/shard_map/ppermute | solution.py:35
  91.9 7.1 %collective-permute-start.18 = (bf16[2,128,512]{2,1,0:T(8,128)(2,1)S(1)}, bf16[2,128,512]{2,1,0:T(8,128)(2,1)S(1)}, u32[]{:S(2)}, u32[]{:S(2)}) collective-permute-start(bf16[2,128,512]{2,1,0:T(8,128)(2,1)S(1)} %get-tuple-element.29), channel_id=1, source_target_pairs={{0,16},{1,5},{2,18},{3,7},{4,20},{5,1},{6,22},{7,3},{8,24},{9,13},... | collective-permute-start | bytes 786440 | tf_op jit(solution)/shard_map/ppermute | solution.py:35
  92.3 9.4 %collective-permute-start.17 = (bf16[2,128,512]{2,1,0:T(8,128)(2,1)S(1)}, bf16[2,128,512]{2,1,0:T(8,128)(2,1)S(1)}, u32[]{:S(2)}, u32[]{:S(2)}) collective-permute-start(bf16[2,128,512]{2,1,0:T(8,128)(2,1)S(1)} %get-tuple-element.30), channel_id=1, source_target_pairs={{0,8},{1,3},{2,10},{3,5},{4,12},{5,7},{6,14},{7,1},{8,16},{9,11},{... | collective-permute-start | bytes 786440 | tf_op jit(solution)/shard_map/ppermute | solution.py:35
  97.8 6.8 %collective-permute-start.23 = (bf16[8,128,128]{2,1,0:T(8,128)(2,1)S(1)}, bf16[8,128,128]{2,1,0:T(8,128)(2,1)S(1)}, u32[]{:S(2)}, u32[]{:S(2)}) collective-permute-start(bf16[8,128,128]{2,1,0:T(8,128)(2,1)S(1)} %slice_bitcast_fusion), channel_id=1, source_target_pairs={{0,1},{1,0},{2,3},{3,2},{4,5},{5,4},{6,7},{7,6},{8,9},{9,8},{10,11... | collective-permute-start | bytes 786440 | tf_op jit(solution)/shard_map/ppermute | solution.py:45
  101.9 3.6 %collective-permute-start.19 = (bf16[128,512]{1,0:T(8,128)(2,1)S(1)}, bf16[128,512]{1,0:T(8,128)(2,1)S(1)}, u32[]{:S(2)}, u32[]{:S(2)}) collective-permute-start(bf16[128,512]{1,0:T(8,128)(2,1)S(1)} %slice_bitcast_fusion.7), channel_id=1, source_target_pairs={{0,1},{1,0},{2,3},{3,2},{4,5},{5,4},{6,7},{7,6},{8,9},{9,8},{10,11... | collective-permute-start | bytes 393224 | tf_op jit(solution)/shard_map/ppermute | solution.py:45

commit v6 on v5

--- a/solution.py
+++ b/solution.py
@@ -52,9 +52,9 @@
     return [slots[step] for step in range(RING)]
 
 
-def reduce(chunks, shift):
+def reduce(chunks, shift, steps=STEPS):
     parts = [chunks[0]]
-    for step in STEPS:
+    for step in steps:
         parts.append(shift(chunks[step], RING - step))
     return sum(part.astype(jnp.float32) for part in parts)
 
@@ -120,9 +120,11 @@
 
 def enter_kernel(
     where_ref, codes_ref, a0, a1, a2, a3, w0, w1, w2, w3,
-    acts, weights, sent, slope, picked, sems,
+    acts, weights, sent, slope, acc, picked, sems,
 ):
-    for copy in load((a0, a1, a2, a3), (w0, w1, w2, w3), acts, weights, sems):
+    copies = load((a0, a1, a2, a3), (w0, w1, w2, w3), acts, weights, sems)
+    acc[...] = jnp.zeros_like(acc)
+    for copy in copies:
         copy.wait()
 
     def for_up(d, r, n):
@@ -154,9 +156,7 @@
     return (came[row].astype(jnp.float32) * slope[row]).astype(jnp.bfloat16)
 
 
-def sums_kernel(where_ref, codes_ref, weights, came, slope, o0, o1, o2, o3, acc):
-    acc[...] = jnp.zeros_like(acc)
-
+def sums_kernel(where_ref, codes_ref, weights, came, slope, zeros, acc, o0, o1, o2, o3):
     def scatter(places, stride, s, product):
         for n in range(2):
             first, half, cols = places[s + n]
@@ -239,9 +239,10 @@
             jax.ShapeDtypeStruct(WEIGHTS, jnp.bfloat16),
             jax.ShapeDtypeStruct(HIDDEN, jnp.bfloat16),
             jax.ShapeDtypeStruct(HIDDEN, jnp.float32),
+            jax.ShapeDtypeStruct(ACTS, jnp.float32),
         ],
         in_specs=[SMEM, SMEM] + [ANY] * 8,
-        out_specs=[VMEM] * 4,
+        out_specs=[VMEM] * 5,
         scratch_shapes=[
             pltpu.VMEM((4, 512, 8 * BLK), jnp.bfloat16),
             pltpu.SemaphoreType.DMA((8,)),
@@ -252,17 +253,17 @@
     )(where, codes, *acts, *weights)
 
 
-def sums(where, codes, weights, came, slope):
+def sums(where, codes, weights, came, slope, zeros):
     return pl.pallas_call(
         sums_kernel,
-        out_shape=[CHUNK] * 4,
-        in_specs=[SMEM, SMEM] + [VMEM] * 3,
-        out_specs=[VMEM] * 4,
-        scratch_shapes=[pltpu.VMEM(ACTS, jnp.float32)],
+        out_shape=[jax.ShapeDtypeStruct(ACTS, jnp.float32)] + [CHUNK] * 4,
+        in_specs=[SMEM, SMEM] + [VMEM] * 4,
+        out_specs=[VMEM] * 5,
+        input_output_aliases={5: 0},
         compiler_params=pltpu.CompilerParams(vmem_limit_bytes=14 << 20),
         cost_estimate=cost(1 << 30, 8 << 20),
         name="sums",
-    )(where, codes, weights, came, slope)
+    )(where, codes, weights, came, slope, zeros)[1:]
 
 
 def block_grads(slots, where, codes, acts, came, slope):
@@ -300,23 +301,23 @@
     acts = gather(jnp.stack(gather(acts, first(True))), first(False))
     weights = gather(weights, z_shift)
 
-    acts, weights, sent, slope = enter(where, codes, acts, weights)
+    acts, weights, sent, slope, zeros = enter(where, codes, acts, weights)
     came = swap(sent)
-    chunks = sums(where, codes, weights, came, slope)
-    grads_1, grads_3 = block_grads((1, 3), where, codes, acts, came, slope)
-    grads_2, grads_0 = block_grads((2, 0), where, codes, acts, came, slope)
+    chunks = sums(where, codes, weights, came, slope, zeros)
+    grads_2, grads_1 = block_grads((2, 1), where, codes, acts, came, slope)
+    grads_3, grads_0 = block_grads((3, 0), where, codes, acts, came, slope)
     grads = [grads_0, grads_1, grads_2, grads_3]
 
     summed = reduce(chunks, first(False)).astype(jnp.bfloat16)
     final = reduce([summed[n] for n in range(RING)], first(True)).astype(jnp.bfloat16)
     grad_scale = 1.0 / math.sqrt(tokens.shape[0] * lax.axis_size("z") * lax.axis_size("x"))
-    scaled = (reduce(grads, z_shift) * grad_scale).astype(jnp.bfloat16)
+    scaled = (reduce(grads, z_shift, (2, 1, 3)) * grad_scale).astype(jnp.bfloat16)
+    came_grad = swap(scaled[1])
+    grad_up = jnp.where(up, scaled[0], came_grad)
+    grad_down = jnp.where(up, came_grad, scaled[0])
     came_act = swap(final[1])
-    came_grad = swap(scaled[1])
     layer_out = jnp.where(up, came_act, final[0])
     grad_tokens = jnp.where(up, final[0], came_act)
-    grad_up = jnp.where(up, scaled[0], came_grad)
-    grad_down = jnp.where(up, came_grad, scaled[0])
     return (layer_out, grad_tokens, grad_up[None], grad_down[None])
 
 

time: 106 us -> 105 us (level)
  waiting for transfers between devices: 46 us -> 37.9 us
  starting transfers between devices: 38.1 us -> 45.5 us
    ppermute x6, waiting for transfers between devices: 22.8 us -> 12.4 us  [z_shift(): return lax.ppermute(values, ('z', 'core'), pairs)]
    ppermute x12, starting transfers between devices: 15.1 us -> 18.3 us  [mixed_shift(): return lax.ppermute(values, MIXED, mixed_pairs(step, first))]
    ppermute x6, starting transfers between devices: 13.3 us -> 15.6 us  [z_shift(): return lax.ppermute(values, ('z', 'core'), pairs)]
    ppermute x12, waiting for transfers between devices: 19.9 us -> 22.3 us  [mixed_shift(): return lax.ppermute(values, MIXED, mixed_pairs(step, first))]
    ppermute x6, starting transfers between devices: 9.71 us -> 11.6 us  [swap(): return lax.ppermute(values, 'core', [(0, 1), (1, 0)])]
  transfers between devices with their start and end apart: 24 -> 24, of which waited for: 11 -> 10; matrix products, arithmetic and copies ran while one was open for 3% -> 3% of each run, Pallas kernels for 4% -> 4%
where the time goes in v6:
time: 105 us
  starting transfers between devices  45.5 us (43%)
  waiting for transfers between devices  37.9 us (36%)
  Pallas kernels  15.6 us (15%)
  other arithmetic  5 us (5%)
    ppermute x12, waiting for transfers between devices, mixed_shift(): return lax.ppermute(values, MIXED, mixed_pairs(step, first))  22.3 us
    ppermute x12, starting transfers between devices, mixed_shift(): return lax.ppermute(values, MIXED, mixed_pairs(step, first))  18.3 us
    ppermute x6, starting transfers between devices, z_shift(): return lax.ppermute(values, ('z', 'core'), pairs)  15.6 us
    ppermute x6, waiting for transfers between devices, z_shift(): return lax.ppermute(values, ('z', 'core'), pairs)  12.4 us
    ppermute x6, starting transfers between devices, swap(): return lax.ppermute(values, 'core', [(0, 1), (1, 0)])  11.6 us
    pallas_call x1, Pallas kernels, sums(): pl.pallas_call(sums_kernel, out_shape=[jax.ShapeDtypeStruct(ACTS, jnp.flo...  5.58 us
    pallas_call x1, Pallas kernels, enter(): pl.pallas_call(enter_kernel, out_shape=[jax.ShapeDtypeStruct(ACTS, jnp.bf...  5.49 us
    pallas_call x2, Pallas kernels, block_grads(): pl.pallas_call(functools.partial(grads_kernel, slots), out_shape=[GRAD] *...  4.51 us
  transfers between devices with their start and end apart: 24, of which 10 were waited for; matrix products, arithmetic and copies ran while one was open for 3% of the time, Pallas kernels for 4%

profile of v6, /device:TPU:1, one launch (start us, length us, event | category | flops | bytes accessed | tf_op | source)
XLA Modules:
  0.0 105.1 jit_solution(6408800365892618636)
XLA Ops:
  0.6 1.0 select_bitcast_fusion.3
  1.6 1.5 %collective-permute-start.1 = (bf16[128,512]{1,0:T(8,128)(2,1)S(1)}, bf16[128,512]{1,0:T(8,128)(2,1)S(1)}, u32[]{:S(2)}, u32[]{:S(2)}) collective-permute-start(bf16[128,512]{1,0:T(8,128)(2,1)S(1)} %get-tuple-element.42), channel_id=1, source_target_pairs={{0,1},{1,0},{2,3},{3,2},{4,5},{5,4},{6,7},{7,6},{8,9},{9,8},{10,11... | collective-permute-start | bytes 393224 | tf_op jit(solution)/shard_map/ppermute | solution.py:45
  3.1 1.1 %broadcast_select_fusion = (bf16[1,8,128,128]{3,2,1,0:T(8,128)(2,1)S(1)}, bf16[8,128,128]{2,1,0:T(8,128)(2,1)S(1)}) fusion(bf16[1,8,128,128]{3,2,1,0:T(8,128)(2,1)} %param.7, bf16[1,8,128,128]{3,2,1,0:T(8,128)(2,1)} %param.9, pred[]{:T(512)S(6)} %eq.3), kind=kLoop, calls=%fused_computation.18 | loop fusion | flops 262144 | bytes 1048577 | tf_op jit(solution)/shard_map/jit(_where)/select_n | solution.py:292
  4.2 0.0 copy-start
  4.2 0.0 copy-start.1
  4.2 0.1 collective-permute-start.8
  4.3 0.0 collective-permute-done.1
  4.4 1.4 %collective-permute-start.2 = (bf16[2,128,512]{2,1,0:T(8,128)(2,1)S(1)}, bf16[2,128,512]{2,1,0:T(8,128)(2,1)S(1)}, u32[]{:S(2)}, u32[]{:S(2)}) collective-permute-start(bf16[2,128,512]{2,1,0:T(8,128)(2,1)S(1)} %get-tuple-element.40), channel_id=1, source_target_pairs={{0,8},{1,3},{2,10},{3,5},{4,12},{5,7},{6,14},{7,1},{8,16},{9,11},{... | collective-permute-start | bytes 786440 | tf_op jit(solution)/shard_map/ppermute | solution.py:35
  5.8 2.6 %collective-permute-start.3 = (bf16[2,128,512]{2,1,0:T(8,128)(2,1)S(1)}, bf16[2,128,512]{2,1,0:T(8,128)(2,1)S(1)}, u32[]{:S(2)}, u32[]{:S(2)}) collective-permute-start(bf16[2,128,512]{2,1,0:T(8,128)(2,1)S(1)} %get-tuple-element.40), channel_id=1, source_target_pairs={{0,16},{1,5},{2,18},{3,7},{4,20},{5,1},{6,22},{7,3},{8,24},{9,13},... | collective-permute-start | bytes 786440 | tf_op jit(solution)/shard_map/ppermute | solution.py:35
  8.4 1.1 %collective-permute-start.4 = (bf16[2,128,512]{2,1,0:T(8,128)(2,1)S(1)}, bf16[2,128,512]{2,1,0:T(8,128)(2,1)S(1)}, u32[]{:S(2)}, u32[]{:S(2)}) collective-permute-start(bf16[2,128,512]{2,1,0:T(8,128)(2,1)S(1)} %get-tuple-element.40), channel_id=1, source_target_pairs={{0,24},{1,7},{2,26},{3,1},{4,28},{5,3},{6,30},{7,5},{8,0},{9,15},{... | collective-permute-start | bytes 786440 | tf_op jit(solution)/shard_map/ppermute | solution.py:35
  9.5 0.0 collective-permute-done.8
  9.5 0.1 pad_maximum_fusion.1.w0
  9.6 3.7 %collective-permute-start.10 = (bf16[2,8,128,128]{3,2,1,0:T(8,128)(2,1)S(1)}, bf16[2,8,128,128]{3,2,1,0:T(8,128)(2,1)S(1)}, u32[]{:S(2)}, u32[]{:S(2)}) collective-permute-start(bf16[2,8,128,128]{3,2,1,0:T(8,128)(2,1)S(1)} %pad_maximum_fusion.1.w0), channel_id=1, source_target_pairs={{0,64},{32,96},{64,0},{96,32},{1,65},{33,97},{65,1},{97,33},{2,66}... | collective-permute-start | bytes 1572872 | tf_op jit(solution)/shard_map/ppermute | solution.py:41
  13.2 0.0 collective-permute-done.2
  13.3 2.1 %collective-permute-done.3 = bf16[2,128,512]{2,1,0:T(8,128)(2,1)S(1)} collective-permute-done((bf16[2,128,512]{2,1,0:T(8,128)(2,1)S(1)}, bf16[2,128,512]{2,1,0:T(8,128)(2,1)S(1)}, u32[]{:S(2)}, u32[]{:S(2)}) %collective-permute-start.3) | collective-permute-done | bytes 262176 | tf_op jit(solution)/shard_map/ppermute | solution.py:35
  15.3 0.0 collective-permute-done.4
  15.3 0.1 pad_maximum_fusion.a0
  15.4 1.3 %collective-permute-start.5 = (bf16[4,2,128,512]{3,2,1,0:T(8,128)(2,1)S(1)}, bf16[4,2,128,512]{3,2,1,0:T(8,128)(2,1)S(1)}, u32[]{:S(2)}, u32[]{:S(2)}) collective-permute-start(bf16[4,2,128,512]{3,2,1,0:T(8,128)(2,1)S(1)} %pad_maximum_fusion.a0), channel_id=1, source_target_pairs={{0,2},{1,9},{2,4},{3,11},{4,6},{5,13},{6,0},{7,15},{8,10},{9,17},{... | collective-permute-start | bytes 3145736 | tf_op jit(solution)/shard_map/ppermute | solution.py:35
  16.7 2.5 %collective-permute-start.6 = (bf16[4,2,128,512]{3,2,1,0:T(8,128)(2,1)S(1)}, bf16[4,2,128,512]{3,2,1,0:T(8,128)(2,1)}, u32[]{:S(2)}, u32[]{:S(2)}) collective-permute-start(bf16[4,2,128,512]{3,2,1,0:T(8,128)(2,1)S(1)} %pad_maximum_fusion.a0), channel_id=1, source_target_pairs={{0,4},{1,17},{2,6},{3,19},{4,0},{5,21},{6,2},{7,23},{8,12},{9,25},... | collective-permute-start | bytes 3145736 | tf_op jit(solution)/shard_map/ppermute | solution.py:35
  19.2 1.2 %collective-permute-start.7 = (bf16[4,2,128,512]{3,2,1,0:T(8,128)(2,1)S(1)}, bf16[4,2,128,512]{3,2,1,0:T(8,128)(2,1)}, u32[]{:S(2)}, u32[]{:S(2)}) collective-permute-start(bf16[4,2,128,512]{3,2,1,0:T(8,128)(2,1)S(1)} %pad_maximum_fusion.a0), channel_id=1, source_target_pairs={{0,6},{1,25},{2,0},{3,27},{4,2},{5,29},{6,4},{7,31},{8,14},{9,1},{... | collective-permute-start | bytes 3145736 | tf_op jit(solution)/shard_map/ppermute | solution.py:35
  20.3 0.1 copy.11
  20.4 0.1 copy.12
  20.5 2.2 %collective-permute-start = (s32[4,8]{1,0:T(4,128)S(1)}, s32[4,8]{1,0:T(4,128)S(1)}, u32[]{:S(2)}, u32[]{:S(2)}) collective-permute-start(s32[4,8]{1,0:T(4,128)S(1)} %bitcast.58), channel_id=1, source_target_pairs={{0,1},{1,0},{2,3},{3,2},{4,5},{5,4},{6,7},{7,6},{8,9},{9,8},{10,11... | collective-permute-start | bytes 392 | tf_op jit(solution)/shard_map/ppermute | solution.py:45
  22.7 0.8 collective-permute-done
  23.5 1.6 %collective-permute-start.11 = (bf16[2,8,128,128]{3,2,1,0:T(8,128)(2,1)S(1)}, bf16[2,8,128,128]{3,2,1,0:T(8,128)(2,1)}, u32[]{:S(2)}, u32[]{:S(2)}) collective-permute-start(bf16[2,8,128,128]{3,2,1,0:T(8,128)(2,1)S(1)} %pad_maximum_fusion.1.w0), channel_id=1, source_target_pairs={{0,96},{32,0},{64,32},{96,64},{1,33},{33,65},{65,97},{97,1},{2,98}... | collective-permute-start | bytes 1572872 | tf_op jit(solution)/shard_map/ppermute | solution.py:41
  25.1 0.0 collective-permute-done.10.w2
  25.1 2.1 %collective-permute-start.9 = (bf16[2,8,128,128]{3,2,1,0:T(8,128)(2,1)S(1)}, bf16[2,8,128,128]{3,2,1,0:T(8,128)(2,1)}, u32[]{:S(2)}, u32[]{:S(2)}) collective-permute-start(bf16[2,8,128,128]{3,2,1,0:T(8,128)(2,1)S(1)} %pad_maximum_fusion.1.w0), channel_id=1, source_target_pairs={{0,32},{32,64},{64,96},{96,0},{1,97},{33,1},{65,33},{97,65},{2,34}... | collective-permute-start | bytes 1572872 | tf_op jit(solution)/shard_map/ppermute | solution.py:41
  27.3 0.1 pad_add_fusion.1.where_ref
  27.3 8.7 %collective-permute-done.11.w3 = bf16[2,8,128,128]{3,2,1,0:T(8,128)(2,1)} collective-permute-done((bf16[2,8,128,128]{3,2,1,0:T(8,128)(2,1)S(1)}, bf16[2,8,128,128]{3,2,1,0:T(8,128)(2,1)}, u32[]{:S(2)}, u32[]{:S(2)}) %collective-permute-start.11) | collective-permute-done | bytes 524320 | tf_op jit(solution)/shard_map/ppermute | solution.py:41
  36.0 2.3 %collective-permute-done.9.w1 = bf16[2,8,128,128]{3,2,1,0:T(8,128)(2,1)} collective-permute-done((bf16[2,8,128,128]{3,2,1,0:T(8,128)(2,1)S(1)}, bf16[2,8,128,128]{3,2,1,0:T(8,128)(2,1)}, u32[]{:S(2)}, u32[]{:S(2)}) %collective-permute-start.9) | collective-permute-done | bytes 524320 | tf_op jit(solution)/shard_map/ppermute | solution.py:41
  38.3 0.0 collective-permute-done.5.a1
  38.3 4.7 %collective-permute-done.6.a2 = bf16[4,2,128,512]{3,2,1,0:T(8,128)(2,1)} collective-permute-done((bf16[4,2,128,512]{3,2,1,0:T(8,128)(2,1)S(1)}, bf16[4,2,128,512]{3,2,1,0:T(8,128)(2,1)}, u32[]{:S(2)}, u32[]{:S(2)}) %collective-permute-start.6) | collective-permute-done | bytes 1048608 | tf_op jit(solution)/shard_map/ppermute | solution.py:35
  43.0 0.0 collective-permute-done.7.a3
  43.0 5.5 %enter.1 = (bf16[4,4,2,128,512]{4,3,2,1,0:T(8,128)(2,1)S(1)}, bf16[4,2,8,128,128]{4,3,2,1,0:T(8,128)(2,1)S(1)}, bf16[8,512,128]{2,1,0:T(8,128)(2,1)S(1)}, f32[8,...) custom-call(s32[2]{0:T(128)S(1)} %pad_add_fusion.1.where_ref, s32[2,4,8]{2,1,0:T(4,128)S(1)} %and_add_fusion.codes_ref, ...), custom_call_target="tpu_custom_call" | custom-call | flops 1073741824 | bytes 8388608 | tf_op jit(solution)/shard_map/enter/pallas_call | solution.py:235
  48.5 3.0 %collective-permute-start.12 = (bf16[8,512,128]{2,1,0:T(8,128)(2,1)S(1)}, bf16[8,512,128]{2,1,0:T(8,128)(2,1)S(1)}, u32[]{:S(2)}, u32[]{:S(2)}) collective-permute-start(bf16[8,512,128]{2,1,0:T(8,128)(2,1)S(1)} %get-tuple-element.18), channel_id=1, source_target_pairs={{0,1},{1,0},{2,3},{3,2},{4,5},{5,4},{6,7},{7,6},{8,9},{9,8},{10,11... | collective-permute-start | bytes 3145736 | tf_op jit(solution)/shard_map/ppermute | solution.py:45
  51.5 2.3 %collective-permute-done.12.came = bf16[8,512,128]{2,1,0:T(8,128)(2,1)S(1)} collective-permute-done((bf16[8,512,128]{2,1,0:T(8,128)(2,1)S(1)}, bf16[8,512,128]{2,1,0:T(8,128)(2,1)S(1)}, u32[]{:S(2)}, u32[]{:S(2)}) %collective-permute-start.12) | collective-permute-done | bytes 1048608 | tf_op jit(solution)/shard_map/ppermute | solution.py:45
  53.8 5.6 %sums.1 = (f32[4,4,2,128,512]{4,3,2,1,0:T(8,128)S(1)}, bf16[4,2,128,512]{3,2,1,0:T(8,128)(2,1)S(1)}, bf16[4,2,128,512]{3,2,1,0:T(8,128)(2,1)S(1)}, bf16[4,2,128,...) custom-call(s32[2]{0:T(128)S(1)} %pad_add_fusion.1.where_ref, ...), custom_call_target="tpu_custom_call", output_to_operand_aliasing={{0}: (5, {})} | custom-call | flops 1073741824 | bytes 8388608 | tf_op jit(solution)/shard_map/sums/pallas_call | solution.py:257
  59.4 2.3 %collective-permute-start.13 = (bf16[4,2,128,512]{3,2,1,0:T(8,128)(2,1)S(1)}, bf16[4,2,128,512]{3,2,1,0:T(8,128)(2,1)S(1)}, u32[]{:S(2)}, u32[]{:S(2)}) collective-permute-start(bf16[4,2,128,512]{3,2,1,0:T(8,128)(2,1)S(1)} %get-tuple-element.22), channel_id=1, source_target_pairs={{0,6},{1,25},{2,0},{3,27},{4,2},{5,29},{6,4},{7,31},{8,14},{9,1},{... | collective-permute-start | bytes 3145736 | tf_op jit(solution)/shard_map/ppermute | solution.py:35
  61.7 0.0 collective-permute-start.14
  61.7 1.9 %collective-permute-start.15 = (bf16[4,2,128,512]{3,2,1,0:T(8,128)(2,1)S(1)}, bf16[4,2,128,512]{3,2,1,0:T(8,128)(2,1)S(1)}, u32[]{:S(2)}, u32[]{:S(2)}) collective-permute-start(bf16[4,2,128,512]{3,2,1,0:T(8,128)(2,1)S(1)} %get-tuple-element.24), channel_id=1, source_target_pairs={{0,4},{1,17},{2,6},{3,19},{4,0},{5,21},{6,2},{7,23},{8,12},{9,25},... | collective-permute-start | bytes 3145736 | tf_op jit(solution)/shard_map/ppermute | solution.py:35
  63.6 2.3 %grads.3 = (bf16[2,8,128,128]{3,2,1,0:T(8,128)(2,1)S(1)}, bf16[2,8,128,128]{3,2,1,0:T(8,128)(2,1)S(1)}) custom-call(s32[2]{0:T(128)S(1)} %pad_add_fusion.1.where_ref, s32[2,4,8]{2,1,0:T(4,128)S(1)} %and_add_fusion.codes_ref, bf16[4,4,2,128,512]{4,3,2,1,0:T(8,128)(2,1)S(1)} %get-tuple-element.25.acts, bf16[8,512,128]{2,1,0:T(8,128)(2,1)S(1)} %collective-permute-done.12.came, ...), custom_call_target="tpu_custom_call" | custom-call | flops 536870912 | bytes 8388608 | tf_op jit(solution)/shard_map/grads/pallas_call | solution.py:270
  65.9 3.7 %collective-permute-start.20 = (bf16[2,8,128,128]{3,2,1,0:T(8,128)(2,1)S(1)}, bf16[2,8,128,128]{3,2,1,0:T(8,128)(2,1)S(1)}, u32[]{:S(2)}, u32[]{:S(2)}) collective-permute-start(bf16[2,8,128,128]{3,2,1,0:T(8,128)(2,1)S(1)} %get-tuple-element.27), channel_id=1, source_target_pairs={{0,64},{32,96},{64,0},{96,32},{1,65},{33,97},{65,1},{97,33},{2,66}... | collective-permute-start | bytes 1572872 | tf_op jit(solution)/shard_map/ppermute | solution.py:41
  69.6 0.7 collective-permute-start.21
  70.3 2.2 %grads.2 = (bf16[2,8,128,128]{3,2,1,0:T(8,128)(2,1)S(1)}, bf16[2,8,128,128]{3,2,1,0:T(8,128)(2,1)S(1)}) custom-call(s32[2]{0:T(128)S(1)} %pad_add_fusion.1.where_ref, s32[2,4,8]{2,1,0:T(4,128)S(1)} %and_add_fusion.codes_ref, bf16[4,4,2,128,512]{4,3,2,1,0:T(8,128)(2,1)S(1)} %get-tuple-element.25.acts, bf16[8,512,128]{2,1,0:T(8,128)(2,1)S(1)} %collective-permute-done.12.came, ...), custom_call_target="tpu_custom_call" | custom-call | flops 536870912 | bytes 8388608 | tf_op jit(solution)/shard_map/grads/pallas_call | solution.py:270
  72.5 12.2 %collective-permute-done.13 = bf16[4,2,128,512]{3,2,1,0:T(8,128)(2,1)S(1)} collective-permute-done((bf16[4,2,128,512]{3,2,1,0:T(8,128)(2,1)S(1)}, bf16[4,2,128,512]{3,2,1,0:T(8,128)(2,1)S(1)}, u32[]{:S(2)}, u32[]{:S(2)}) %collective-permute-start.13) | collective-permute-done | bytes 1048608 | tf_op jit(solution)/shard_map/ppermute | solution.py:35
  84.7 3.8 %collective-permute-start.22 = (bf16[2,8,128,128]{3,2,1,0:T(8,128)(2,1)S(1)}, bf16[2,8,128,128]{3,2,1,0:T(8,128)(2,1)S(1)}, u32[]{:S(2)}, u32[]{:S(2)}) collective-permute-start(bf16[2,8,128,128]{3,2,1,0:T(8,128)(2,1)S(1)} %get-tuple-element.29), channel_id=1, source_target_pairs={{0,32},{32,64},{64,96},{96,0},{1,97},{33,1},{65,33},{97,65},{2,34}... | collective-permute-start | bytes 1572872 | tf_op jit(solution)/shard_map/ppermute | solution.py:41
  88.5 0.0 collective-permute-done.14
  88.5 0.0 collective-permute-done.15
  88.5 0.6 add_convert_fusion
  89.1 0.1 slice_bitcast_fusion.4
  89.2 2.1 %collective-permute-start.16 = (bf16[2,128,512]{2,1,0:T(8,128)(2,1)S(1)}, bf16[2,128,512]{2,1,0:T(8,128)(2,1)S(1)}, u32[]{:S(2)}, u32[]{:S(2)}) collective-permute-start(bf16[2,128,512]{2,1,0:T(8,128)(2,1)S(1)} %get-tuple-element.30), channel_id=1, source_target_pairs={{0,24},{1,7},{2,26},{3,1},{4,28},{5,3},{6,30},{7,5},{8,0},{9,15},{... | collective-permute-start | bytes 786440 | tf_op jit(solution)/shard_map/ppermute | solution.py:35
  91.3 0.0 collective-permute-start.17
  91.3 0.0 collective-permute-done.20
  91.3 2.0 %collective-permute-start.18 = (bf16[2,128,512]{2,1,0:T(8,128)(2,1)S(1)}, bf16[2,128,512]{2,1,0:T(8,128)(2,1)S(1)}, u32[]{:S(2)}, u32[]{:S(2)}) collective-permute-start(bf16[2,128,512]{2,1,0:T(8,128)(2,1)S(1)} %get-tuple-element.31), channel_id=1, source_target_pairs={{0,16},{1,5},{2,18},{3,7},{4,20},{5,1},{6,22},{7,3},{8,24},{9,13},... | collective-permute-start | bytes 786440 | tf_op jit(solution)/shard_map/ppermute | solution.py:35
  93.3 1.4 %collective-permute-done.22 = bf16[2,8,128,128]{3,2,1,0:T(8,128)(2,1)S(1)} collective-permute-done((bf16[2,8,128,128]{3,2,1,0:T(8,128)(2,1)S(1)}, bf16[2,8,128,128]{3,2,1,0:T(8,128)(2,1)S(1)}, u32[]{:S(2)}, u32[]{:S(2)}) %collective-permute-start.22) | collective-permute-done | bytes 524320 | tf_op jit(solution)/shard_map/ppermute | solution.py:41
  94.6 0.3 multiply_convert_fusion
  95.0 2.4 %collective-permute-start.23 = (bf16[8,128,128]{2,1,0:T(8,128)(2,1)S(1)}, bf16[8,128,128]{2,1,0:T(8,128)(2,1)S(1)}, u32[]{:S(2)}, u32[]{:S(2)}) collective-permute-start(bf16[8,128,128]{2,1,0:T(8,128)(2,1)S(1)} %slice_bitcast_fusion), channel_id=1, source_target_pairs={{0,1},{1,0},{2,3},{3,2},{4,5},{5,4},{6,7},{7,6},{8,9},{9,8},{10,11... | collective-permute-start | bytes 786440 | tf_op jit(solution)/shard_map/ppermute | solution.py:45
  97.4 3.4 %collective-permute-done.17 = bf16[2,128,512]{2,1,0:T(8,128)(2,1)S(1)} collective-permute-done((bf16[2,128,512]{2,1,0:T(8,128)(2,1)S(1)}, bf16[2,128,512]{2,1,0:T(8,128)(2,1)S(1)}, u32[]{:S(2)}, u32[]{:S(2)}) %collective-permute-start.17) | collective-permute-done | bytes 262176 | tf_op jit(solution)/shard_map/ppermute | solution.py:35
  100.8 0.0 collective-permute-done.18
  100.8 0.1 fusion.2
  101.0 2.4 %collective-permute-start.19 = (bf16[128,512]{1,0:T(8,128)(2,1)S(1)}, bf16[128,512]{1,0:T(8,128)(2,1)S(1)}, u32[]{:S(2)}, u32[]{:S(2)}) collective-permute-start(bf16[128,512]{1,0:T(8,128)(2,1)S(1)} %slice_bitcast_fusion.7), channel_id=1, source_target_pairs={{0,1},{1,0},{2,3},{3,2},{4,5},{5,4},{6,7},{7,6},{8,9},{9,8},{10,11... | collective-permute-start | bytes 393224 | tf_op jit(solution)/shard_map/ppermute | solution.py:45
  103.3 0.8 select_bitcast_fusion
  104.2 0.2 collective-permute-done.19
  104.3 0.7 broadcast_select_fusion.1
  (10 shorter events, 0.1 us)
Async XLA Ops:
  1.6 2.7 %collective-permute-start.1 = (bf16[128,512]{1,0:T(8,128)(2,1)S(1)}, bf16[128,512]{1,0:T(8,128)(2,1)S(1)}, u32[]{:S(2)}, u32[]{:S(2)}) collective-permute-start(bf16[128,512]{1,0:T(8,128)(2,1)S(1)} %get-tuple-element.42), channel_id=1, source_target_pairs={{0,1},{1,0},{2,3},{3,2},{4,5},{5,4},{6,7},{7,6},{8,9},{9,8},{10,11... | collective-permute-start | bytes 393224 | tf_op jit(solution)/shard_map/ppermute | solution.py:45
  4.2 16.1 %copy-start = (s32[16,8]{0,1:T(8,128)S(1)}, s32[16,8]{0,1:T(8,128)}, u32[]{:S(2)}) copy-start(s32[16,8]{0,1:T(8,128)} %param.8) | copy-start | bytes 1540
  4.2 16.2 %copy-start.1 = (s32[16,8]{0,1:T(8,128)S(1)}, s32[16,8]{0,1:T(8,128)}, u32[]{:S(2)}) copy-start(s32[16,8]{0,1:T(8,128)} %param.10) | copy-start | bytes 1540
  4.2 5.3 %collective-permute-start.8 = (bf16[8,128,128]{2,1,0:T(8,128)(2,1)S(1)}, bf16[8,128,128]{2,1,0:T(8,128)(2,1)S(1)}, u32[]{:S(2)}, u32[]{:S(2)}) collective-permute-start(bf16[8,128,128]{2,1,0:T(8,128)(2,1)S(1)} %get-tuple-element.36), channel_id=1, source_target_pairs={{0,1},{1,0},{2,3},{3,2},{4,5},{5,4},{6,7},{7,6},{8,9},{9,8},{10,11... | collective-permute-start | bytes 786440 | tf_op jit(solution)/shard_map/ppermute | solution.py:45
  4.4 8.9 %collective-permute-start.2 = (bf16[2,128,512]{2,1,0:T(8,128)(2,1)S(1)}, bf16[2,128,512]{2,1,0:T(8,128)(2,1)S(1)}, u32[]{:S(2)}, u32[]{:S(2)}) collective-permute-start(bf16[2,128,512]{2,1,0:T(8,128)(2,1)S(1)} %get-tuple-element.40), channel_id=1, source_target_pairs={{0,8},{1,3},{2,10},{3,5},{4,12},{5,7},{6,14},{7,1},{8,16},{9,11},{... | collective-permute-start | bytes 786440 | tf_op jit(solution)/shard_map/ppermute | solution.py:35
  5.8 9.5 %collective-permute-start.3 = (bf16[2,128,512]{2,1,0:T(8,128)(2,1)S(1)}, bf16[2,128,512]{2,1,0:T(8,128)(2,1)S(1)}, u32[]{:S(2)}, u32[]{:S(2)}) collective-permute-start(bf16[2,128,512]{2,1,0:T(8,128)(2,1)S(1)} %get-tuple-element.40), channel_id=1, source_target_pairs={{0,16},{1,5},{2,18},{3,7},{4,20},{5,1},{6,22},{7,3},{8,24},{9,13},... | collective-permute-start | bytes 786440 | tf_op jit(solution)/shard_map/ppermute | solution.py:35
  8.4 6.9 %collective-permute-start.4 = (bf16[2,128,512]{2,1,0:T(8,128)(2,1)S(1)}, bf16[2,128,512]{2,1,0:T(8,128)(2,1)S(1)}, u32[]{:S(2)}, u32[]{:S(2)}) collective-permute-start(bf16[2,128,512]{2,1,0:T(8,128)(2,1)S(1)} %get-tuple-element.40), channel_id=1, source_target_pairs={{0,24},{1,7},{2,26},{3,1},{4,28},{5,3},{6,30},{7,5},{8,0},{9,15},{... | collective-permute-start | bytes 786440 | tf_op jit(solution)/shard_map/ppermute | solution.py:35
  9.6 15.6 %collective-permute-start.10 = (bf16[2,8,128,128]{3,2,1,0:T(8,128)(2,1)S(1)}, bf16[2,8,128,128]{3,2,1,0:T(8,128)(2,1)S(1)}, u32[]{:S(2)}, u32[]{:S(2)}) collective-permute-start(bf16[2,8,128,128]{3,2,1,0:T(8,128)(2,1)S(1)} %pad_maximum_fusion.1.w0), channel_id=1, source_target_pairs={{0,64},{32,96},{64,0},{96,32},{1,65},{33,97},{65,1},{97,33},{2,66}... | collective-permute-start | bytes 1572872 | tf_op jit(solution)/shard_map/ppermute | solution.py:41
  15.4 22.9 %collective-permute-start.5 = (bf16[4,2,128,512]{3,2,1,0:T(8,128)(2,1)S(1)}, bf16[4,2,128,512]{3,2,1,0:T(8,128)(2,1)S(1)}, u32[]{:S(2)}, u32[]{:S(2)}) collective-permute-start(bf16[4,2,128,512]{3,2,1,0:T(8,128)(2,1)S(1)} %pad_maximum_fusion.a0), channel_id=1, source_target_pairs={{0,2},{1,9},{2,4},{3,11},{4,6},{5,13},{6,0},{7,15},{8,10},{9,17},{... | collective-permute-start | bytes 3145736 | tf_op jit(solution)/shard_map/ppermute | solution.py:35
  16.7 26.3 %collective-permute-start.6 = (bf16[4,2,128,512]{3,2,1,0:T(8,128)(2,1)S(1)}, bf16[4,2,128,512]{3,2,1,0:T(8,128)(2,1)}, u32[]{:S(2)}, u32[]{:S(2)}) collective-permute-start(bf16[4,2,128,512]{3,2,1,0:T(8,128)(2,1)S(1)} %pad_maximum_fusion.a0), channel_id=1, source_target_pairs={{0,4},{1,17},{2,6},{3,19},{4,0},{5,21},{6,2},{7,23},{8,12},{9,25},... | collective-permute-start | bytes 3145736 | tf_op jit(solution)/shard_map/ppermute | solution.py:35
  19.2 23.8 %collective-permute-start.7 = (bf16[4,2,128,512]{3,2,1,0:T(8,128)(2,1)S(1)}, bf16[4,2,128,512]{3,2,1,0:T(8,128)(2,1)}, u32[]{:S(2)}, u32[]{:S(2)}) collective-permute-start(bf16[4,2,128,512]{3,2,1,0:T(8,128)(2,1)S(1)} %pad_maximum_fusion.a0), channel_id=1, source_target_pairs={{0,6},{1,25},{2,0},{3,27},{4,2},{5,29},{6,4},{7,31},{8,14},{9,1},{... | collective-permute-start | bytes 3145736 | tf_op jit(solution)/shard_map/ppermute | solution.py:35
  20.5 3.0 %collective-permute-start = (s32[4,8]{1,0:T(4,128)S(1)}, s32[4,8]{1,0:T(4,128)S(1)}, u32[]{:S(2)}, u32[]{:S(2)}) collective-permute-start(s32[4,8]{1,0:T(4,128)S(1)} %bitcast.58), channel_id=1, source_target_pairs={{0,1},{1,0},{2,3},{3,2},{4,5},{5,4},{6,7},{7,6},{8,9},{9,8},{10,11... | collective-permute-start | bytes 392 | tf_op jit(solution)/shard_map/ppermute | solution.py:45
  23.5 12.5 %collective-permute-start.11 = (bf16[2,8,128,128]{3,2,1,0:T(8,128)(2,1)S(1)}, bf16[2,8,128,128]{3,2,1,0:T(8,128)(2,1)}, u32[]{:S(2)}, u32[]{:S(2)}) collective-permute-start(bf16[2,8,128,128]{3,2,1,0:T(8,128)(2,1)S(1)} %pad_maximum_fusion.1.w0), channel_id=1, source_target_pairs={{0,96},{32,0},{64,32},{96,64},{1,33},{33,65},{65,97},{97,1},{2,98}... | collective-permute-start | bytes 1572872 | tf_op jit(solution)/shard_map/ppermute | solution.py:41
  25.1 13.2 %collective-permute-start.9 = (bf16[2,8,128,128]{3,2,1,0:T(8,128)(2,1)S(1)}, bf16[2,8,128,128]{3,2,1,0:T(8,128)(2,1)}, u32[]{:S(2)}, u32[]{:S(2)}) collective-permute-start(bf16[2,8,128,128]{3,2,1,0:T(8,128)(2,1)S(1)} %pad_maximum_fusion.1.w0), channel_id=1, source_target_pairs={{0,32},{32,64},{64,96},{96,0},{1,97},{33,1},{65,33},{97,65},{2,34}... | collective-permute-start | bytes 1572872 | tf_op jit(solution)/shard_map/ppermute | solution.py:41
  48.5 5.3 %collective-permute-start.12 = (bf16[8,512,128]{2,1,0:T(8,128)(2,1)S(1)}, bf16[8,512,128]{2,1,0:T(8,128)(2,1)S(1)}, u32[]{:S(2)}, u32[]{:S(2)}) collective-permute-start(bf16[8,512,128]{2,1,0:T(8,128)(2,1)S(1)} %get-tuple-element.18), channel_id=1, source_target_pairs={{0,1},{1,0},{2,3},{3,2},{4,5},{5,4},{6,7},{7,6},{8,9},{9,8},{10,11... | collective-permute-start | bytes 3145736 | tf_op jit(solution)/shard_map/ppermute | solution.py:45
  59.4 25.3 %collective-permute-start.13 = (bf16[4,2,128,512]{3,2,1,0:T(8,128)(2,1)S(1)}, bf16[4,2,128,512]{3,2,1,0:T(8,128)(2,1)S(1)}, u32[]{:S(2)}, u32[]{:S(2)}) collective-permute-start(bf16[4,2,128,512]{3,2,1,0:T(8,128)(2,1)S(1)} %get-tuple-element.22), channel_id=1, source_target_pairs={{0,6},{1,25},{2,0},{3,27},{4,2},{5,29},{6,4},{7,31},{8,14},{9,1},{... | collective-permute-start | bytes 3145736 | tf_op jit(solution)/shard_map/ppermute | solution.py:35
  61.7 26.8 %collective-permute-start.14 = (bf16[4,2,128,512]{3,2,1,0:T(8,128)(2,1)S(1)}, bf16[4,2,128,512]{3,2,1,0:T(8,128)(2,1)S(1)}, u32[]{:S(2)}, u32[]{:S(2)}) collective-permute-start(bf16[4,2,128,512]{3,2,1,0:T(8,128)(2,1)S(1)} %get-tuple-element.23), channel_id=1, source_target_pairs={{0,2},{1,9},{2,4},{3,11},{4,6},{5,13},{6,0},{7,15},{8,10},{9,17},{... | collective-permute-start | bytes 3145736 | tf_op jit(solution)/shard_map/ppermute | solution.py:35
  61.7 26.8 %collective-permute-start.15 = (bf16[4,2,128,512]{3,2,1,0:T(8,128)(2,1)S(1)}, bf16[4,2,128,512]{3,2,1,0:T(8,128)(2,1)S(1)}, u32[]{:S(2)}, u32[]{:S(2)}) collective-permute-start(bf16[4,2,128,512]{3,2,1,0:T(8,128)(2,1)S(1)} %get-tuple-element.24), channel_id=1, source_target_pairs={{0,4},{1,17},{2,6},{3,19},{4,0},{5,21},{6,2},{7,23},{8,12},{9,25},... | collective-permute-start | bytes 3145736 | tf_op jit(solution)/shard_map/ppermute | solution.py:35
  65.9 25.4 %collective-permute-start.20 = (bf16[2,8,128,128]{3,2,1,0:T(8,128)(2,1)S(1)}, bf16[2,8,128,128]{3,2,1,0:T(8,128)(2,1)S(1)}, u32[]{:S(2)}, u32[]{:S(2)}) collective-permute-start(bf16[2,8,128,128]{3,2,1,0:T(8,128)(2,1)S(1)} %get-tuple-element.27), channel_id=1, source_target_pairs={{0,64},{32,96},{64,0},{96,32},{1,65},{33,97},{65,1},{97,33},{2,66}... | collective-permute-start | bytes 1572872 | tf_op jit(solution)/shard_map/ppermute | solution.py:41
  69.6 23.7 %collective-permute-start.21 = (bf16[2,8,128,128]{3,2,1,0:T(8,128)(2,1)S(1)}, bf16[2,8,128,128]{3,2,1,0:T(8,128)(2,1)S(1)}, u32[]{:S(2)}, u32[]{:S(2)}) collective-permute-start(bf16[2,8,128,128]{3,2,1,0:T(8,128)(2,1)S(1)} %get-tuple-element.28), channel_id=1, source_target_pairs={{0,96},{32,0},{64,32},{96,64},{1,33},{33,65},{65,97},{97,1},{2,98}... | collective-permute-start | bytes 1572872 | tf_op jit(solution)/shard_map/ppermute | solution.py:41
  84.7 9.9 %collective-permute-start.22 = (bf16[2,8,128,128]{3,2,1,0:T(8,128)(2,1)S(1)}, bf16[2,8,128,128]{3,2,1,0:T(8,128)(2,1)S(1)}, u32[]{:S(2)}, u32[]{:S(2)}) collective-permute-start(bf16[2,8,128,128]{3,2,1,0:T(8,128)(2,1)S(1)} %get-tuple-element.29), channel_id=1, source_target_pairs={{0,32},{32,64},{64,96},{96,0},{1,97},{33,1},{65,33},{97,65},{2,34}... | collective-permute-start | bytes 1572872 | tf_op jit(solution)/shard_map/ppermute | solution.py:41
  89.2 8.2 %collective-permute-start.16 = (bf16[2,128,512]{2,1,0:T(8,128)(2,1)S(1)}, bf16[2,128,512]{2,1,0:T(8,128)(2,1)S(1)}, u32[]{:S(2)}, u32[]{:S(2)}) collective-permute-start(bf16[2,128,512]{2,1,0:T(8,128)(2,1)S(1)} %get-tuple-element.30), channel_id=1, source_target_pairs={{0,24},{1,7},{2,26},{3,1},{4,28},{5,3},{6,30},{7,5},{8,0},{9,15},{... | collective-permute-start | bytes 786440 | tf_op jit(solution)/shard_map/ppermute | solution.py:35
  91.3 9.5 %collective-permute-start.17 = (bf16[2,128,512]{2,1,0:T(8,128)(2,1)S(1)}, bf16[2,128,512]{2,1,0:T(8,128)(2,1)S(1)}, u32[]{:S(2)}, u32[]{:S(2)}) collective-permute-start(bf16[2,128,512]{2,1,0:T(8,128)(2,1)S(1)} %get-tuple-element.32), channel_id=1, source_target_pairs={{0,8},{1,3},{2,10},{3,5},{4,12},{5,7},{6,14},{7,1},{8,16},{9,11},{... | collective-permute-start | bytes 786440 | tf_op jit(solution)/shard_map/ppermute | solution.py:35
  91.3 9.5 %collective-permute-start.18 = (bf16[2,128,512]{2,1,0:T(8,128)(2,1)S(1)}, bf16[2,128,512]{2,1,0:T(8,128)(2,1)S(1)}, u32[]{:S(2)}, u32[]{:S(2)}) collective-permute-start(bf16[2,128,512]{2,1,0:T(8,128)(2,1)S(1)} %get-tuple-element.31), channel_id=1, source_target_pairs={{0,16},{1,5},{2,18},{3,7},{4,20},{5,1},{6,22},{7,3},{8,24},{9,13},... | collective-permute-start | bytes 786440 | tf_op jit(solution)/shard_map/ppermute | solution.py:35
  95.0 8.3 %collective-permute-start.23 = (bf16[8,128,128]{2,1,0:T(8,128)(2,1)S(1)}, bf16[8,128,128]{2,1,0:T(8,128)(2,1)S(1)}, u32[]{:S(2)}, u32[]{:S(2)}) collective-permute-start(bf16[8,128,128]{2,1,0:T(8,128)(2,1)S(1)} %slice_bitcast_fusion), channel_id=1, source_target_pairs={{0,1},{1,0},{2,3},{3,2},{4,5},{5,4},{6,7},{7,6},{8,9},{9,8},{10,11... | collective-permute-start | bytes 786440 | tf_op jit(solution)/shard_map/ppermute | solution.py:45
  101.0 3.4 %collective-permute-start.19 = (bf16[128,512]{1,0:T(8,128)(2,1)S(1)}, bf16[128,512]{1,0:T(8,128)(2,1)S(1)}, u32[]{:S(2)}, u32[]{:S(2)}) collective-permute-start(bf16[128,512]{1,0:T(8,128)(2,1)S(1)} %slice_bitcast_fusion.7), channel_id=1, source_target_pairs={{0,1},{1,0},{2,3},{3,2},{4,5},{5,4},{6,7},{7,6},{8,9},{9,8},{10,11... | collective-permute-start | bytes 393224 | tf_op jit(solution)/shard_map/ppermute | solution.py:45

commit v7 on v6

--- a/solution.py
+++ b/solution.py
@@ -309,7 +309,7 @@
     grads = [grads_0, grads_1, grads_2, grads_3]
 
     summed = reduce(chunks, first(False)).astype(jnp.bfloat16)
-    final = reduce([summed[n] for n in range(RING)], first(True)).astype(jnp.bfloat16)
+    final = reduce([summed[n] for n in range(RING)], first(True), (2, 1, 3)).astype(jnp.bfloat16)
     grad_scale = 1.0 / math.sqrt(tokens.shape[0] * lax.axis_size("z") * lax.axis_size("x"))
     scaled = (reduce(grads, z_shift, (2, 1, 3)) * grad_scale).astype(jnp.bfloat16)
     came_grad = swap(scaled[1])

time: 105 us -> 104 us (level)
  waiting for transfers between devices: 37.9 us -> 36.7 us
    ppermute x12, waiting for transfers between devices: 22.3 us -> 21.1 us  [mixed_shift(): return lax.ppermute(values, MIXED, mixed_pairs(step, first))]
  transfers between devices with their start and end apart: 24 -> 24, of which waited for: 10 -> 11; matrix products, arithmetic and copies ran while one was open for 3% -> 3% of each run, Pallas kernels for 4% -> 4%
where the time goes in v7:
time: 104 us
  starting transfers between devices  45.9 us (44%)
  waiting for transfers between devices  36.7 us (35%)
  Pallas kernels  15.6 us (15%)
  other arithmetic  5 us (5%)
    ppermute x12, waiting for transfers between devices, mixed_shift(): return lax.ppermute(values, MIXED, mixed_pairs(step, first))  21.1 us
    ppermute x12, starting transfers between devices, mixed_shift(): return lax.ppermute(values, MIXED, mixed_pairs(step, first))  18.4 us
    ppermute x6, starting transfers between devices, z_shift(): return lax.ppermute(values, ('z', 'core'), pairs)  15.6 us
    ppermute x6, waiting for transfers between devices, z_shift(): return lax.ppermute(values, ('z', 'core'), pairs)  12.3 us
    ppermute x6, starting transfers between devices, swap(): return lax.ppermute(values, 'core', [(0, 1), (1, 0)])  11.9 us
    pallas_call x1, Pallas kernels, sums(): pl.pallas_call(sums_kernel, out_shape=[jax.ShapeDtypeStruct(ACTS, jnp.flo...  5.58 us
    pallas_call x1, Pallas kernels, enter(): pl.pallas_call(enter_kernel, out_shape=[jax.ShapeDtypeStruct(ACTS, jnp.bf...  5.52 us
    pallas_call x2, Pallas kernels, block_grads(): pl.pallas_call(functools.partial(grads_kernel, slots), out_shape=[GRAD] *...  4.54 us
  transfers between devices with their start and end apart: 24, of which 11 were waited for; matrix products, arithmetic and copies ran while one was open for 3% of the time, Pallas kernels for 4%

profile of v7, /device:TPU:1, one launch (start us, length us, event | category | flops | bytes accessed | tf_op | source)
XLA Modules:
  0.0 104.3 jit_solution(17823641358214969756)
XLA Ops:
  0.6 1.0 select_bitcast_fusion.3
  1.6 1.5 %collective-permute-start.1 = (bf16[128,512]{1,0:T(8,128)(2,1)S(1)}, bf16[128,512]{1,0:T(8,128)(2,1)S(1)}, u32[]{:S(2)}, u32[]{:S(2)}) collective-permute-start(bf16[128,512]{1,0:T(8,128)(2,1)S(1)} %get-tuple-element.42), channel_id=1, source_target_pairs={{0,1},{1,0},{2,3},{3,2},{4,5},{5,4},{6,7},{7,6},{8,9},{9,8},{10,11... | collective-permute-start | bytes 393224 | tf_op jit(solution)/shard_map/ppermute | solution.py:45
  3.1 1.1 %broadcast_select_fusion = (bf16[1,8,128,128]{3,2,1,0:T(8,128)(2,1)S(1)}, bf16[8,128,128]{2,1,0:T(8,128)(2,1)S(1)}) fusion(bf16[1,8,128,128]{3,2,1,0:T(8,128)(2,1)} %param.7, bf16[1,8,128,128]{3,2,1,0:T(8,128)(2,1)} %param.9, pred[]{:T(512)S(6)} %eq.3), kind=kLoop, calls=%fused_computation.18 | loop fusion | flops 262144 | bytes 1048577 | tf_op jit(solution)/shard_map/jit(_where)/select_n | solution.py:292
  4.2 0.0 copy-start
  4.2 0.0 copy-start.1
  4.2 0.1 collective-permute-start.8
  4.3 0.0 collective-permute-done.1
  4.4 1.4 %collective-permute-start.2 = (bf16[2,128,512]{2,1,0:T(8,128)(2,1)S(1)}, bf16[2,128,512]{2,1,0:T(8,128)(2,1)S(1)}, u32[]{:S(2)}, u32[]{:S(2)}) collective-permute-start(bf16[2,128,512]{2,1,0:T(8,128)(2,1)S(1)} %get-tuple-element.40), channel_id=1, source_target_pairs={{0,8},{1,3},{2,10},{3,5},{4,12},{5,7},{6,14},{7,1},{8,16},{9,11},{... | collective-permute-start | bytes 786440 | tf_op jit(solution)/shard_map/ppermute | solution.py:35
  5.8 2.6 %collective-permute-start.3 = (bf16[2,128,512]{2,1,0:T(8,128)(2,1)S(1)}, bf16[2,128,512]{2,1,0:T(8,128)(2,1)S(1)}, u32[]{:S(2)}, u32[]{:S(2)}) collective-permute-start(bf16[2,128,512]{2,1,0:T(8,128)(2,1)S(1)} %get-tuple-element.40), channel_id=1, source_target_pairs={{0,16},{1,5},{2,18},{3,7},{4,20},{5,1},{6,22},{7,3},{8,24},{9,13},... | collective-permute-start | bytes 786440 | tf_op jit(solution)/shard_map/ppermute | solution.py:35
  8.4 1.1 %collective-permute-start.4 = (bf16[2,128,512]{2,1,0:T(8,128)(2,1)S(1)}, bf16[2,128,512]{2,1,0:T(8,128)(2,1)S(1)}, u32[]{:S(2)}, u32[]{:S(2)}) collective-permute-start(bf16[2,128,512]{2,1,0:T(8,128)(2,1)S(1)} %get-tuple-element.40), channel_id=1, source_target_pairs={{0,24},{1,7},{2,26},{3,1},{4,28},{5,3},{6,30},{7,5},{8,0},{9,15},{... | collective-permute-start | bytes 786440 | tf_op jit(solution)/shard_map/ppermute | solution.py:35
  9.5 0.0 collective-permute-done.8
  9.5 0.1 pad_maximum_fusion.1.w0
  9.6 3.7 %collective-permute-start.10 = (bf16[2,8,128,128]{3,2,1,0:T(8,128)(2,1)S(1)}, bf16[2,8,128,128]{3,2,1,0:T(8,128)(2,1)S(1)}, u32[]{:S(2)}, u32[]{:S(2)}) collective-permute-start(bf16[2,8,128,128]{3,2,1,0:T(8,128)(2,1)S(1)} %pad_maximum_fusion.1.w0), channel_id=1, source_target_pairs={{0,64},{32,96},{64,0},{96,32},{1,65},{33,97},{65,1},{97,33},{2,66}... | collective-permute-start | bytes 1572872 | tf_op jit(solution)/shard_map/ppermute | solution.py:41
  13.2 0.0 collective-permute-done.2
  13.3 2.1 %collective-permute-done.3 = bf16[2,128,512]{2,1,0:T(8,128)(2,1)S(1)} collective-permute-done((bf16[2,128,512]{2,1,0:T(8,128)(2,1)S(1)}, bf16[2,128,512]{2,1,0:T(8,128)(2,1)S(1)}, u32[]{:S(2)}, u32[]{:S(2)}) %collective-permute-start.3) | collective-permute-done | bytes 262176 | tf_op jit(solution)/shard_map/ppermute | solution.py:35
  15.3 0.0 collective-permute-done.4
  15.3 0.1 pad_maximum_fusion.a0
  15.4 1.3 %collective-permute-start.5 = (bf16[4,2,128,512]{3,2,1,0:T(8,128)(2,1)S(1)}, bf16[4,2,128,512]{3,2,1,0:T(8,128)(2,1)S(1)}, u32[]{:S(2)}, u32[]{:S(2)}) collective-permute-start(bf16[4,2,128,512]{3,2,1,0:T(8,128)(2,1)S(1)} %pad_maximum_fusion.a0), channel_id=1, source_target_pairs={{0,2},{1,9},{2,4},{3,11},{4,6},{5,13},{6,0},{7,15},{8,10},{9,17},{... | collective-permute-start | bytes 3145736 | tf_op jit(solution)/shard_map/ppermute | solution.py:35
  16.7 2.5 %collective-permute-start.6 = (bf16[4,2,128,512]{3,2,1,0:T(8,128)(2,1)S(1)}, bf16[4,2,128,512]{3,2,1,0:T(8,128)(2,1)}, u32[]{:S(2)}, u32[]{:S(2)}) collective-permute-start(bf16[4,2,128,512]{3,2,1,0:T(8,128)(2,1)S(1)} %pad_maximum_fusion.a0), channel_id=1, source_target_pairs={{0,4},{1,17},{2,6},{3,19},{4,0},{5,21},{6,2},{7,23},{8,12},{9,25},... | collective-permute-start | bytes 3145736 | tf_op jit(solution)/shard_map/ppermute | solution.py:35
  19.2 1.2 %collective-permute-start.7 = (bf16[4,2,128,512]{3,2,1,0:T(8,128)(2,1)S(1)}, bf16[4,2,128,512]{3,2,1,0:T(8,128)(2,1)}, u32[]{:S(2)}, u32[]{:S(2)}) collective-permute-start(bf16[4,2,128,512]{3,2,1,0:T(8,128)(2,1)S(1)} %pad_maximum_fusion.a0), channel_id=1, source_target_pairs={{0,6},{1,25},{2,0},{3,27},{4,2},{5,29},{6,4},{7,31},{8,14},{9,1},{... | collective-permute-start | bytes 3145736 | tf_op jit(solution)/shard_map/ppermute | solution.py:35
  20.3 0.1 copy.11
  20.4 0.1 copy.12
  20.5 2.2 %collective-permute-start = (s32[4,8]{1,0:T(4,128)S(1)}, s32[4,8]{1,0:T(4,128)S(1)}, u32[]{:S(2)}, u32[]{:S(2)}) collective-permute-start(s32[4,8]{1,0:T(4,128)S(1)} %bitcast.58), channel_id=1, source_target_pairs={{0,1},{1,0},{2,3},{3,2},{4,5},{5,4},{6,7},{7,6},{8,9},{9,8},{10,11... | collective-permute-start | bytes 392 | tf_op jit(solution)/shard_map/ppermute | solution.py:45
  22.7 0.8 collective-permute-done
  23.5 1.6 %collective-permute-start.11 = (bf16[2,8,128,128]{3,2,1,0:T(8,128)(2,1)S(1)}, bf16[2,8,128,128]{3,2,1,0:T(8,128)(2,1)}, u32[]{:S(2)}, u32[]{:S(2)}) collective-permute-start(bf16[2,8,128,128]{3,2,1,0:T(8,128)(2,1)S(1)} %pad_maximum_fusion.1.w0), channel_id=1, source_target_pairs={{0,96},{32,0},{64,32},{96,64},{1,33},{33,65},{65,97},{97,1},{2,98}... | collective-permute-start | bytes 1572872 | tf_op jit(solution)/shard_map/ppermute | solution.py:41
  25.1 0.0 collective-permute-done.10.w2
  25.1 2.1 %collective-permute-start.9 = (bf16[2,8,128,128]{3,2,1,0:T(8,128)(2,1)S(1)}, bf16[2,8,128,128]{3,2,1,0:T(8,128)(2,1)}, u32[]{:S(2)}, u32[]{:S(2)}) collective-permute-start(bf16[2,8,128,128]{3,2,1,0:T(8,128)(2,1)S(1)} %pad_maximum_fusion.1.w0), channel_id=1, source_target_pairs={{0,32},{32,64},{64,96},{96,0},{1,97},{33,1},{65,33},{97,65},{2,34}... | collective-permute-start | bytes 1572872 | tf_op jit(solution)/shard_map/ppermute | solution.py:41
  27.3 0.1 pad_add_fusion.1.where_ref
  27.3 8.7 %collective-permute-done.11.w3 = bf16[2,8,128,128]{3,2,1,0:T(8,128)(2,1)} collective-permute-done((bf16[2,8,128,128]{3,2,1,0:T(8,128)(2,1)S(1)}, bf16[2,8,128,128]{3,2,1,0:T(8,128)(2,1)}, u32[]{:S(2)}, u32[]{:S(2)}) %collective-permute-start.11) | collective-permute-done | bytes 524320 | tf_op jit(solution)/shard_map/ppermute | solution.py:41
  36.0 2.3 %collective-permute-done.9.w1 = bf16[2,8,128,128]{3,2,1,0:T(8,128)(2,1)} collective-permute-done((bf16[2,8,128,128]{3,2,1,0:T(8,128)(2,1)S(1)}, bf16[2,8,128,128]{3,2,1,0:T(8,128)(2,1)}, u32[]{:S(2)}, u32[]{:S(2)}) %collective-permute-start.9) | collective-permute-done | bytes 524320 | tf_op jit(solution)/shard_map/ppermute | solution.py:41
  38.3 0.0 collective-permute-done.5.a1
  38.3 4.7 %collective-permute-done.6.a2 = bf16[4,2,128,512]{3,2,1,0:T(8,128)(2,1)} collective-permute-done((bf16[4,2,128,512]{3,2,1,0:T(8,128)(2,1)S(1)}, bf16[4,2,128,512]{3,2,1,0:T(8,128)(2,1)}, u32[]{:S(2)}, u32[]{:S(2)}) %collective-permute-start.6) | collective-permute-done | bytes 1048608 | tf_op jit(solution)/shard_map/ppermute | solution.py:35
  43.0 0.0 collective-permute-done.7.a3
  43.0 5.5 %enter.1 = (bf16[4,4,2,128,512]{4,3,2,1,0:T(8,128)(2,1)S(1)}, bf16[4,2,8,128,128]{4,3,2,1,0:T(8,128)(2,1)S(1)}, bf16[8,512,128]{2,1,0:T(8,128)(2,1)S(1)}, f32[8,...) custom-call(s32[2]{0:T(128)S(1)} %pad_add_fusion.1.where_ref, s32[2,4,8]{2,1,0:T(4,128)S(1)} %and_add_fusion.codes_ref, ...), custom_call_target="tpu_custom_call" | custom-call | flops 1073741824 | bytes 8388608 | tf_op jit(solution)/shard_map/enter/pallas_call | solution.py:235
  48.5 3.0 %collective-permute-start.12 = (bf16[8,512,128]{2,1,0:T(8,128)(2,1)S(1)}, bf16[8,512,128]{2,1,0:T(8,128)(2,1)S(1)}, u32[]{:S(2)}, u32[]{:S(2)}) collective-permute-start(bf16[8,512,128]{2,1,0:T(8,128)(2,1)S(1)} %get-tuple-element.18), channel_id=1, source_target_pairs={{0,1},{1,0},{2,3},{3,2},{4,5},{5,4},{6,7},{7,6},{8,9},{9,8},{10,11... | collective-permute-start | bytes 3145736 | tf_op jit(solution)/shard_map/ppermute | solution.py:45
  51.5 2.3 %collective-permute-done.12.came = bf16[8,512,128]{2,1,0:T(8,128)(2,1)S(1)} collective-permute-done((bf16[8,512,128]{2,1,0:T(8,128)(2,1)S(1)}, bf16[8,512,128]{2,1,0:T(8,128)(2,1)S(1)}, u32[]{:S(2)}, u32[]{:S(2)}) %collective-permute-start.12) | collective-permute-done | bytes 1048608 | tf_op jit(solution)/shard_map/ppermute | solution.py:45
  53.8 5.6 %sums.1 = (f32[4,4,2,128,512]{4,3,2,1,0:T(8,128)S(1)}, bf16[4,2,128,512]{3,2,1,0:T(8,128)(2,1)S(1)}, bf16[4,2,128,512]{3,2,1,0:T(8,128)(2,1)S(1)}, bf16[4,2,128,...) custom-call(s32[2]{0:T(128)S(1)} %pad_add_fusion.1.where_ref, ...), custom_call_target="tpu_custom_call", output_to_operand_aliasing={{0}: (5, {})} | custom-call | flops 1073741824 | bytes 8388608 | tf_op jit(solution)/shard_map/sums/pallas_call | solution.py:257
  59.4 2.3 %collective-permute-start.13 = (bf16[4,2,128,512]{3,2,1,0:T(8,128)(2,1)S(1)}, bf16[4,2,128,512]{3,2,1,0:T(8,128)(2,1)S(1)}, u32[]{:S(2)}, u32[]{:S(2)}) collective-permute-start(bf16[4,2,128,512]{3,2,1,0:T(8,128)(2,1)S(1)} %get-tuple-element.22), channel_id=1, source_target_pairs={{0,6},{1,25},{2,0},{3,27},{4,2},{5,29},{6,4},{7,31},{8,14},{9,1},{... | collective-permute-start | bytes 3145736 | tf_op jit(solution)/shard_map/ppermute | solution.py:35
  61.7 0.0 collective-permute-start.14
  61.7 1.9 %collective-permute-start.15 = (bf16[4,2,128,512]{3,2,1,0:T(8,128)(2,1)S(1)}, bf16[4,2,128,512]{3,2,1,0:T(8,128)(2,1)S(1)}, u32[]{:S(2)}, u32[]{:S(2)}) collective-permute-start(bf16[4,2,128,512]{3,2,1,0:T(8,128)(2,1)S(1)} %get-tuple-element.24), channel_id=1, source_target_pairs={{0,4},{1,17},{2,6},{3,19},{4,0},{5,21},{6,2},{7,23},{8,12},{9,25},... | collective-permute-start | bytes 3145736 | tf_op jit(solution)/shard_map/ppermute | solution.py:35
  63.6 2.3 %grads.3 = (bf16[2,8,128,128]{3,2,1,0:T(8,128)(2,1)S(1)}, bf16[2,8,128,128]{3,2,1,0:T(8,128)(2,1)S(1)}) custom-call(s32[2]{0:T(128)S(1)} %pad_add_fusion.1.where_ref, s32[2,4,8]{2,1,0:T(4,128)S(1)} %and_add_fusion.codes_ref, bf16[4,4,2,128,512]{4,3,2,1,0:T(8,128)(2,1)S(1)} %get-tuple-element.25.acts, bf16[8,512,128]{2,1,0:T(8,128)(2,1)S(1)} %collective-permute-done.12.came, ...), custom_call_target="tpu_custom_call" | custom-call | flops 536870912 | bytes 8388608 | tf_op jit(solution)/shard_map/grads/pallas_call | solution.py:270
  65.9 3.7 %collective-permute-start.20 = (bf16[2,8,128,128]{3,2,1,0:T(8,128)(2,1)S(1)}, bf16[2,8,128,128]{3,2,1,0:T(8,128)(2,1)S(1)}, u32[]{:S(2)}, u32[]{:S(2)}) collective-permute-start(bf16[2,8,128,128]{3,2,1,0:T(8,128)(2,1)S(1)} %get-tuple-element.27), channel_id=1, source_target_pairs={{0,64},{32,96},{64,0},{96,32},{1,65},{33,97},{65,1},{97,33},{2,66}... | collective-permute-start | bytes 1572872 | tf_op jit(solution)/shard_map/ppermute | solution.py:41
  69.6 0.7 collective-permute-start.21
  70.3 2.3 %grads.2 = (bf16[2,8,128,128]{3,2,1,0:T(8,128)(2,1)S(1)}, bf16[2,8,128,128]{3,2,1,0:T(8,128)(2,1)S(1)}) custom-call(s32[2]{0:T(128)S(1)} %pad_add_fusion.1.where_ref, s32[2,4,8]{2,1,0:T(4,128)S(1)} %and_add_fusion.codes_ref, bf16[4,4,2,128,512]{4,3,2,1,0:T(8,128)(2,1)S(1)} %get-tuple-element.25.acts, bf16[8,512,128]{2,1,0:T(8,128)(2,1)S(1)} %collective-permute-done.12.came, ...), custom_call_target="tpu_custom_call" | custom-call | flops 536870912 | bytes 8388608 | tf_op jit(solution)/shard_map/grads/pallas_call | solution.py:270
  72.6 12.2 %collective-permute-done.13 = bf16[4,2,128,512]{3,2,1,0:T(8,128)(2,1)S(1)} collective-permute-done((bf16[4,2,128,512]{3,2,1,0:T(8,128)(2,1)S(1)}, bf16[4,2,128,512]{3,2,1,0:T(8,128)(2,1)S(1)}, u32[]{:S(2)}, u32[]{:S(2)}) %collective-permute-start.13) | collective-permute-done | bytes 1048608 | tf_op jit(solution)/shard_map/ppermute | solution.py:35
  84.7 3.7 %collective-permute-start.22 = (bf16[2,8,128,128]{3,2,1,0:T(8,128)(2,1)S(1)}, bf16[2,8,128,128]{3,2,1,0:T(8,128)(2,1)S(1)}, u32[]{:S(2)}, u32[]{:S(2)}) collective-permute-start(bf16[2,8,128,128]{3,2,1,0:T(8,128)(2,1)S(1)} %get-tuple-element.29), channel_id=1, source_target_pairs={{0,32},{32,64},{64,96},{96,0},{1,97},{33,1},{65,33},{97,65},{2,34}... | collective-permute-start | bytes 1572872 | tf_op jit(solution)/shard_map/ppermute | solution.py:41
  88.5 0.0 collective-permute-done.14
  88.5 0.6 add_convert_fusion
  89.1 0.1 slice_bitcast_fusion.4
  89.1 2.7 %collective-permute-start.16 = (bf16[2,128,512]{2,1,0:T(8,128)(2,1)S(1)}, bf16[2,128,512]{2,1,0:T(8,128)(2,1)S(1)}, u32[]{:S(2)}, u32[]{:S(2)}) collective-permute-start(bf16[2,128,512]{2,1,0:T(8,128)(2,1)S(1)} %get-tuple-element.30), channel_id=1, source_target_pairs={{0,16},{1,5},{2,18},{3,7},{4,20},{5,1},{6,22},{7,3},{8,24},{9,13},... | collective-permute-start | bytes 786440 | tf_op jit(solution)/shard_map/ppermute | solution.py:35
  91.8 1.1 %collective-permute-start.17 = (bf16[2,128,512]{2,1,0:T(8,128)(2,1)S(1)}, bf16[2,128,512]{2,1,0:T(8,128)(2,1)S(1)}, u32[]{:S(2)}, u32[]{:S(2)}) collective-permute-start(bf16[2,128,512]{2,1,0:T(8,128)(2,1)S(1)} %get-tuple-element.32), channel_id=1, source_target_pairs={{0,24},{1,7},{2,26},{3,1},{4,28},{5,3},{6,30},{7,5},{8,0},{9,15},{... | collective-permute-start | bytes 786440 | tf_op jit(solution)/shard_map/ppermute | solution.py:35
  93.0 0.0 collective-permute-done.20
  93.0 0.3 collective-permute-start.18
  93.3 1.3 %collective-permute-done.22 = bf16[2,8,128,128]{3,2,1,0:T(8,128)(2,1)S(1)} collective-permute-done((bf16[2,8,128,128]{3,2,1,0:T(8,128)(2,1)S(1)}, bf16[2,8,128,128]{3,2,1,0:T(8,128)(2,1)S(1)}, u32[]{:S(2)}, u32[]{:S(2)}) %collective-permute-start.22) | collective-permute-done | bytes 524320 | tf_op jit(solution)/shard_map/ppermute | solution.py:41
  94.6 0.3 multiply_convert_fusion
  95.0 2.5 %collective-permute-start.23 = (bf16[8,128,128]{2,1,0:T(8,128)(2,1)S(1)}, bf16[8,128,128]{2,1,0:T(8,128)(2,1)S(1)}, u32[]{:S(2)}, u32[]{:S(2)}) collective-permute-start(bf16[8,128,128]{2,1,0:T(8,128)(2,1)S(1)} %slice_bitcast_fusion), channel_id=1, source_target_pairs={{0,1},{1,0},{2,3},{3,2},{4,5},{5,4},{6,7},{7,6},{8,9},{9,8},{10,11... | collective-permute-start | bytes 786440 | tf_op jit(solution)/shard_map/ppermute | solution.py:45
  97.4 0.0 collective-permute-done.16
  97.4 1.3 %collective-permute-done.17 = bf16[2,128,512]{2,1,0:T(8,128)(2,1)S(1)} collective-permute-done((bf16[2,128,512]{2,1,0:T(8,128)(2,1)S(1)}, bf16[2,128,512]{2,1,0:T(8,128)(2,1)S(1)}, u32[]{:S(2)}, u32[]{:S(2)}) %collective-permute-start.17) | collective-permute-done | bytes 262176 | tf_op jit(solution)/shard_map/ppermute | solution.py:35
  98.7 1.0 collective-permute-done.18
  99.7 0.1 fusion.2
  99.8 2.7 %collective-permute-start.19 = (bf16[128,512]{1,0:T(8,128)(2,1)S(1)}, bf16[128,512]{1,0:T(8,128)(2,1)S(1)}, u32[]{:S(2)}, u32[]{:S(2)}) collective-permute-start(bf16[128,512]{1,0:T(8,128)(2,1)S(1)} %slice_bitcast_fusion.7), channel_id=1, source_target_pairs={{0,1},{1,0},{2,3},{3,2},{4,5},{5,4},{6,7},{7,6},{8,9},{9,8},{10,11... | collective-permute-start | bytes 393224 | tf_op jit(solution)/shard_map/ppermute | solution.py:45
  102.5 0.8 select_bitcast_fusion
  103.4 0.2 collective-permute-done.19
  103.5 0.7 broadcast_select_fusion.1
  (10 shorter events, 0.1 us)
Async XLA Ops:
  1.6 2.7 %collective-permute-start.1 = (bf16[128,512]{1,0:T(8,128)(2,1)S(1)}, bf16[128,512]{1,0:T(8,128)(2,1)S(1)}, u32[]{:S(2)}, u32[]{:S(2)}) collective-permute-start(bf16[128,512]{1,0:T(8,128)(2,1)S(1)} %get-tuple-element.42), channel_id=1, source_target_pairs={{0,1},{1,0},{2,3},{3,2},{4,5},{5,4},{6,7},{7,6},{8,9},{9,8},{10,11... | collective-permute-start | bytes 393224 | tf_op jit(solution)/shard_map/ppermute | solution.py:45
  4.2 16.1 %copy-start = (s32[16,8]{0,1:T(8,128)S(1)}, s32[16,8]{0,1:T(8,128)}, u32[]{:S(2)}) copy-start(s32[16,8]{0,1:T(8,128)} %param.8) | copy-start | bytes 1540
  4.2 16.2 %copy-start.1 = (s32[16,8]{0,1:T(8,128)S(1)}, s32[16,8]{0,1:T(8,128)}, u32[]{:S(2)}) copy-start(s32[16,8]{0,1:T(8,128)} %param.10) | copy-start | bytes 1540
  4.2 5.3 %collective-permute-start.8 = (bf16[8,128,128]{2,1,0:T(8,128)(2,1)S(1)}, bf16[8,128,128]{2,1,0:T(8,128)(2,1)S(1)}, u32[]{:S(2)}, u32[]{:S(2)}) collective-permute-start(bf16[8,128,128]{2,1,0:T(8,128)(2,1)S(1)} %get-tuple-element.36), channel_id=1, source_target_pairs={{0,1},{1,0},{2,3},{3,2},{4,5},{5,4},{6,7},{7,6},{8,9},{9,8},{10,11... | collective-permute-start | bytes 786440 | tf_op jit(solution)/shard_map/ppermute | solution.py:45
  4.4 8.9 %collective-permute-start.2 = (bf16[2,128,512]{2,1,0:T(8,128)(2,1)S(1)}, bf16[2,128,512]{2,1,0:T(8,128)(2,1)S(1)}, u32[]{:S(2)}, u32[]{:S(2)}) collective-permute-start(bf16[2,128,512]{2,1,0:T(8,128)(2,1)S(1)} %get-tuple-element.40), channel_id=1, source_target_pairs={{0,8},{1,3},{2,10},{3,5},{4,12},{5,7},{6,14},{7,1},{8,16},{9,11},{... | collective-permute-start | bytes 786440 | tf_op jit(solution)/shard_map/ppermute | solution.py:35
  5.8 9.5 %collective-permute-start.3 = (bf16[2,128,512]{2,1,0:T(8,128)(2,1)S(1)}, bf16[2,128,512]{2,1,0:T(8,128)(2,1)S(1)}, u32[]{:S(2)}, u32[]{:S(2)}) collective-permute-start(bf16[2,128,512]{2,1,0:T(8,128)(2,1)S(1)} %get-tuple-element.40), channel_id=1, source_target_pairs={{0,16},{1,5},{2,18},{3,7},{4,20},{5,1},{6,22},{7,3},{8,24},{9,13},... | collective-permute-start | bytes 786440 | tf_op jit(solution)/shard_map/ppermute | solution.py:35
  8.4 6.9 %collective-permute-start.4 = (bf16[2,128,512]{2,1,0:T(8,128)(2,1)S(1)}, bf16[2,128,512]{2,1,0:T(8,128)(2,1)S(1)}, u32[]{:S(2)}, u32[]{:S(2)}) collective-permute-start(bf16[2,128,512]{2,1,0:T(8,128)(2,1)S(1)} %get-tuple-element.40), channel_id=1, source_target_pairs={{0,24},{1,7},{2,26},{3,1},{4,28},{5,3},{6,30},{7,5},{8,0},{9,15},{... | collective-permute-start | bytes 786440 | tf_op jit(solution)/shard_map/ppermute | solution.py:35
  9.6 15.6 %collective-permute-start.10 = (bf16[2,8,128,128]{3,2,1,0:T(8,128)(2,1)S(1)}, bf16[2,8,128,128]{3,2,1,0:T(8,128)(2,1)S(1)}, u32[]{:S(2)}, u32[]{:S(2)}) collective-permute-start(bf16[2,8,128,128]{3,2,1,0:T(8,128)(2,1)S(1)} %pad_maximum_fusion.1.w0), channel_id=1, source_target_pairs={{0,64},{32,96},{64,0},{96,32},{1,65},{33,97},{65,1},{97,33},{2,66}... | collective-permute-start | bytes 1572872 | tf_op jit(solution)/shard_map/ppermute | solution.py:41
  15.4 22.9 %collective-permute-start.5 = (bf16[4,2,128,512]{3,2,1,0:T(8,128)(2,1)S(1)}, bf16[4,2,128,512]{3,2,1,0:T(8,128)(2,1)S(1)}, u32[]{:S(2)}, u32[]{:S(2)}) collective-permute-start(bf16[4,2,128,512]{3,2,1,0:T(8,128)(2,1)S(1)} %pad_maximum_fusion.a0), channel_id=1, source_target_pairs={{0,2},{1,9},{2,4},{3,11},{4,6},{5,13},{6,0},{7,15},{8,10},{9,17},{... | collective-permute-start | bytes 3145736 | tf_op jit(solution)/shard_map/ppermute | solution.py:35
  16.7 26.3 %collective-permute-start.6 = (bf16[4,2,128,512]{3,2,1,0:T(8,128)(2,1)S(1)}, bf16[4,2,128,512]{3,2,1,0:T(8,128)(2,1)}, u32[]{:S(2)}, u32[]{:S(2)}) collective-permute-start(bf16[4,2,128,512]{3,2,1,0:T(8,128)(2,1)S(1)} %pad_maximum_fusion.a0), channel_id=1, source_target_pairs={{0,4},{1,17},{2,6},{3,19},{4,0},{5,21},{6,2},{7,23},{8,12},{9,25},... | collective-permute-start | bytes 3145736 | tf_op jit(solution)/shard_map/ppermute | solution.py:35
  19.2 23.8 %collective-permute-start.7 = (bf16[4,2,128,512]{3,2,1,0:T(8,128)(2,1)S(1)}, bf16[4,2,128,512]{3,2,1,0:T(8,128)(2,1)}, u32[]{:S(2)}, u32[]{:S(2)}) collective-permute-start(bf16[4,2,128,512]{3,2,1,0:T(8,128)(2,1)S(1)} %pad_maximum_fusion.a0), channel_id=1, source_target_pairs={{0,6},{1,25},{2,0},{3,27},{4,2},{5,29},{6,4},{7,31},{8,14},{9,1},{... | collective-permute-start | bytes 3145736 | tf_op jit(solution)/shard_map/ppermute | solution.py:35
  20.5 3.0 %collective-permute-start = (s32[4,8]{1,0:T(4,128)S(1)}, s32[4,8]{1,0:T(4,128)S(1)}, u32[]{:S(2)}, u32[]{:S(2)}) collective-permute-start(s32[4,8]{1,0:T(4,128)S(1)} %bitcast.58), channel_id=1, source_target_pairs={{0,1},{1,0},{2,3},{3,2},{4,5},{5,4},{6,7},{7,6},{8,9},{9,8},{10,11... | collective-permute-start | bytes 392 | tf_op jit(solution)/shard_map/ppermute | solution.py:45
  23.5 12.5 %collective-permute-start.11 = (bf16[2,8,128,128]{3,2,1,0:T(8,128)(2,1)S(1)}, bf16[2,8,128,128]{3,2,1,0:T(8,128)(2,1)}, u32[]{:S(2)}, u32[]{:S(2)}) collective-permute-start(bf16[2,8,128,128]{3,2,1,0:T(8,128)(2,1)S(1)} %pad_maximum_fusion.1.w0), channel_id=1, source_target_pairs={{0,96},{32,0},{64,32},{96,64},{1,33},{33,65},{65,97},{97,1},{2,98}... | collective-permute-start | bytes 1572872 | tf_op jit(solution)/shard_map/ppermute | solution.py:41
  25.1 13.2 %collective-permute-start.9 = (bf16[2,8,128,128]{3,2,1,0:T(8,128)(2,1)S(1)}, bf16[2,8,128,128]{3,2,1,0:T(8,128)(2,1)}, u32[]{:S(2)}, u32[]{:S(2)}) collective-permute-start(bf16[2,8,128,128]{3,2,1,0:T(8,128)(2,1)S(1)} %pad_maximum_fusion.1.w0), channel_id=1, source_target_pairs={{0,32},{32,64},{64,96},{96,0},{1,97},{33,1},{65,33},{97,65},{2,34}... | collective-permute-start | bytes 1572872 | tf_op jit(solution)/shard_map/ppermute | solution.py:41
  48.5 5.3 %collective-permute-start.12 = (bf16[8,512,128]{2,1,0:T(8,128)(2,1)S(1)}, bf16[8,512,128]{2,1,0:T(8,128)(2,1)S(1)}, u32[]{:S(2)}, u32[]{:S(2)}) collective-permute-start(bf16[8,512,128]{2,1,0:T(8,128)(2,1)S(1)} %get-tuple-element.18), channel_id=1, source_target_pairs={{0,1},{1,0},{2,3},{3,2},{4,5},{5,4},{6,7},{7,6},{8,9},{9,8},{10,11... | collective-permute-start | bytes 3145736 | tf_op jit(solution)/shard_map/ppermute | solution.py:45
  59.4 25.3 %collective-permute-start.13 = (bf16[4,2,128,512]{3,2,1,0:T(8,128)(2,1)S(1)}, bf16[4,2,128,512]{3,2,1,0:T(8,128)(2,1)S(1)}, u32[]{:S(2)}, u32[]{:S(2)}) collective-permute-start(bf16[4,2,128,512]{3,2,1,0:T(8,128)(2,1)S(1)} %get-tuple-element.22), channel_id=1, source_target_pairs={{0,6},{1,25},{2,0},{3,27},{4,2},{5,29},{6,4},{7,31},{8,14},{9,1},{... | collective-permute-start | bytes 3145736 | tf_op jit(solution)/shard_map/ppermute | solution.py:35
  61.7 26.7 %collective-permute-start.14 = (bf16[4,2,128,512]{3,2,1,0:T(8,128)(2,1)S(1)}, bf16[4,2,128,512]{3,2,1,0:T(8,128)(2,1)S(1)}, u32[]{:S(2)}, u32[]{:S(2)}) collective-permute-start(bf16[4,2,128,512]{3,2,1,0:T(8,128)(2,1)S(1)} %get-tuple-element.23), channel_id=1, source_target_pairs={{0,2},{1,9},{2,4},{3,11},{4,6},{5,13},{6,0},{7,15},{8,10},{9,17},{... | collective-permute-start | bytes 3145736 | tf_op jit(solution)/shard_map/ppermute | solution.py:35
  61.7 26.7 %collective-permute-start.15 = (bf16[4,2,128,512]{3,2,1,0:T(8,128)(2,1)S(1)}, bf16[4,2,128,512]{3,2,1,0:T(8,128)(2,1)S(1)}, u32[]{:S(2)}, u32[]{:S(2)}) collective-permute-start(bf16[4,2,128,512]{3,2,1,0:T(8,128)(2,1)S(1)} %get-tuple-element.24), channel_id=1, source_target_pairs={{0,4},{1,17},{2,6},{3,19},{4,0},{5,21},{6,2},{7,23},{8,12},{9,25},... | collective-permute-start | bytes 3145736 | tf_op jit(solution)/shard_map/ppermute | solution.py:35
  65.9 27.1 %collective-permute-start.20 = (bf16[2,8,128,128]{3,2,1,0:T(8,128)(2,1)S(1)}, bf16[2,8,128,128]{3,2,1,0:T(8,128)(2,1)S(1)}, u32[]{:S(2)}, u32[]{:S(2)}) collective-permute-start(bf16[2,8,128,128]{3,2,1,0:T(8,128)(2,1)S(1)} %get-tuple-element.27), channel_id=1, source_target_pairs={{0,64},{32,96},{64,0},{96,32},{1,65},{33,97},{65,1},{97,33},{2,66}... | collective-permute-start | bytes 1572872 | tf_op jit(solution)/shard_map/ppermute | solution.py:41
  69.6 23.7 %collective-permute-start.21 = (bf16[2,8,128,128]{3,2,1,0:T(8,128)(2,1)S(1)}, bf16[2,8,128,128]{3,2,1,0:T(8,128)(2,1)S(1)}, u32[]{:S(2)}, u32[]{:S(2)}) collective-permute-start(bf16[2,8,128,128]{3,2,1,0:T(8,128)(2,1)S(1)} %get-tuple-element.28), channel_id=1, source_target_pairs={{0,96},{32,0},{64,32},{96,64},{1,33},{33,65},{65,97},{97,1},{2,98}... | collective-permute-start | bytes 1572872 | tf_op jit(solution)/shard_map/ppermute | solution.py:41
  84.7 9.9 %collective-permute-start.22 = (bf16[2,8,128,128]{3,2,1,0:T(8,128)(2,1)S(1)}, bf16[2,8,128,128]{3,2,1,0:T(8,128)(2,1)S(1)}, u32[]{:S(2)}, u32[]{:S(2)}) collective-permute-start(bf16[2,8,128,128]{3,2,1,0:T(8,128)(2,1)S(1)} %get-tuple-element.29), channel_id=1, source_target_pairs={{0,32},{32,64},{64,96},{96,0},{1,97},{33,1},{65,33},{97,65},{2,34}... | collective-permute-start | bytes 1572872 | tf_op jit(solution)/shard_map/ppermute | solution.py:41
  89.1 8.3 %collective-permute-start.16 = (bf16[2,128,512]{2,1,0:T(8,128)(2,1)S(1)}, bf16[2,128,512]{2,1,0:T(8,128)(2,1)S(1)}, u32[]{:S(2)}, u32[]{:S(2)}) collective-permute-start(bf16[2,128,512]{2,1,0:T(8,128)(2,1)S(1)} %get-tuple-element.30), channel_id=1, source_target_pairs={{0,16},{1,5},{2,18},{3,7},{4,20},{5,1},{6,22},{7,3},{8,24},{9,13},... | collective-permute-start | bytes 786440 | tf_op jit(solution)/shard_map/ppermute | solution.py:35
  91.8 6.9 %collective-permute-start.17 = (bf16[2,128,512]{2,1,0:T(8,128)(2,1)S(1)}, bf16[2,128,512]{2,1,0:T(8,128)(2,1)S(1)}, u32[]{:S(2)}, u32[]{:S(2)}) collective-permute-start(bf16[2,128,512]{2,1,0:T(8,128)(2,1)S(1)} %get-tuple-element.32), channel_id=1, source_target_pairs={{0,24},{1,7},{2,26},{3,1},{4,28},{5,3},{6,30},{7,5},{8,0},{9,15},{... | collective-permute-start | bytes 786440 | tf_op jit(solution)/shard_map/ppermute | solution.py:35
  93.0 6.7 %collective-permute-start.18 = (bf16[2,128,512]{2,1,0:T(8,128)(2,1)S(1)}, bf16[2,128,512]{2,1,0:T(8,128)(2,1)S(1)}, u32[]{:S(2)}, u32[]{:S(2)}) collective-permute-start(bf16[2,128,512]{2,1,0:T(8,128)(2,1)S(1)} %get-tuple-element.31), channel_id=1, source_target_pairs={{0,8},{1,3},{2,10},{3,5},{4,12},{5,7},{6,14},{7,1},{8,16},{9,11},{... | collective-permute-start | bytes 786440 | tf_op jit(solution)/shard_map/ppermute | solution.py:35
  95.0 7.6 %collective-permute-start.23 = (bf16[8,128,128]{2,1,0:T(8,128)(2,1)S(1)}, bf16[8,128,128]{2,1,0:T(8,128)(2,1)S(1)}, u32[]{:S(2)}, u32[]{:S(2)}) collective-permute-start(bf16[8,128,128]{2,1,0:T(8,128)(2,1)S(1)} %slice_bitcast_fusion), channel_id=1, source_target_pairs={{0,1},{1,0},{2,3},{3,2},{4,5},{5,4},{6,7},{7,6},{8,9},{9,8},{10,11... | collective-permute-start | bytes 786440 | tf_op jit(solution)/shard_map/ppermute | solution.py:45
  99.8 3.7 %collective-permute-start.19 = (bf16[128,512]{1,0:T(8,128)(2,1)S(1)}, bf16[128,512]{1,0:T(8,128)(2,1)S(1)}, u32[]{:S(2)}, u32[]{:S(2)}) collective-permute-start(bf16[128,512]{1,0:T(8,128)(2,1)S(1)} %slice_bitcast_fusion.7), channel_id=1, source_target_pairs={{0,1},{1,0},{2,3},{3,2},{4,5},{5,4},{6,7},{7,6},{8,9},{9,8},{10,11... | collective-permute-start | bytes 393224 | tf_op jit(solution)/shard_map/ppermute | solution.py:45
